TPU v7x, 32 devices: a whole 2x2x4 slice. The times are simulated.
32 devices in a mesh: dp: 8 (over y, x, core), tensor: 4 (over z).
Axes of the slice: x: 2, y: 2, z: 4, core: 2. Of those that a mesh axis runs over, the one named last changes fastest.
Arguments:
- tokens: bfloat16 [16384, 1024], P(('dp', 'tensor')), may hold values from -6 to 6
- cotangent: bfloat16 [16384, 1024], P(('dp', 'tensor')), may hold values from -6 to 6
- lengths: int32 [8, 3], P('dp'), may hold values from 1 to 1024, 1920 in all within a row
- token_order: int32 [16384], P(('dp', 'tensor')), may hold values from 0 to 16383, as said below
- token_return: int32 [16384], P(('dp', 'tensor')), may hold values from 0 to 16383, as said below
- w_mix: float32 [1024, 8, 768], P('dp', 'tensor'), may hold values from -0.1875 to 0.1875
- w_ba: float32 [1024, 8, 2], P('dp', 'tensor'), may hold values from -0.1875 to 0.1875
- conv_w: float32 [512, 8, 4], P('dp', 'tensor'), may hold values from -3 to 3
- w_out: float32 [1024, 8, 256], P('dp', 'tensor'), may hold values from -0.1875 to 0.1875
- w_gate_up: float32 [1024, 2, 2816], P('dp', None, 'tensor'), may hold values from -0.1875 to 0.1875
- w_down: float32 [1024, 2816], P('dp', 'tensor'), may hold values from -0.15625 to 0.15625
- gain_attn: float32 [1024], replicated, may hold values from 0.25 to 1.75
- gain_ffn: float32 [1024], replicated, may hold values from 0.25 to 1.75
- gain_out: float32 [256], replicated, may hold values from 0.25 to 1.75
- decay_log: float32 [8], replicated, may hold values from -8 to -3.5
- decay_bias: float32 [8], replicated, may hold values from -1 to 1
Outputs:
- layer_out: bfloat16 [16384, 1024], P(('dp', 'tensor'))
- input_grad: bfloat16 [16384, 1024], P(('dp', 'tensor'))
- grad_w_mix: float32 [1024, 8, 768], P('dp', 'tensor')
- grad_w_ba: float32 [1024, 8, 2], P('dp', 'tensor')
- grad_conv_w: float32 [512, 8, 4], P('dp', 'tensor')
- grad_w_out: float32 [1024, 8, 256], P('dp', 'tensor')
- grad_w_gate_up: float32 [1024, 2, 2816], P('dp', None, 'tensor')
- grad_w_down: float32 [1024, 2816], P('dp', 'tensor')
- grad_gain_attn: float32 [1024], replicated
- grad_gain_ffn: float32 [1024], replicated
- grad_gain_out: float32 [256], replicated
- grad_decay_log: float32 [8], replicated
- grad_decay_bias: float32 [8], replicated
Inputs may be any that keep to these rules, and one draw needn't show every extreme that they name: `lengths`: each row sums to 1920, and its largest entry is 1024. `token_order`: a permutation. Writing a row as 2048 * g + 512 * s + i with 0 <= i < 512, packed row and given row have the same s, and for every g and g' exactly 64 packed rows of group g' with a given s take given rows of group g. `token_return`: the inverse permutation of token_order.
All inputs are finite; a program needn't handle non-finite values.
Results may differ from a plain program's by a relative error of at most 0.015.
The roundings to bfloat16 on the way count: a program that leaves them out, or rounds other values in their place, can miss the bound.
Values may be sent and summed in bfloat16 or wider, within the bound.
No kernel may reach another device: no remote copies, remote signals or barrier semaphores. Data moves between devices by JAX's collectives and lax.ppermute only.
A program may use at most 256 MiB of HBM per device.

v0:
```python
import jax
import jax.numpy as jnp
from jax import lax
from jax.sharding import PartitionSpec as P

DK = 128
DV = 256
SPAN = 64
SEQS = 3


highest_precision = lax.Precision.HIGHEST
epsilon = 1e-06


def rms_scale(values):
    return lax.rsqrt(jnp.mean(values * values, axis=-1, keepdims=True) + epsilon)


def norm_rows(values, gain):
    return values * rms_scale(values) * gain


def segments(length_row, group_rows):
    seq_ends = jnp.cumsum(length_row)
    positions = jnp.arange(group_rows, dtype=jnp.int32)
    return jnp.sum((positions[:, None] >= seq_ends[None, :]).astype(jnp.int32), axis=1)


def short_conv(inputs, weights, segment_ids):
    row_count = inputs.shape[0]
    running = inputs * jnp.transpose(weights[:, :, 0])[None]
    for offset in range(1, weights.shape[2]):
        shifted = jnp.concatenate(
            [jnp.zeros((offset,) + inputs.shape[1:], inputs.dtype), inputs[: row_count - offset]],
            axis=0,
        )
        earlier = jnp.concatenate(
            [jnp.full((offset,), -1, jnp.int32), segment_ids[: row_count - offset]]
        )
        running = (
            running
            + jnp.where((earlier == segment_ids)[:, None, None], shifted, 0.0)
            * jnp.transpose(weights[:, :, offset])[None]
        )
    return running


def mixer_core(
    projected, small_proj, conv_weights, decay_rate, decay_shift, gain_norm, segment_ids, recurrence
):
    conv_width = 2 * DK + DV
    active = jax.nn.silu(short_conv(projected[:, :, :conv_width], conv_weights, segment_ids))
    query_vec = active[:, :, :DK]
    key_vec = active[:, :, DK : 2 * DK]
    value_vec = active[:, :, 2 * DK :]
    query_vec = (
        query_vec
        * lax.rsqrt(jnp.sum(query_vec * query_vec, axis=-1, keepdims=True) + epsilon)
        * DK ** (-0.5)
    )
    key_vec = key_vec * lax.rsqrt(jnp.sum(key_vec * key_vec, axis=-1, keepdims=True) + epsilon)
    beta_gate = jax.nn.sigmoid(small_proj[:, :, 0])
    log_decay = -jnp.exp(decay_rate)[None, :] * jax.nn.softplus(
        small_proj[:, :, 1] + decay_shift[None, :]
    )
    result = recurrence(query_vec, key_vec, value_vec, beta_gate, log_decay, segment_ids)
    normed = result * rms_scale(result) * gain_norm
    gated_out = normed * jax.nn.silu(projected[:, :, conv_width:])
    return gated_out * (segment_ids < SEQS).astype(gated_out.dtype)[:, None, None]


def delta_blocks(query_vec, key_vec, value_vec, beta_gate, log_decay, segment_ids):
    total_rows = query_vec.shape[0]
    block_count = total_rows // SPAN
    before_ids = jnp.concatenate([jnp.full((1,), -1, jnp.int32), segment_ids[:-1]])[::SPAN]
    lower_tri = jnp.tril(jnp.ones((SPAN, SPAN), dtype=bool))
    strict_tri = jnp.tril(jnp.ones((SPAN, SPAN), dtype=bool), -1)

    def split_rows(array):
        return array.reshape((block_count, SPAN) + array.shape[1:])

    def one_block(recurrent_matrix, pieces):
        query_rows, block_of_keys, values_block, beta_rows, decays, seg_block, before_id = pieces
        cumulative = jnp.cumsum(decays, axis=0)
        same_seg = seg_block[:, None] == seg_block[None, :]
        log_gap = cumulative[:, None, :] - cumulative[None, :, :]
        pairwise_decay = jnp.where(
            (same_seg & lower_tri)[:, :, None], jnp.exp(jnp.minimum(log_gap, 0.0)), 0.0
        )
        pairwise_decay = jnp.transpose(pairwise_decay, (2, 0, 1))
        carry_scale = jnp.transpose(
            jnp.where((seg_block == before_id)[:, None], jnp.exp(cumulative), 0.0)
        )
        beta_cols = jnp.transpose(beta_rows)[:, :, None]
        key_key = jnp.einsum(
            "ihk,jhk->hij", block_of_keys, block_of_keys, precision=highest_precision
        )
        lower_part = jnp.where(strict_tri[None], pairwise_decay * key_key, 0.0) * beta_cols
        key_state_product = jnp.einsum(
            "grm,rmj->rgj", block_of_keys, recurrent_matrix, precision=highest_precision
        )
        right_side = beta_cols * (
            jnp.transpose(values_block, (1, 0, 2)) - carry_scale[:, :, None] * key_state_product
        )
        delta_update_rows = jax.scipy.linalg.solve_triangular(
            lower_part, right_side, lower=True, unit_diagonal=True
        )
        query_state_product = jnp.einsum(
            "grm,rmj->rgj", query_rows, recurrent_matrix, precision=highest_precision
        )
        query_key = jnp.einsum(
            "ihk,jhk->hij", query_rows, block_of_keys, precision=highest_precision
        )
        outputs = carry_scale[:, :, None] * query_state_product + jnp.einsum(
            "hij,hjv->hiv",
            query_key * pairwise_decay,
            delta_update_rows,
            precision=highest_precision,
        )
        new_state = carry_scale[:, -1][:, None, None] * recurrent_matrix + jnp.einsum(
            "tdx,dt,dtg->dxg",
            block_of_keys,
            pairwise_decay[:, -1, :],
            delta_update_rows,
            precision=highest_precision,
        )
        return (new_state, jnp.transpose(outputs, (1, 0, 2)))

    block_items = (
        split_rows(query_vec),
        split_rows(key_vec),
        split_rows(value_vec),
        split_rows(beta_gate),
        split_rows(log_decay),
        split_rows(segment_ids),
        before_ids,
    )
    initial = jnp.zeros((query_vec.shape[1], DK, DV), query_vec.dtype)
    outputs = lax.scan(jax.checkpoint(one_block), initial, block_items)[1]
    return outputs.reshape(total_rows, query_vec.shape[1], DV)


def body(
    tokens,
    cotangent,
    lengths,
    token_order,
    token_return,
    w_mix,
    w_ba,
    conv_w,
    w_out,
    w_gate_up,
    w_down,
    gain_attn,
    gain_ffn,
    gain_out,
    decay_log,
    decay_bias,
):
    groups = lax.axis_size("dp")
    splits = lax.axis_size("tensor")
    local_rows = tokens.shape[0]
    model_width = tokens.shape[1]
    group_rows = local_rows * splits
    per_peer = local_rows // groups
    send_key = token_return // group_rows * local_rows + token_return % local_rows
    send_order = jnp.argsort(send_key)
    recv_key = token_order // group_rows * local_rows + jnp.arange(local_rows, dtype=jnp.int32)
    recv_order = jnp.argsort(recv_key)
    recv_place = jnp.argsort(recv_order)
    arrived = (
        lax.all_to_all(
            tokens[send_order].reshape(groups, per_peer, model_width),
            "dp",
            split_axis=0,
            concat_axis=0,
            tiled=True,
        ),
        lax.all_to_all(
            cotangent[send_order].reshape(groups, per_peer, model_width),
            "dp",
            split_axis=0,
            concat_axis=0,
            tiled=True,
        ),
    )
    packed_in = arrived[0].reshape(local_rows, model_width)[recv_place]
    packed_grad = arrived[1].reshape(local_rows, model_width)[recv_place]
    segment_ids = segments(lengths[0], group_rows)
    row_mask = (segment_ids < SEQS).astype(jnp.float32)[:, None]
    mix_all, small_all, conv_all, out_all, ffn_all, down_all = (
        lax.all_gather(w_mix.astype(jnp.bfloat16), "dp", axis=0, tiled=True),
        lax.all_gather(w_ba.astype(jnp.bfloat16), "dp", axis=0, tiled=True),
        lax.all_gather(conv_w.astype(jnp.bfloat16), "dp", axis=0, tiled=True),
        lax.all_gather(w_out.astype(jnp.bfloat16), "dp", axis=0, tiled=True),
        lax.all_gather(w_gate_up.astype(jnp.bfloat16), "dp", axis=0, tiled=True),
        lax.all_gather(w_down.astype(jnp.bfloat16), "dp", axis=0, tiled=True),
    )
    input_f32 = packed_in.astype(jnp.float32)
    normed_f32, norm_attn_back = jax.vjp(norm_rows, input_f32, gain_attn)
    normed_all, grad_all = (
        lax.all_gather(normed_f32.astype(jnp.bfloat16), "tensor", axis=0, tiled=True),
        lax.all_gather(packed_grad, "tensor", axis=0, tiled=True),
    )
    projected = jnp.einsum("td,dhp->thp", normed_all, mix_all, preferred_element_type=jnp.float32)
    small_proj = jnp.einsum(
        "td,dhc->thc", normed_all, small_all, preferred_element_type=jnp.float32
    )
    heads_here = mix_all.shape[1]
    head_start = lax.axis_index("tensor") * heads_here
    rate_here = lax.dynamic_slice_in_dim(decay_log, head_start, heads_here)
    shift_here = lax.dynamic_slice_in_dim(decay_bias, head_start, heads_here)

    def core_pass(proj_in, small_in, conv_in, rate_in, shift_in, gain_in):
        return mixer_core(
            proj_in, small_in, conv_in, rate_in, shift_in, gain_in, segment_ids, delta_blocks
        )

    gated_f32, core_back = jax.vjp(
        core_pass,
        projected,
        small_proj,
        conv_all.astype(jnp.float32),
        rate_here,
        shift_here,
        gain_out,
    )
    gated_out = gated_f32.astype(jnp.bfloat16)
    middle = input_f32 + lax.psum_scatter(
        jnp.einsum("thv,dhv->td", gated_out, out_all, preferred_element_type=jnp.float32),
        "tensor",
        scatter_dimension=0,
        tiled=True,
    )
    normed_mid_f32, norm_ffn_back = jax.vjp(norm_rows, middle, gain_ffn)
    normed_mid_all = lax.all_gather(
        normed_mid_f32.astype(jnp.bfloat16), "tensor", axis=0, tiled=True
    )
    gate_up = jnp.einsum("td,dcf->tcf", normed_mid_all, ffn_all, preferred_element_type=jnp.float32)

    def activate(pair_in):
        return jax.nn.silu(pair_in[:, 0]) * pair_in[:, 1] * row_mask

    hidden_f32, act_back = jax.vjp(activate, gate_up)
    hidden = hidden_f32.astype(jnp.bfloat16)
    layer_rows = (
        middle
        + lax.psum_scatter(
            jnp.einsum("tf,df->td", hidden, down_all, preferred_element_type=jnp.float32).astype(
                jnp.bfloat16
            ),
            "tensor",
            scatter_dimension=0,
            tiled=True,
        ).astype(jnp.float32)
    ).astype(jnp.bfloat16)
    grad_down = jnp.einsum("td,tf->df", grad_all, hidden, preferred_element_type=jnp.float32)
    grad_hidden = jnp.einsum("td,df->tf", grad_all, down_all, preferred_element_type=jnp.float32)
    grad_pair = act_back(grad_hidden)[0].astype(jnp.bfloat16)
    grad_ffn_w = jnp.einsum(
        "td,tcf->dcf", normed_mid_all, grad_pair, preferred_element_type=jnp.float32
    )
    grad_mid_norm, grad_gain_ffn = norm_ffn_back(
        lax.psum_scatter(
            jnp.einsum("tcf,dcf->td", grad_pair, ffn_all, preferred_element_type=jnp.float32),
            "tensor",
            scatter_dimension=0,
            tiled=True,
        )
    )
    grad_middle = packed_grad.astype(jnp.float32) + grad_mid_norm
    grad_middle_all = lax.all_gather(grad_middle.astype(jnp.bfloat16), "tensor", axis=0, tiled=True)
    grad_out_w = jnp.einsum(
        "thv,td->dhv", gated_out, grad_middle_all, preferred_element_type=jnp.float32
    )
    grad_gated = jnp.einsum(
        "td,dhv->thv", grad_middle_all, out_all, preferred_element_type=jnp.float32
    )
    grad_proj, grad_small, grad_conv, grad_rate, grad_shift, grad_gain_out = core_back(grad_gated)
    grad_proj = grad_proj.astype(jnp.bfloat16)
    grad_small = grad_small.astype(jnp.bfloat16)
    grad_mix_w = jnp.einsum(
        "td,thp->dhp", normed_all, grad_proj, preferred_element_type=jnp.float32
    )
    grad_small_w = jnp.einsum(
        "td,thc->dhc", normed_all, grad_small, preferred_element_type=jnp.float32
    )
    grad_normed = lax.psum_scatter(
        (
            jnp.einsum("thp,dhp->td", grad_proj, mix_all, preferred_element_type=jnp.float32)
            + jnp.einsum("thc,dhc->td", grad_small, small_all, preferred_element_type=jnp.float32)
        ).astype(jnp.bfloat16),
        "tensor",
        scatter_dimension=0,
        tiled=True,
    ).astype(jnp.float32)
    grad_input_norm, grad_gain_attn = norm_attn_back(grad_normed)
    grad_rows = (grad_middle + grad_input_norm).astype(jnp.bfloat16)
    owned = (
        lax.psum_scatter(grad_mix_w, "dp", scatter_dimension=0, tiled=True),
        lax.psum_scatter(grad_small_w, "dp", scatter_dimension=0, tiled=True),
        lax.psum_scatter(grad_conv, "dp", scatter_dimension=0, tiled=True),
        lax.psum_scatter(grad_out_w, "dp", scatter_dimension=0, tiled=True),
        lax.psum_scatter(grad_ffn_w, "dp", scatter_dimension=0, tiled=True),
        lax.psum_scatter(grad_down, "dp", scatter_dimension=0, tiled=True),
    )
    head_total = decay_log.shape[0]
    rate_full = lax.dynamic_update_slice_in_dim(
        jnp.zeros((head_total,), jnp.float32), grad_rate, head_start, 0
    )
    shift_full = lax.dynamic_update_slice_in_dim(
        jnp.zeros((head_total,), jnp.float32), grad_shift, head_start, 0
    )
    small_sums = lax.psum(
        (grad_gain_attn, grad_gain_ffn, grad_gain_out, rate_full, shift_full), ("dp", "tensor")
    )
    returned = (
        lax.all_to_all(
            layer_rows[recv_order].reshape(groups, per_peer, model_width),
            "dp",
            split_axis=0,
            concat_axis=0,
            tiled=True,
        ),
        lax.all_to_all(
            grad_rows[recv_order].reshape(groups, per_peer, model_width),
            "dp",
            split_axis=0,
            concat_axis=0,
            tiled=True,
        ),
    )
    back_place = jnp.argsort(send_order)
    layer_out = returned[0].reshape(local_rows, model_width)[back_place]
    input_grad = returned[1].reshape(local_rows, model_width)[back_place]
    return (
        layer_out,
        input_grad,
        owned[0],
        owned[1],
        owned[2],
        owned[3],
        owned[4],
        owned[5],
        small_sums[0],
        small_sums[1],
        small_sums[2],
        small_sums[3],
        small_sums[4],
    )


def solution(mesh):
    placed = (
        P(("dp", "tensor"), None),
        P(("dp", "tensor"), None),
        P("dp", None),
        P(("dp", "tensor")),
        P(("dp", "tensor")),
        P("dp", "tensor", None),
        P("dp", "tensor", None),
        P("dp", "tensor", None),
        P("dp", "tensor", None),
        P("dp", None, "tensor"),
        P("dp", "tensor"),
        P(),
        P(),
        P(),
        P(),
        P(),
    )
    return jax.shard_map(
        body,
        mesh=mesh,
        in_specs=placed,
        out_specs=(
            P(("dp", "tensor"), None),
            P(("dp", "tensor"), None),
            P("dp", "tensor", None),
            P("dp", "tensor", None),
            P("dp", "tensor", None),
            P("dp", "tensor", None),
            P("dp", None, "tensor"),
            P("dp", "tensor"),
            P(),
            P(),
            P(),
            P(),
            P(),
        ),
        check_vma=False,
    )
```

profile of v0, /device:TPU:2, one launch (start us, length us, event | category | flops | bytes accessed | tf_op | source)
XLA Modules:
  0.0 3141.1 jit_solution(17922218729090918797)
XLA Ops:
  66.5 66.1 %all-gather.10.cloned.1.call-done = bf16[2048,1024]{1,0:T(8,128)(2,1)} async-done(((bf16[512,1024]{1,0:T(8,128)(2,1)}), bf16[2048,1024]{1,0:T(8,128)(2,1)}) %all-gather.10.cloned.1.call-update) | async-done | bytes 4194320 | tf_op jit(solution)/shard_map/all_gather | solution.py:204
  132.5 9.9 fusion.156
  156.4 14.5 fusion.136
  190.9 640.9 %while.41 = (s32[]{:T(128)}, f32[2,128,256]{2,1,0:T(8,128)S(1)}, f32[32,64,2,256]{3,1,2,0:T(8,128)}, f32[32,2,128,256]{3,2,1,0:T(8,128)}, s32[32,64]{1,0:T(8,128...) while((s32[]{:T(128)}, f32[2,128,256]{2,1,0:T(8,128)S(1)}, ...), condition=%wide.region_10.12_spmd.clone, body=%wide.region_8.11_spmd.clone.sunk | while | flops 227238144 | bytes 3428001 | solution.py:140
  515.6 9.8 custom-call.42
  615.8 9.8 custom-call.42
  655.9 9.8 custom-call.42
  852.1 141.1 %reduce-scatter.15.cloned.1.call-done = f32[512,1024]{1,0:T(8,128)} async-done(((f32[2048,1024]{1,0:T(8,128)}), f32[512,1024]{1,0:T(8,128)}) %reduce-scatter.15.cloned.1.call-update) | async-done | bytes 2097168 | tf_op jit(solution)/shard_map/reduce_scatter | solution.py:231
  1000.9 20.7 all_to_all.20
  1024.5 11.1 all-gather.18.cloned.1.call-done
  1035.6 82.8 %all-gather.16.cloned.1.call-done = bf16[2048,1024]{1,0:T(8,128)(2,1)} async-done(((bf16[512,1024]{1,0:T(8,128)(2,1)}), bf16[2048,1024]{1,0:T(8,128)(2,1)}) %all-gather.16.cloned.1.call-update) | async-done | bytes 4194320 | tf_op jit(solution)/shard_map/all_gather | solution.py:238
  1118.4 11.8 fusion.149
  1130.3 14.4 all-gather.20.cloned.1.call-done
  1144.7 82.4 %all-gather.24.cloned.1.call-done = bf16[2048,1024]{1,0:T(8,128)(2,1)} async-done(((bf16[512,1024]{1,0:T(8,128)(2,1)}), bf16[2048,1024]{1,0:T(8,128)(2,1)}) %all-gather.24.cloned.1.call-update) | async-done | bytes 4194320 | tf_op jit(solution)/shard_map/all_gather | solution.py:205
  1227.1 11.4 multiply_bitcast_fusion
  1251.9 143.0 %reduce-scatter.19.cloned.1.call-done = f32[512,1024]{1,0:T(8,128)} async-done(((f32[2048,1024]{1,0:T(8,128)}), f32[512,1024]{1,0:T(8,128)}) %reduce-scatter.19.cloned.1.call-update) | async-done | bytes 2097168 | tf_op jit(solution)/shard_map/reduce_scatter | solution.py:266
  1401.6 79.7 %all-gather.22.cloned.1.call-done = bf16[2048,1024]{1,0:T(8,128)(2,1)} async-done(((bf16[512,1024]{1,0:T(8,128)(2,1)}), bf16[2048,1024]{1,0:T(8,128)(2,1)}) %all-gather.22.cloned.1.call-update) | async-done | bytes 4194320 | tf_op jit(solution)/shard_map/all_gather | solution.py:274
  1481.3 10.9 multiply_reduce_fusion.9
  1501.6 1109.0 %while.42 = (s32[]{:T(128)}, f32[2,128,256]{2,1,0:T(8,128)}, f32[32,64,2,128]{3,1,0,2:T(8,128)}, f32[32,64,2,128]{3,1,0,2:T(8,128)S(1)}, f32[32,64,2,256]{3,1,0,...) while((s32[]{:T(128)}, f32[2,128,256]{2,1,0:T(8,128)}, ...), condition=%wide.region_29.31_spmd.clone, body=%wide.region_19.30_spmd.clone.sunk | while | flops 612151424 | bytes 10787363 | solution.py:140
  2624.9 16.1 multiply_reduce_fusion.8
  2652.8 13.7 multiply_add_fusion
  2699.7 12.9 fusion.152
  2720.9 11.8 fusion.147
  2733.4 21.7 reduce-scatter.21.cloned.1.call-done
  2757.2 77.4 %reduce-scatter.17.cloned.1.call-done = bf16[512,1024]{1,0:T(8,128)(2,1)} async-done(((bf16[2048,1024]{1,0:T(8,128)(2,1)}), bf16[512,1024]{1,0:T(8,128)(2,1)}) %reduce-scatter.17.cloned.1.call-update) | async-done | bytes 1048592 | tf_op jit(solution)/shard_map/reduce_scatter | solution.py:250
  2848.2 11.1 all-to-all-done.3
  2874.0 37.3 %reduce-scatter.31.cloned.1.call-done = f32[128,4]{1,0:T(8,128)} async-done(((f32[1024,4]{1,0:T(8,128)}), f32[128,4]{1,0:T(8,128)}) %reduce-scatter.31.cloned.1.call-update) | async-done | bytes 2064
  2912.8 42.9 %reduce-scatter.25.cloned.1.call-done = f32[128,2,256]{2,0,1:T(8,128)} async-done(((f32[1024,2,256]{2,0,1:T(8,128)}), f32[128,2,256]{2,0,1:T(8,128)}) %reduce-scatter.25.cloned.1.call-update) | async-done | bytes 262160 | tf_op jit(solution)/shard_map/reduce_scatter | solution.py:305
  2957.6 40.9 %all-reduce.23 = (f32[1024]{0:T(1024)}, f32[1024]{0:T(1024)}, f32[256]{0:T(256)}, f32[8]{0:T(128)}, f32[8]{0:T(128)}) all-reduce(f32[1024]{0:T(1024)S(1)} %get-tuple-element.900, f32[1024]{0:T(1024)S(1)} %copy-done.65, f32[256]{0:T(256)S(1)} %copy-done.85, ...), channel_id=1, replica_groups=mesh['dp'=8,'tensor'=4] {'dp','tensor'}, use_global_device_ids=true, to_apply=%region_45.47 | all-reduce | flops 2320 | bytes 18560 | tf_op jit(solution)/shard_map/psum | solution.py:316
  3004.0 17.7 reduce-scatter.23.cloned.1.call-done
  3024.3 46.1 %reduce-scatter.29.cloned.1.call-done = f32[128,704]{0,1:T(8,128)} async-done(((f32[1024,704]{0,1:T(8,128)}), f32[128,704]{0,1:T(8,128)}) %reduce-scatter.29.cloned.1.call-update) | async-done | bytes 360464 | tf_op jit(solution)/shard_map/reduce_scatter | solution.py:307
  3070.4 63.3 %reduce-scatter.27.cloned.1.call-done = f32[128,2,704]{0,2,1:T(8,128)} async-done(((f32[1024,2,704]{0,2,1:T(8,128)}), f32[128,2,704]{0,2,1:T(8,128)}) %reduce-scatter.27.cloned.1.call-update) | async-done | bytes 720912 | tf_op jit(solution)/shard_map/reduce_scatter | solution.py:306
  (2959 shorter events, 1973.7 us)
Async XLA Ops:
  7.2 59.3 %all-gather.12.cloned.1.call-start = ((), (), s32[]{:S(2)}) async-start(), calls=%async_computation.15 | async-start | bytes 3538944 | tf_op jit(solution)/shard_map/all_gather | solution.py:194
  17.1 20.5 all-to-all-start
  21.4 111.1 %all-gather.10.cloned.1.call-start = ((), (), s32[]{:S(2)}) async-start(), calls=%async_computation.14 | async-start | bytes 5242880 | tf_op jit(solution)/shard_map/all_gather | solution.py:204
  41.4 801.1 %all-gather.14.cloned.1.call-start = ((), (), s32[]{:S(2)}) async-start(), calls=%async_computation.16 | async-start | bytes 1179648 | tf_op jit(solution)/shard_map/all_gather | solution.py:197
  42.2 951.0 %reduce-scatter.15.cloned.1.call-start = ((), (), s32[]{:S(2)}) async-start(), calls=%async_computation.17 | async-start | bytes 10485760 | tf_op jit(solution)/shard_map/reduce_scatter | solution.py:231
  66.4 771.8 %copy-start.55 = (f32[2048]{0:T(1024)}, f32[2048]{0:T(1024)S(1)}, u32[]{:S(2)}) copy-start(f32[2048]{0:T(1024)S(1)} %get-tuple-element.1014) | copy-start | bytes 24580
  66.4 1333.2 %copy-start.48 = (pred[2048]{0:T(1024)(128)(4,1)}, pred[2048]{0:T(1024)(128)(4,1)S(1)}, u32[]{:S(2)}) copy-start(pred[2048]{0:T(1024)(128)(4,1)S(1)} %get-tuple-element.1015) | copy-start | bytes 6148
  66.4 1333.8 %copy-start.50 = (pred[2048]{0:T(1024)(128)(4,1)}, pred[2048]{0:T(1024)(128)(4,1)S(1)}, u32[]{:S(2)}) copy-start(pred[2048]{0:T(1024)(128)(4,1)S(1)} %get-tuple-element.1016) | copy-start | bytes 6148
  850.1 145.8 %copy-start.32 = (f32[1024]{0:T(1024)S(1)}, f32[1024]{0:T(1024)}, u32[]{:S(2)}) copy-start(f32[1024]{0:T(1024)} %param.34) | copy-start | bytes 12292
  850.1 185.5 %all-gather.18.cloned.1.call-start = ((), (), s32[]{:S(2)}) async-start(), calls=%async_computation.19 | async-start | bytes 3244032 | tf_op jit(solution)/shard_map/all_gather | solution.py:198
  852.0 145.2 %copy-start.21 = (f32[128,704]{0,1:T(8,128)S(1)}, f32[128,704]{0,1:T(8,128)}, u32[]{:S(2)}) copy-start(f32[128,704]{0,1:T(8,128)} %param.32) | copy-start | bytes 1081348
  852.0 146.0 %copy-start.4 = (bf16[512,1024]{1,0:T(8,128)(2,1)S(1)}, bf16[512,1024]{1,0:T(8,128)(2,1)}, u32[]{:S(2)}) copy-start(bf16[512,1024]{1,0:T(8,128)(2,1)} %param.23) | copy-start | bytes 3145732
  852.0 266.4 %all-gather.16.cloned.1.call-start = ((), (), s32[]{:S(2)}) async-start(), calls=%async_computation.18 | async-start | bytes 5242880 | tf_op jit(solution)/shard_map/all_gather | solution.py:238
  995.4 402.5 %copy-start.5 = (f32[512,1024]{1,0:T(8,128)}, f32[512,1024]{1,0:T(8,128)S(1)}, u32[]{:S(2)}) copy-start(f32[512,1024]{1,0:T(8,128)S(1)} %get-tuple-element.970) | copy-start | bytes 6291460
  995.9 402.0 %copy-start.35 = (f32[512]{0:T(512)}, f32[512]{0:T(512)S(1)}, u32[]{:S(2)}) copy-start(f32[512]{0:T(512)S(1)} %fusion.195) | copy-start | bytes 6148
  997.2 147.5 %all-gather.20.cloned.1.call-start = ((), (), s32[]{:S(2)}) async-start(), calls=%async_computation.20 | async-start | bytes 1622016 | tf_op jit(solution)/shard_map/all_gather | solution.py:199
  998.0 229.1 %all-gather.24.cloned.1.call-start = ((), (), s32[]{:S(2)}) async-start(), calls=%async_computation.29 | async-start | bytes 5242880 | tf_op jit(solution)/shard_map/all_gather | solution.py:205
  1024.4 202.7 %copy-start.56 = (f32[2048]{0:T(1024)S(1)}, f32[2048]{0:T(1024)}, u32[]{:S(2)}) copy-start(f32[2048]{0:T(1024)} %copy-done.55) | copy-start | bytes 24580
  1024.4 370.5 %reduce-scatter.19.cloned.1.call-start = ((), (), s32[]{:S(2)}) async-start(), calls=%async_computation.22 | async-start | bytes 10485760 | tf_op jit(solution)/shard_map/reduce_scatter | solution.py:266
  1251.9 146.0 %copy-start.64 = (f32[512]{0:T(512)S(1)}, f32[512]{0:T(512)}, u32[]{:S(2)}) copy-start(f32[512]{0:T(512)} %copy-done.63) | copy-start | bytes 6148
  1251.9 146.0 %copy-start.11 = (bf16[512,1024]{1,0:T(8,128)(2,1)S(1)}, bf16[512,1024]{1,0:T(8,128)(2,1)}, u32[]{:S(2)}) copy-start(bf16[512,1024]{1,0:T(8,128)(2,1)} %gather_fusion.5) | copy-start | bytes 3145732
  1251.9 229.4 %all-gather.22.cloned.1.call-start = ((), (), s32[]{:S(2)}) async-start(), calls=%async_computation.23 | async-start | bytes 5242880 | tf_op jit(solution)/shard_map/all_gather | solution.py:274
  1399.5 1355.5 %reduce-scatter.21.cloned.1.call-start = ((), (), s32[]{:S(2)}) async-start(), calls=%async_computation.24 | async-start | bytes 5242880 | tf_op jit(solution)/shard_map/reduce_scatter | solution.py:290
  2679.6 155.0 %reduce-scatter.17.cloned.1.call-start = ((), (), s32[]{:S(2)}) async-start(), calls=%async_computation.21 | async-start | bytes 5242880 | tf_op jit(solution)/shard_map/reduce_scatter | solution.py:250
  2687.8 184.6 %reduce-scatter.33.cloned.1.call-start = ((), (), s32[]{:S(2)}) async-start(), calls=%async_computation.31 | async-start | bytes 294912
  2689.5 221.8 %reduce-scatter.31.cloned.1.call-start = ((), (), s32[]{:S(2)}) async-start(), calls=%async_computation.30 | async-start | bytes 589824
  2693.7 262.0 %reduce-scatter.25.cloned.1.call-start = ((), (), s32[]{:S(2)}) async-start(), calls=%async_computation.26 | async-start | bytes 2359296 | tf_op jit(solution)/shard_map/reduce_scatter | solution.py:305
  2699.7 322.0 %reduce-scatter.23.cloned.1.call-start = ((), (), s32[]{:S(2)}) async-start(), calls=%async_computation.25 | async-start | bytes 7077888 | tf_op jit(solution)/shard_map/reduce_scatter | solution.py:302
  2712.7 357.8 %reduce-scatter.29.cloned.1.call-start = ((), (), s32[]{:S(2)}) async-start(), calls=%async_computation.28 | async-start | bytes 3244032 | tf_op jit(solution)/shard_map/reduce_scatter | solution.py:307
  2720.6 413.2 %reduce-scatter.27.cloned.1.call-start = ((), (), s32[]{:S(2)}) async-start(), calls=%async_computation.27 | async-start | bytes 6488064 | tf_op jit(solution)/shard_map/reduce_scatter | solution.py:306
  2841.2 18.1 all-to-all-start.3
  2859.3 141.9 %all-to-all-start.1 = ((bf16[8,64,1024]{2,1,0:T(8,128)(2,1)}), bf16[8,64,1024]{2,1,0:T(8,128)(2,1)S(1)}, u32[]{:S(2)}, u32[]{:S(2)}) async-start(bf16[8,64,1024]{2,1,0:T(8,128)(2,1)} %bitcast.548), calls=%async_computation.3 | async-start | bytes 2097152 | tf_op jit(solution)/shard_map/all_to_all | solution.py:320
  (117 other events, 2357.9 us)
Sparse Core Ops, SparseCore 0:
  10.5 39.0 all-gather.11
  51.7 80.7 all-gather.9
  135.0 21.9 all-gather.13
  850.2 142.9 reduce-scatter.14
  995.5 40.0 all-gather.17
  1037.6 80.7 all-gather.15
  1120.9 23.7 all-gather.19
  1146.3 80.7 all-gather.23
  1252.0 142.9 reduce-scatter.18
  1399.6 81.5 all-gather.21
  2679.7 75.2 reduce-scatter.20
  2757.3 77.2 reduce-scatter.16
  2838.2 34.1 reduce-scatter.32
  2876.2 35.0 reduce-scatter.30
  2914.4 41.2 reduce-scatter.24
  2959.3 62.3 reduce-scatter.22
  3025.5 44.9 reduce-scatter.28
  3074.7 58.9 reduce-scatter.26
where the time goes:
time: 3170 us; the launch traced here: 3140 us
  other arithmetic  978 us (31%)
  waiting for transfers between devices  949 us (30%)
  matrix products  627 us (20%)
  local copies, waits for them, and re-layouts  469 us (15%)
  blocking collectives  78.8 us (2%)
    another operation x256, other arithmetic, one_block(): jax.scipy.linalg.solve_triangular(lower_part, right_side, lower=True, uni...  638 us
    squeeze x256, local copies, waits for them, and re-layouts, delta_blocks(): outputs = lax.scan(jax.checkpoint(one_block), initial, block_items)[1]  187 us
    reduce_scatter x1, waiting for transfers between devices, body(): lax.psum_scatter(jnp.einsum('tcf,dcf->td', grad_pair, ffn_all, preferred_...  143 us
    reduce_scatter x1, waiting for transfers between devices, body(): lax.psum_scatter(jnp.einsum('thv,dhv->td', gated_out, out_all, preferred_...  141 us
    dot_general x128, matrix products, one_block(): jnp.einsum('ihk,jhk->hij', query_rows, block_of_keys, precision=highest_p...  109 us
    dot_general x128, matrix products, one_block(): jnp.einsum('grm,rmj->rgj', block_of_keys, recurrent_matrix, precision=hig...  101 us
    dot_general x128, matrix products, one_block(): jnp.einsum('grm,rmj->rgj', query_rows, recurrent_matrix, precision=highes...  95.9 us
    all_gather x1, waiting for transfers between devices, body(): lax.all_gather(normed_mid_f32.astype(jnp.bfloat16), 'tensor', axis=0, til...  82.8 us
  transfers between devices with their start and end apart: 21, of which 18 were waited for; matrix products, arithmetic and copies ran while one was open for 27% of the time, Pallas kernels for 0%

commit v1 on v0

v1 whole, which is shorter than its diff:
```python
import functools
import jax
import jax.numpy as jnp
from jax import lax
from jax.experimental import pallas as pl
from jax.experimental.pallas import tpu as pltpu
from jax.sharding import Mesh
from jax.sharding import PartitionSpec as P

DK = 128
DV = 256
SEQS = 3
CHUNK = 128
epsilon = 1e-06
f32 = jnp.float32
bf16 = jnp.bfloat16


def dot(a, b, ca=1, cb=0):
    return lax.dot_general(a, b, (((ca,), (cb,)), ((), ())), preferred_element_type=f32)


def halves(x):
    high = x.astype(bf16)
    return high, (x - high.astype(f32)).astype(bf16)


def dot1(a, b, ca=1, cb=0):
    return dot(a.astype(bf16), b.astype(bf16), ca, cb)


def dot3(a, b, ca=1, cb=0):
    ah, al = halves(a)
    bh, bl = halves(b)
    return dot(ah, bh, ca, cb) + (dot(ah, bl, ca, cb) + dot(al, bh, ca, cb))


def dot_exact(a, b, ca=1, cb=0):
    ah = a.astype(bf16)
    bh, bl = halves(b)
    bt = (b - bh.astype(f32) - bl.astype(f32)).astype(bf16)
    return dot(ah, bh, ca, cb) + (dot(ah, bl, ca, cb) + dot(ah, bt, ca, cb))


def sigmoid(x):
    return 1.0 / (1.0 + jnp.exp(-x))


def segment_of(position, ends):
    return sum((position >= e).astype(jnp.int32) for e in ends)


def iota(shape, axis):
    return lax.broadcasted_iota(jnp.int32, shape, axis)


def conv_masks(base, rows, ends, taps, sign):
    t = base + iota((rows, 1), 0)
    own = segment_of(t, ends)
    masks = []
    for j in range(1, taps):
        other = t - sign * j
        same = segment_of(other, ends) == own
        masks.append(jnp.where(same & (other >= 0), 1.0, 0.0))
    return masks


def chunk_terms(base, ends, g_col, g_row, q, k, beta):
    c = CHUNK
    ti = base + iota((c, 1), 0)
    tj = base + iota((1, c), 1)
    si = segment_of(ti, ends)
    sj = segment_of(tj, ends)
    ii = iota((c, c), 0)
    jj = iota((c, c), 1)
    decay = jnp.where((si == sj) & (ii >= jj), jnp.exp(jnp.minimum(g_col - g_row, 0.0)), 0.0)
    before = jnp.where(base > 0, segment_of(base - 1, ends), -1)
    last = segment_of(base + c - 1, ends)
    carry = jnp.where(si == before, jnp.exp(g_col), 0.0)
    g_last = g_col[c - 1 :, :]
    tail = jnp.where(si == last, jnp.exp(jnp.minimum(g_last - g_col, 0.0)), 0.0)
    return decay, carry, tail, ii, jj


def invert(lower, ii, jj, mul):
    first = ((ii ^ jj) == 1) & (ii > jj)
    eye = jnp.where(ii == jj, 1.0, 0.0)
    inv = [eye - jnp.where(first, a, 0.0) for a in lower]
    size = 2
    while size < CHUNK:
        joins = ((ii // (2 * size)) == (jj // (2 * size))) & ((ii & size) != 0) & ((jj & size) == 0)
        half = [mul(jnp.where(joins, a, 0.0), t) for a, t in zip(lower, inv)]
        inv = [t - mul(t, x) for t, x in zip(inv, half)]
        size *= 2
    return inv


def silu_parts(u):
    s = sigmoid(u)
    return u * s, s


def forward_kernel(
    ends_ref, proj_ref, taps_ref, rate_ref, shift_ref, gain_ref,
    gated_ref, o_ref, u_ref, s_ref, t_ref, qe_ref, m_ref,
    xs, state, *, heads, rows, taps,
):
    i = pl.program_id(0)
    wide = 2 * DK + DV
    full = wide + DV
    ends = [ends_ref[k] for k in range(SEQS)]
    base = i * rows
    c = CHUNK

    @pl.when(i == 0)
    def _():
        xs[0:8, :] = jnp.zeros((8, heads * wide), f32)
        state[...] = jnp.zeros_like(state)

    @pl.when(i > 0)
    def _():
        xs[0:8, :] = xs[rows : rows + 8, :]

    for h in range(heads):
        xs[8:, h * wide : (h + 1) * wide] = proj_ref[:, h * full : h * full + wide]
    small = proj_ref[:, heads * full :]
    beta_all = sigmoid(small)
    shifted = small + shift_ref[...]
    ld_all = -jnp.exp(rate_ref[...]) * (jnp.maximum(shifted, 0.0) + jnp.log1p(jnp.exp(-jnp.abs(shifted))))
    masks = conv_masks(base, rows, ends, taps, 1)
    qs, ks, vs = [], [], []
    for h in range(heads):
        sl = slice(h * wide, (h + 1) * wide)
        run = xs[8:, sl] * taps_ref[0:1, sl]
        for j in range(1, taps):
            run = run + (xs[8 - j : 8 - j + rows, sl] * masks[j - 1]) * taps_ref[j : j + 1, sl]
        act = run * sigmoid(run)
        q, k, v = act[:, :DK], act[:, DK : 2 * DK], act[:, 2 * DK :]
        qs.append(q * (lax.rsqrt(jnp.sum(q * q, axis=-1, keepdims=True) + epsilon) * DK ** (-0.5)))
        ks.append(k * lax.rsqrt(jnp.sum(k * k, axis=-1, keepdims=True) + epsilon))
        vs.append(v)
    lower_tri = jnp.where(iota((c, c), 0) >= iota((c, c), 1), 1.0, 0.0)
    n = rows // c
    probs = []
    for b in range(n):
        rs = slice(b * c, (b + 1) * c)
        g_all = dot_exact(lower_tri, ld_all[rs])
        g_t = g_all.T
        for h in range(heads):
            q, k, v = qs[h][rs], ks[h][rs], vs[h][rs]
            beta = beta_all[rs, 2 * h : 2 * h + 1]
            g_col = g_all[:, 2 * h + 1 : 2 * h + 2]
            g_row = g_t[2 * h + 1 : 2 * h + 2, :]
            decay, carry, tail, ii, jj = chunk_terms(base + b * c, ends, g_col, g_row, q, k, beta)
            qkk = DOT_QK(jnp.concatenate([q, k], axis=0), k, 1, 1)
            p = qkk[:c] * decay
            a = jnp.where(ii > jj, qkk[c:] * decay, 0.0) * beta
            probs.append(dict(b=b, h=h, q=q, k=k, v=v, beta=beta, carry=carry, tail=tail, p=p, a=a))
    inv = invert([x["a"] for x in probs], ii, jj, DOT_INV)
    for x, t in zip(probs, inv):
        x["t"] = t
        rhs = jnp.concatenate([(x["beta"] * x["carry"]) * x["k"], x["beta"] * x["v"]], axis=1)
        x["wv"] = DOT_WV(t, rhs)
    for x in probs:
        pwv = DOT_P(x["p"], x["wv"])
        x["qe"] = x["carry"] * x["q"] - pwv[:, :DK]
        x["pv"] = pwv[:, DK:]
        kwv = DOT_K(x["tail"] * x["k"], x["wv"], 0, 0)
        c_last = x["carry"][c - 1 :, :]
        x["m"] = jnp.where(ii == jj, c_last, 0.0) - kwv[:, :DK]
        x["bf"] = kwv[:, DK:]
    for x in probs:
        b, h = x["b"], x["h"]
        s = state[h]
        s_ref[b, h] = s
        t_ref[b, h] = x["t"]
        qe_ref[b, h] = x["qe"]
        m_ref[b, h] = x["m"]
        w = x["wv"][:, :DK]
        state[h] = x["bf"] + DOT_S(x["m"], s)
        wq = DOT_O(jnp.concatenate([w, x["qe"]], axis=0), s)
        u_ref[b * c : (b + 1) * c, h * DV : (h + 1) * DV] = x["wv"][:, DK:] - wq[:c]
        o_ref[b * c : (b + 1) * c, h * DV : (h + 1) * DV] = x["pv"] + wq[c:]
    live = jnp.where(segment_of(base + iota((rows, 1), 0), ends) < SEQS, 1.0, 0.0)
    for h in range(heads):
        o = o_ref[:, h * DV : (h + 1) * DV]
        z = proj_ref[:, h * full + wide : (h + 1) * full]
        r = lax.rsqrt(jnp.mean(o * o, axis=-1, keepdims=True) + epsilon)
        gated_ref[:, h * DV : (h + 1) * DV] = (o * (r * live) * gain_ref[...] * (z * sigmoid(z))).astype(bf16)


def backward_kernel(
    ends_ref, proj_ref, halo_ref, taps_ref, rate_ref, shift_ref, gain_ref,
    dgated_ref, o_ref, u_ref, s_ref, t_ref, qe_ref, m_ref,
    dproj_ref, dtaps_ref, dgain_ref, ddecay_ref,
    xs, ds, dstate, *, heads, rows, taps, blocks,
):
    step = pl.program_id(0)
    i = blocks - 1 - step
    wide = 2 * DK + DV
    full = wide + DV
    ends = [ends_ref[k] for k in range(SEQS)]
    base = i * rows
    c = CHUNK

    @pl.when(step == 0)
    def _():
        ds[...] = jnp.zeros_like(ds)
        dstate[...] = jnp.zeros_like(dstate)
        dtaps_ref[...] = jnp.zeros_like(dtaps_ref)
        dgain_ref[...] = jnp.zeros_like(dgain_ref)
        ddecay_ref[...] = jnp.zeros_like(ddecay_ref)

    @pl.when(step > 0)
    def _():
        ds[rows : rows + 8, :] = ds[0:8, :]

    for h in range(heads):
        xs[0:8, h * wide : (h + 1) * wide] = halo_ref[:, h * full : h * full + wide]
        xs[8:, h * wide : (h + 1) * wide] = proj_ref[:, h * full : h * full + wide]
    small = proj_ref[:, heads * full :]
    beta_all = sigmoid(small)
    shifted = small + shift_ref[...]
    rate = -jnp.exp(rate_ref[...])
    ld_all = rate * (jnp.maximum(shifted, 0.0) + jnp.log1p(jnp.exp(-jnp.abs(shifted))))
    masks = conv_masks(base, rows, ends, taps, 1)
    live = jnp.where(segment_of(base + iota((rows, 1), 0), ends) < SEQS, 1.0, 0.0)
    acts = []
    dos = []
    for h in range(heads):
        sl = slice(h * wide, (h + 1) * wide)
        run = xs[8:, sl] * taps_ref[0:1, sl]
        for j in range(1, taps):
            run = run + (xs[8 - j : 8 - j + rows, sl] * masks[j - 1]) * taps_ref[j : j + 1, sl]
        sg = sigmoid(run)
        act = run * sg
        dact = sg * (1.0 + run * (1.0 - sg))
        q, k, v = act[:, :DK], act[:, DK : 2 * DK], act[:, 2 * DK :]
        rq = lax.rsqrt(jnp.sum(q * q, axis=-1, keepdims=True) + epsilon)
        rk = lax.rsqrt(jnp.sum(k * k, axis=-1, keepdims=True) + epsilon)
        acts.append((q * rq, k * rk, v, dact, rq, rk))
        o = o_ref[:, h * DV : (h + 1) * DV]
        z = proj_ref[:, h * full + wide : (h + 1) * full]
        dg = dgated_ref[:, h * DV : (h + 1) * DV] * live
        r = lax.rsqrt(jnp.mean(o * o, axis=-1, keepdims=True) + epsilon)
        nrm = o * r
        sz = sigmoid(z)
        dz = dg * nrm * gain_ref[...] * (sz * (1.0 + z * (1.0 - sz)))
        dng = dg * (z * sz)
        dgain_ref[...] += jnp.sum((dng * nrm).reshape(rows // 8, 8, DV), axis=0)
        dn = dng * gain_ref[...]
        dos.append(r * (dn - nrm * jnp.mean(dn * nrm, axis=-1, keepdims=True)))
        dproj_ref[:, h * full + wide : (h + 1) * full] = dz.astype(bf16)
    low_i = iota((c, c), 0)
    low_j = iota((c, c), 1)
    lower_tri = jnp.where(low_i >= low_j, 1.0, 0.0)
    upper_tri = jnp.where(low_i <= low_j, 1.0, 0.0)
    strict_low = jnp.where(low_i > low_j, 1.0, 0.0)
    n = rows // c
    probs = []
    for b in reversed(range(n)):
        rs = slice(b * c, (b + 1) * c)
        g_all = dot_exact(lower_tri, ld_all[rs])
        g_t = g_all.T
        for h in range(heads):
            q, k, v = acts[h][0][rs] * DK ** (-0.5), acts[h][1][rs], acts[h][2][rs]
            beta = beta_all[rs, 2 * h : 2 * h + 1]
            g_col = g_all[:, 2 * h + 1 : 2 * h + 2]
            g_row = g_t[2 * h + 1 : 2 * h + 2, :]
            decay, carry, tail, ii, jj = chunk_terms(base + b * c, ends, g_col, g_row, q, k, beta)
            qkk = DOT_QK(jnp.concatenate([q, k], axis=0), k, 1, 1)
            p = qkk[:c] * decay
            dkk = jnp.where(ii > jj, qkk[c:] * decay, 0.0)
            do = dos[h][rs]
            u = u_ref[rs, h * DV : (h + 1) * DV]
            dp = DOT_B(do, u, 1, 1)
            pdo = DOT_B(p, do, 0, 0)
            qdo = DOT_B(qe_ref[b, h], do, 0, 0)
            f = DOT_B(do, s_ref[b, h], 1, 1)
            probs.append(dict(b=b, h=h, q=q, k=k, v=v, beta=beta, carry=carry, tail=tail, decay=decay, p=p, dkk=dkk,
                              do=do, u=u, dp=dp, pdo=pdo, qdo=qdo, f=f))
    for x in probs:
        b, h = x["b"], x["h"]
        dnext = dstate[h]
        x["dnext"] = dnext
        dstate[h] = DOT_S(m_ref[b, h], dnext, 0, 0) + x["qdo"]
    for x in probs:
        du = x["pdo"] + DOT_B(x["tail"] * x["k"], x["dnext"])
        x["dr"] = DOT_B(t_ref[x["b"], x["h"]], du, 0, 0)
        x["j"] = DOT_B(x["u"], x["dnext"], 1, 1)
    dq_all = [[None] * n for _ in range(heads)]
    dk_all = [[None] * n for _ in range(heads)]
    dv_all = [[None] * n for _ in range(heads)]
    dsmall = [[None] * heads for _ in range(n)]
    lane = iota((c, DK), 1)
    for x in probs:
        b, h, q, k, beta, carry = x["b"], x["h"], x["q"], x["k"], x["beta"], x["carry"]
        dr = x["dr"]
        s = s_ref[b, h]
        neg = DOT_B(dr, x["u"], 1, 1)
        hh = DOT_B(dr, s, 1, 1)
        neg = jnp.where(ii > jj, neg, 0.0)
        adk = neg * x["dkk"]
        dbeta = (
            jnp.sum(dr * x["v"], axis=-1, keepdims=True)
            - carry * jnp.sum(k * hh, axis=-1, keepdims=True)
            - jnp.sum(adk, axis=-1, keepdims=True)
        )
        dcarry = jnp.sum(q * x["f"], axis=-1, keepdims=True) - beta * jnp.sum(k * hh, axis=-1, keepdims=True)
        e = x["dp"] * x["p"] - beta * adk
        dqk = x["dp"] * x["decay"]
        dkk = -(neg * beta) * jnp.where(ii > jj, x["decay"], 0.0)
        dtail = x["tail"] * jnp.sum(k * x["j"], axis=-1, keepdims=True)
        dcl = carry[c - 1 :, :] * jnp.sum(x["dnext"] * s, keepdims=True)
        col = carry * dcarry + jnp.where(iota((c, 1), 0) == c - 1, dcl, 0.0)
        straddle = jnp.where(ii > jj, dot_exact(upper_tri, e), 0.0)
        both = dot_exact(upper_tri, jnp.where(lane == 0, col, 0.0)) + dot_exact(
            strict_low, jnp.where(lane == 0, dtail, 0.0)
        )
        dld = jnp.sum(straddle, axis=-1, keepdims=True) + both[:, 0:1]
        dq_all[h][b] = carry * x["f"] + DOT_B(dqk, k)
        dk_all[h][b] = (
            x["tail"] * x["j"] - (carry * beta) * hh + DOT_B(dqk, q, 0, 0) + DOT_B(dkk, k) + DOT_B(dkk, k, 0, 0)
        )
        dv_all[h][b] = beta * dr
        dsmall[b][h] = (dbeta, dld)
    for b in range(n):
        rs = slice(b * c, (b + 1) * c)
        tile = jnp.zeros((c, DK), f32)
        for h in range(heads):
            dbeta, dld = dsmall[b][h]
            tile = jnp.where(lane == 2 * h, dbeta, jnp.where(lane == 2 * h + 1, dld, tile))
        bet = beta_all[rs]
        dshift = rate * tile * sigmoid(shifted[rs])
        even = (lane & 1) == 0
        inside = lane < 2 * heads
        ddecay_ref[0:8, :] += jnp.sum(jnp.where(even, 0.0, tile * ld_all[rs]).reshape(c // 8, 8, DK), axis=0)
        ddecay_ref[8:16, :] += jnp.sum(jnp.where(even, 0.0, dshift).reshape(c // 8, 8, DK), axis=0)
        dproj_ref[rs, heads * full :] = jnp.where(
            inside, jnp.where(even, tile * (bet * (1.0 - bet)), dshift), 0.0
        ).astype(bf16)
    for h in range(heads):
        qn, kn, v, dact, rq, rk = acts[h]
        dq = jnp.concatenate(dq_all[h], axis=0) * DK ** (-0.5)
        dk = jnp.concatenate(dk_all[h], axis=0)
        dq = rq * (dq - qn * jnp.sum(dq * qn, axis=-1, keepdims=True))
        dk = rk * (dk - kn * jnp.sum(dk * kn, axis=-1, keepdims=True))
        dv = jnp.concatenate(dv_all[h], axis=0)
        o = h * wide
        ds[0:rows, o : o + DK] = dq * dact[:, :DK]
        ds[0:rows, o + DK : o + 2 * DK] = dk * dact[:, DK : 2 * DK]
        ds[0:rows, o + 2 * DK : o + wide] = dv * dact[:, 2 * DK :]
    ahead = conv_masks(base, rows, ends, taps, -1)
    for h in range(heads):
        sl = slice(h * wide, (h + 1) * wide)
        own = ds[0:rows, sl]
        total = own * taps_ref[0:1, sl]
        dtaps_ref[0:8, sl] += jnp.sum((own * xs[8:, sl]).reshape(rows // 8, 8, wide), axis=0)
        for j in range(1, taps):
            total = total + (ds[j : j + rows, sl] * ahead[j - 1]) * taps_ref[j : j + 1, sl]
            dtaps_ref[8 * j : 8 * j + 8, sl] += jnp.sum(
                (own * (xs[8 - j : 8 - j + rows, sl] * masks[j - 1])).reshape(rows // 8, 8, wide), axis=0
            )
        dproj_ref[:, h * full : h * full + wide] = total.astype(bf16)


DOT_QK = dot3
DOT_INV = dot3
DOT_WV = dot3
DOT_P = dot3
DOT_K = dot3
DOT_S = dot3
DOT_O = dot3
DOT_B = dot3


def mixer_forward(ends, proj, taps, rate, shift, gain, *, heads, rows):
    total, width = proj.shape
    blocks = total // rows
    n = rows // CHUNK
    row = lambda i, e: (i, 0)
    same = lambda i, e: (0, 0)
    quad = lambda i, e: (i, 0, 0, 0)
    wide = 2 * DK + DV
    chunks = total // CHUNK
    kernel = functools.partial(forward_kernel, heads=heads, rows=rows, taps=taps.shape[0])
    return pl.pallas_call(
        kernel,
        grid_spec=pltpu.PrefetchScalarGridSpec(
            num_scalar_prefetch=1,
            grid=(blocks,),
            in_specs=[
                pl.BlockSpec((rows, width), row),
                pl.BlockSpec(taps.shape, same),
                pl.BlockSpec(rate.shape, same),
                pl.BlockSpec(shift.shape, same),
                pl.BlockSpec(gain.shape, same),
            ],
            out_specs=[
                pl.BlockSpec((rows, heads * DV), row),
                pl.BlockSpec((rows, heads * DV), row),
                pl.BlockSpec((rows, heads * DV), row),
                pl.BlockSpec((n, heads, DK, DV), quad),
                pl.BlockSpec((n, heads, CHUNK, CHUNK), quad),
                pl.BlockSpec((n, heads, CHUNK, DK), quad),
                pl.BlockSpec((n, heads, DK, DK), quad),
            ],
            scratch_shapes=[
                pltpu.VMEM((rows + 8, heads * wide), f32),
                pltpu.VMEM((heads, DK, DV), f32),
            ],
        ),
        out_shape=[
            jax.ShapeDtypeStruct((total, heads * DV), bf16),
            jax.ShapeDtypeStruct((total, heads * DV), f32),
            jax.ShapeDtypeStruct((total, heads * DV), f32),
            jax.ShapeDtypeStruct((chunks, heads, DK, DV), f32),
            jax.ShapeDtypeStruct((chunks, heads, CHUNK, CHUNK), f32),
            jax.ShapeDtypeStruct((chunks, heads, CHUNK, DK), f32),
            jax.ShapeDtypeStruct((chunks, heads, DK, DK), f32),
        ],
        compiler_params=pltpu.CompilerParams(
            dimension_semantics=("arbitrary",), vmem_limit_bytes=56 * 1024 * 1024
        ),
        name="mixer_forward",
    )(ends, proj, taps, rate, shift, gain)


def mixer_backward(ends, proj, taps, rate, shift, gain, dgated, saved, *, heads, rows):
    total, width = proj.shape
    blocks = total // rows
    n = rows // CHUNK
    row = lambda s, e: (blocks - 1 - s, 0)
    halo = lambda s, e: (jnp.maximum((blocks - 1 - s) * (rows // 8) - 1, 0), 0)
    same = lambda s, e: (0, 0)
    quad = lambda s, e: (blocks - 1 - s, 0, 0, 0)
    wide = 2 * DK + DV
    kernel = functools.partial(backward_kernel, heads=heads, rows=rows, taps=taps.shape[0], blocks=blocks)
    return pl.pallas_call(
        kernel,
        grid_spec=pltpu.PrefetchScalarGridSpec(
            num_scalar_prefetch=1,
            grid=(blocks,),
            in_specs=[
                pl.BlockSpec((rows, width), row),
                pl.BlockSpec((8, width), halo),
                pl.BlockSpec(taps.shape, same),
                pl.BlockSpec(rate.shape, same),
                pl.BlockSpec(shift.shape, same),
                pl.BlockSpec(gain.shape, same),
                pl.BlockSpec((rows, heads * DV), row),
                pl.BlockSpec((rows, heads * DV), row),
                pl.BlockSpec((rows, heads * DV), row),
                pl.BlockSpec((n, heads, DK, DV), quad),
                pl.BlockSpec((n, heads, CHUNK, CHUNK), quad),
                pl.BlockSpec((n, heads, CHUNK, DK), quad),
                pl.BlockSpec((n, heads, DK, DK), quad),
            ],
            out_specs=[
                pl.BlockSpec((rows, width), row),
                pl.BlockSpec((32, heads * wide), same),
                pl.BlockSpec((8, DV), same),
                pl.BlockSpec((16, 128), same),
            ],
            scratch_shapes=[
                pltpu.VMEM((rows + 8, heads * wide), f32),
                pltpu.VMEM((rows + 8, heads * wide), f32),
                pltpu.VMEM((heads, DK, DV), f32),
            ],
        ),
        out_shape=[
            jax.ShapeDtypeStruct((total, width), bf16),
            jax.ShapeDtypeStruct((32, heads * wide), f32),
            jax.ShapeDtypeStruct((8, DV), f32),
            jax.ShapeDtypeStruct((16, 128), f32),
        ],
        compiler_params=pltpu.CompilerParams(
            dimension_semantics=("arbitrary",), vmem_limit_bytes=56 * 1024 * 1024
        ),
        name="mixer_backward",
    )(ends, proj, proj, taps, rate, shift, gain, dgated, *saved)


BLOCK_ROWS = 256


def rms_scale(values):
    return lax.rsqrt(jnp.mean(values * values, axis=-1, keepdims=True) + epsilon)


def norm_back(values, scale, gain, grad):
    u = gain * grad
    back = scale * u - values * (scale * scale * scale) * jnp.mean(values * u, axis=-1, keepdims=True)
    return back, jnp.sum(grad * (values * scale), axis=0)


def swap(x, axis, bit):
    size = lax.axis_size(axis)
    return lax.ppermute(x, axis, [(i, i ^ bit) for i in range(size)])


def exchange_roles(x):
    n = lax.axis_size("lo")
    return lax.ppermute(x, ("lo", "tensor"), [(a * n + b, b * n + a) for a in range(n) for b in range(n)])


def bits(size):
    return [1 << k for k in range(size.bit_length() - 1)]


def gather_rows(x):
    pieces = {0: x}
    for bit in reversed(bits(lax.axis_size("lo"))):
        pieces.update({k ^ bit: swap(p, "lo", bit) for k, p in list(pieces.items())})
    return jnp.concatenate([pieces[k] for k in sorted(pieces)], axis=0)


def scatter_sum(x):
    n = lax.axis_size("lo")
    rows = x.shape[0] // n
    held = {k: x[k * rows : (k + 1) * rows] for k in range(n)}
    for bit in bits(n):
        sent = [k for k in held if k & bit]
        sums = {}
        for k in sent:
            got = swap(held[k].astype(x.dtype), "lo", bit)
            sums[k ^ bit] = held[k ^ bit].astype(f32) + got.astype(f32)
        held = sums
    return held[0]


def sum_everywhere(x):
    for axis in ("lo", "tensor", "hi"):
        for bit in bits(lax.axis_size(axis)):
            x = x + swap(x, axis, bit)
    return x


def rank_of(key):
    return jnp.sum((key[..., None, :] < key[..., :, None]).astype(jnp.int32), axis=-1)


def after(x, *first):
    return lax.optimization_barrier((x, first))[0]


def widen(columns):
    return lax.all_gather(exchange_roles(columns), ("hi", "tensor"), axis=0, tiled=True)


def narrow(columns):
    return exchange_roles(
        lax.psum_scatter(columns.astype(bf16), ("hi", "tensor"), scatter_dimension=0, tiled=True)
    ).astype(f32)


def product(a, b, ca=1, cb=0, dtype=f32):
    return lax.dot_general(a, b, (((ca,), (cb,)), ((), ())), preferred_element_type=f32).astype(dtype)


def body(
    tokens,
    cotangent,
    lengths,
    token_order,
    token_return,
    w_mix,
    w_ba,
    conv_w,
    w_out,
    w_gate_up,
    w_down,
    gain_attn,
    gain_ffn,
    gain_out,
    decay_log,
    decay_bias,
):
    splits = lax.axis_size("lo")
    groups = lax.axis_size("hi") * splits
    me = lax.axis_index("lo")
    local_rows, model_width = tokens.shape
    group_rows = local_rows * splits
    per_peer = local_rows // groups
    weight_rows, heads, head_width = w_mix.shape
    units = w_down.shape[1]
    taps = conv_w.shape[2]
    conv_width = head_width - DV
    proj_width = heads * head_width

    spread = ("hi", "tensor")
    width = lax.axis_size("hi")
    span = jnp.arange(local_rows, dtype=jnp.int32)

    send_rank = rank_of(token_return // group_rows * local_rows + token_return % local_rows)
    send_hot = (span[:, None] == send_rank[None, :]).astype(bf16)

    def across(rows):
        moved = lax.all_to_all(
            rows.reshape(groups, per_peer, model_width), spread, split_axis=0, concat_axis=0, tiled=True
        )
        return moved.reshape(local_rows, model_width)

    def pack(rows):
        return across(product(send_hot, rows, dtype=bf16))

    def unpack(rows):
        return product(send_hot, across(rows), 0, 0, bf16)

    orders = gather_rows(exchange_roles(token_order)).reshape(splits, local_rows)
    orders = jnp.take(orders, jnp.arange(splits, dtype=jnp.int32) ^ me, axis=0)
    given = orders // group_rows
    place_of = rank_of(given * local_rows + span[None, :]) % per_peer
    held_at = (((given % splits) ^ me) * width + given // splits) * per_peer + place_of
    order_hot = (held_at[:, :, None] == span[None, None, :]).astype(bf16)

    def to_sequence(rows):
        parts = rows.reshape(splits * width, splits, per_peer, -1)
        parts = jnp.transpose(parts, (1, 0, 2, 3)).reshape(splits, local_rows, -1)
        return lax.dot_general(
            order_hot, parts, (((2,), (1,)), ((0,), (0,))), preferred_element_type=f32
        ).astype(bf16).reshape(group_rows, -1)

    def from_sequence(rows):
        parts = lax.dot_general(
            order_hot, rows.reshape(splits, local_rows, -1), (((1,), (1,)), ((0,), (0,))), preferred_element_type=f32
        ).astype(bf16).reshape(splits, splits * width, per_peer, -1)
        return jnp.transpose(parts, (1, 0, 2, 3)).reshape(group_rows, -1)

    own_lengths = exchange_roles(lengths)
    ends = jnp.sum(jnp.where(jnp.tri(SEQS, dtype=bool), own_lengths, 0), axis=1).astype(jnp.int32)
    spare = 128 - heads * w_ba.shape[2] - taps
    mix_all = widen(
        jnp.concatenate(
            [
                w_mix.reshape(weight_rows, proj_width).astype(bf16),
                w_ba.reshape(weight_rows, -1).astype(bf16),
                conv_w.reshape(weight_rows, taps).astype(bf16),
                jnp.zeros((weight_rows, spare), bf16),
            ],
            axis=1,
        )
    )
    packed_in = pack(tokens)
    out_all = widen(after(w_out.reshape(weight_rows, heads * DV).astype(bf16), packed_in))
    ffn_all = widen(
        after(
            jnp.concatenate(
                [w_gate_up.reshape(weight_rows, 2 * units).astype(bf16), w_down.astype(bf16)], axis=1
            ),
            packed_in,
        )
    )

    input_f32 = packed_in.astype(f32)
    input_scale = rms_scale(input_f32)
    gathered = gather_rows((input_f32 * input_scale * gain_attn).astype(bf16))
    packed_grad = pack(after(cotangent, gathered))
    normed_seq = to_sequence(gathered)

    small_at = proj_width
    conv_at = small_at + heads * w_ba.shape[2]
    conv_all = mix_all[:, conv_at : conv_at + taps].reshape(-1, heads, taps).astype(f32)
    tap_rows = jnp.transpose(conv_all, (2, 1, 0)).reshape(taps, heads * conv_width)
    projected = product(normed_seq, mix_all)
    head_start = me * heads
    lanes = jnp.zeros((1, 128), f32)
    rate_row = lanes.at[0, 1 : 2 * heads : 2].set(lax.dynamic_slice_in_dim(decay_log, head_start, heads))
    shift_row = lanes.at[0, 1 : 2 * heads : 2].set(lax.dynamic_slice_in_dim(decay_bias, head_start, heads))
    gain_row = gain_out[None]
    saved = mixer_forward(
        ends, projected, tap_rows, rate_row, shift_row, gain_row, heads=heads, rows=BLOCK_ROWS
    )
    grad_all = gather_rows(packed_grad)
    gated = saved[0]
    middle = input_f32 + scatter_sum(product(from_sequence(gated), out_all, 1, 1))
    mid_scale = rms_scale(middle)
    normed_mid_all = gather_rows((middle * mid_scale * gain_ffn).astype(bf16))

    in_sequence = jnp.arange(group_rows, dtype=jnp.int32).reshape(splits, local_rows, 1) < ends[SEQS - 1]
    live = from_sequence(jnp.broadcast_to(in_sequence, (splits, local_rows, 128)).astype(bf16))[:, :1].astype(f32)
    w_pair = ffn_all[:, : 2 * units]
    w_last = ffn_all[:, 2 * units :]
    grad_hidden = product(grad_all, w_last) * live
    gate_up = product(normed_mid_all, w_pair)
    gate, up = gate_up[:, :units], gate_up[:, units:]
    s = sigmoid(gate)
    hidden = (gate * s * up * live).astype(bf16)
    grad_pair = jnp.concatenate(
        [grad_hidden * up * (s * (1.0 + gate * (1.0 - s))), grad_hidden * (gate * s)], axis=1
    ).astype(bf16)
    grad_norm_terms = product(grad_pair, w_pair, 1, 1, bf16)
    grad_norm_mid = scatter_sum(grad_norm_terms)
    hidden, grad_pair = after((hidden, grad_pair), grad_norm_terms)
    grad_ffn = jnp.concatenate(
        [product(normed_mid_all, grad_pair, 0, 0, bf16), product(grad_all, hidden, 0, 0, bf16)], axis=1
    )
    layer_terms = product(hidden, w_last, 1, 1, bf16)
    grad_mid_norm, grad_gain_ffn = norm_back(middle, mid_scale, gain_ffn, grad_norm_mid)
    grad_middle = packed_grad.astype(f32) + grad_mid_norm
    grad_middle_all = gather_rows(after(grad_middle.astype(bf16), grad_ffn, layer_terms))
    grad_ffn = narrow(grad_ffn)

    grad_middle_seq = to_sequence(grad_middle_all)
    grad_gated = product(grad_middle_seq, out_all)
    grad_out_w = product(grad_middle_seq, gated, 0, 0, bf16)
    grad_gated, layer_terms = after((grad_gated, layer_terms), grad_out_w)
    grad_out_w = narrow(grad_out_w)
    layer_out = unpack((middle + scatter_sum(layer_terms)).astype(bf16))
    grad_proj, grad_taps, grad_gain_out, grad_decay = mixer_backward(
        ends, projected, tap_rows, rate_row, shift_row, gain_row, grad_gated, saved[1:],
        heads=heads, rows=BLOCK_ROWS,
    )
    grad_conv = jnp.sum(grad_taps.reshape(taps, 8, heads, conv_width), axis=1)
    grad_conv = jnp.transpose(grad_conv, (2, 1, 0)).reshape(-1, taps).astype(bf16)
    grad_mix = product(normed_seq, grad_proj, 0, 0, bf16)
    grad_mix = jnp.concatenate([grad_mix[:, :conv_at], grad_conv, grad_mix[:, conv_at + taps :]], axis=1)
    grad_normed = scatter_sum(from_sequence(product(after(grad_proj, grad_mix), mix_all, 1, 1, bf16)))
    grad_mix = narrow(grad_mix)
    grad_input_norm, grad_gain_attn = norm_back(input_f32, input_scale, gain_attn, grad_normed)
    input_grad = unpack((grad_middle + grad_input_norm).astype(bf16))

    head_total = decay_log.shape[0]
    decay_sums = jnp.sum(grad_decay.reshape(2, 8, 128), axis=1)[:, 1 : 2 * heads : 2]
    decay_full = lax.dynamic_update_slice(jnp.zeros((2, head_total), f32), decay_sums, (0, head_start))
    flat = jnp.concatenate(
        [grad_gain_attn, grad_gain_ffn, jnp.sum(grad_gain_out, axis=0), decay_full.reshape(-1)]
    )
    flat = sum_everywhere(jnp.pad(flat, (0, -flat.shape[0] % 1024)).reshape(8, -1)).reshape(-1)
    at = 0
    sums = []
    for size in (model_width, model_width, gain_out.shape[0], head_total, head_total):
        sums.append(flat[at : at + size])
        at += size
    return (
        layer_out,
        input_grad,
        grad_mix[:, :small_at].reshape(w_mix.shape),
        grad_mix[:, small_at:conv_at].reshape(w_ba.shape),
        grad_mix[:, conv_at : conv_at + taps].reshape(conv_w.shape),
        grad_out_w.reshape(w_out.shape),
        grad_ffn[:, : 2 * units].reshape(w_gate_up.shape),
        grad_ffn[:, 2 * units :],
        *sums,
    )


def solution(mesh):
    dp, splits = mesh.shape["dp"], mesh.shape["tensor"]
    roles = Mesh(mesh.devices.reshape(dp // splits, splits, splits), ("hi", "lo", "tensor"))
    group = ("hi", "lo")
    rows = P((*group, "tensor"))
    by_head = P(group, "tensor", None)
    by_unit = (P(group, None, "tensor"), P(group, "tensor"))
    return jax.shard_map(
        body,
        mesh=roles,
        in_specs=(rows, rows, P(group), rows, rows, by_head, by_head, by_head, by_head, *by_unit)
        + (P(),) * 5,
        out_specs=(rows, rows, by_head, by_head, by_head, by_head, *by_unit) + (P(),) * 5,
        check_vma=False,
    )
```

time: 3170 us -> 785 us (0.25)
  other arithmetic: 978 us -> 46.1 us
  waiting for transfers between devices: 949 us -> 318 us
  matrix products: 627 us -> 128 us
  local copies, waits for them, and re-layouts: 469 us -> 47.9 us
  Pallas kernels: 0 us -> 124 us
  starting transfers between devices: 14.6 us -> 58.4 us
  blocking collectives: 78.8 us -> 41.4 us
    another operation x418 -> x0, other arithmetic: 711 us -> none  [the longest x256 638 us: one_block(): jax.scipy.linalg.solve_triangular(lower_part, right_side, lower=True, uni...]
    reduce_scatter x8 -> x3, waiting for transfers between devices: 553 us -> 32.3 us  [narrow(): lax.psum_scatter(columns.astype(bf16), ('hi', 'tensor'), scatter_dimensio...]
    dot_general x751 -> x21, matrix products: 566 us -> 128 us  [the longest x16 115 us: product(): lax.dot_general(a, b, (((ca,), (cb,)), ((), ())), preferred_element_type=...]
    all_gather x8 -> x3, waiting for transfers between devices: 337 us -> 0.02 us  [widen(): lax.all_gather(exchange_roles(columns), ('hi', 'tensor'), axis=0, tiled=T...]
    ppermute x0 -> x40, waiting for transfers between devices: none -> 276 us  [the longest x32 220 us: swap(): return lax.ppermute(x, axis, [(i, i ^ bit) for i in range(size)])]
    squeeze x257 -> x0, local copies, waits for them, and re-layouts: 188 us -> none  [the longest x256 187 us: delta_blocks(): outputs = lax.scan(jax.checkpoint(one_block), initial, block_items)[1]]
    pallas_call x0 -> x2, Pallas kernels: none -> 124 us  [the longest x1 76.9 us: mixer_backward(): pl.pallas_call(kernel, grid_spec=pltpu.PrefetchScalarGridSpec(num_scalar_...]
    dynamic_slice x65 -> x2, local copies, waits for them, and re-layouts: 79.4 us -> 0.15 us  [the longest x1 0.07 us: body(): lax.dynamic_slice_in_dim(decay_bias, head_start, heads)]
  transfers between devices with their start and end apart: 21 -> 49, of which waited for: 18 -> 25; matrix products, arithmetic and copies ran while one was open for 27% -> 20% of each run, Pallas kernels for 0% -> 16%
where the time goes in v1:
time: 785 us; the launch traced here: 780 us
  waiting for transfers between devices  318 us (41%)
  matrix products  128 us (16%)
  Pallas kernels  124 us (16%)
  starting transfers between devices  58.4 us (7%)
  local copies, waits for them, and re-layouts  47.9 us (6%)
  other arithmetic  46.1 us (6%)
  blocking collectives  41.4 us (5%)
  between operations  15.1 us (2%)
    ppermute x32, waiting for transfers between devices, swap(): return lax.ppermute(x, axis, [(i, i ^ bit) for i in range(size)])  220 us
    dot_general x16, matrix products, product(): lax.dot_general(a, b, (((ca,), (cb,)), ((), ())), preferred_element_type=...  115 us
    pallas_call x1, Pallas kernels, mixer_backward(): pl.pallas_call(kernel, grid_spec=pltpu.PrefetchScalarGridSpec(num_scalar_...  76.9 us
    ppermute x8, waiting for transfers between devices, exchange_roles(): lax.ppermute(x, ('lo', 'tensor'), [(a * n + b, b * n + a) for a in range(...  55.4 us
    pallas_call x1, Pallas kernels, mixer_forward(): pl.pallas_call(kernel, grid_spec=pltpu.PrefetchScalarGridSpec(num_scalar_...  47.4 us
    all_to_all x1, blocking collectives, across(): lax.all_to_all(rows.reshape(groups, per_peer, model_width), spread, split...  41.4 us
    reduce_scatter x3, waiting for transfers between devices, narrow(): lax.psum_scatter(columns.astype(bf16), ('hi', 'tensor'), scatter_dimensio...  32.3 us
    ppermute x8, starting transfers between devices, exchange_roles(): lax.ppermute(x, ('lo', 'tensor'), [(a * n + b, b * n + a) for a in range(...  29.8 us
  transfers between devices with their start and end apart: 49, of which 25 were waited for; matrix products, arithmetic and copies ran while one was open for 20% of the time, Pallas kernels for 16%

profile of v1, /device:TPU:2, one launch (start us, length us, event | category | flops | bytes accessed | tf_op | source)
XLA Modules:
  0.0 779.9 jit_solution(11266347085930102686)
XLA Ops:
  15.0 20.6 %collective-permute-done.8 = bf16[128,1664]{1,0:T(8,128)(2,1)S(1)} collective-permute-done((bf16[128,1664]{1,0:T(8,128)(2,1)S(1)}, bf16[128,1664]{1,0:T(8,128)(2,1)S(1)}, u32[]{:S(2)}, u32[]{:S(2)}) %collective-permute-start.8) | collective-permute-done | bytes 426016 | tf_op jit(solution)/shard_map/ppermute | solution.py:504
  38.2 41.4 %all_to_all.20 = bf16[8,64,1024]{2,1,0:T(8,128)(2,1)S(1)} all-to-all(bf16[8,64,1024]{2,1,0:T(8,128)(2,1)S(1)} %bitcast.131), channel_id=1, replica_groups=mesh['hi'=2,'lo'=4,'tensor'=4] {'hi','tensor'}, dimensions={0} | all-to-all | bytes 2097152 | tf_op jit(solution)/shard_map/all_to_all | solution.py:599
  93.3 13.3 %collective-permute-done.6 = bf16[512,1024]{1,0:T(8,128)(2,1)S(1)} collective-permute-done((bf16[512,1024]{1,0:T(8,128)(2,1)S(1)}, bf16[512,1024]{1,0:T(8,128)(2,1)S(1)}, u32[]{:S(2)}, u32[]{:S(2)}) %collective-permute-start.6) | collective-permute-done | bytes 1048608 | tf_op jit(solution)/shard_map/ppermute | solution.py:499
  122.2 14.6 %collective-permute-done.9 = bf16[128,512]{1,0:T(8,128)(2,1)S(1)} collective-permute-done((bf16[128,512]{1,0:T(8,128)(2,1)S(1)}, bf16[128,512]{1,0:T(8,128)(2,1)S(1)}, u32[]{:S(2)}, u32[]{:S(2)}) %collective-permute-start.9) | collective-permute-done | bytes 131104 | tf_op jit(solution)/shard_map/ppermute | solution.py:504
  146.9 13.3 %fusion.71.proj_ref.halo_ref = f32[2048,1664]{1,0:T(8,128)} fusion(bf16[2048,1024]{1,0:T(8,128)(2,1)} %bitcast.153, bf16[1024,1664]{1,0:T(8,128)(2,1)} %all-gather.4.cloned.1.call-done), kind=kOutput, calls=%fused_computation.164 | convolution fusion | flops 6979321856 | bytes 21233664 | tf_op jit(solution)/shard_map/dot_general | solution.py:558
  160.2 47.4 %mixer_forward.1 = (bf16[2048,512]{1,0:T(8,128)(2,1)}, f32[2048,512]{1,0:T(8,128)}, f32[2048,512]{1,0:T(8,128)}, f32[16,2,128,256]{3,2,1,0:T(8,128)}, f32[16,2,1...) custom-call(s32[3]{0:T(128)} %select_reduce_fusion.ends_ref, ...), custom_call_target="tpu_custom_call" | custom-call | tf_op jit(solution)/shard_map/mixer_forward/pallas_call | solution.py:387
  219.5 5.9 collective-permute-done.11
  238.3 39.4 %collective-permute-done.12 = f32[512,1024]{1,0:T(8,128)} collective-permute-done((f32[512,1024]{1,0:T(8,128)}, f32[512,1024]{1,0:T(8,128)}, u32[]{:S(2)}, u32[]{:S(2)}) %collective-permute-start.12) | collective-permute-done | bytes 2097184 | tf_op jit(solution)/shard_map/ppermute | solution.py:499
  284.3 24.4 %collective-permute-done.18 = bf16[512,1024]{1,0:T(8,128)(2,1)} collective-permute-done((bf16[512,1024]{1,0:T(8,128)(2,1)}, bf16[512,1024]{1,0:T(8,128)(2,1)}, u32[]{:S(2)}, u32[]{:S(2)}) %collective-permute-start.18) | collective-permute-done | bytes 1048608 | tf_op jit(solution)/shard_map/ppermute | solution.py:499
  312.1 17.3 %collective-permute-done.14 = bf16[512,1024]{1,0:T(8,128)(2,1)} collective-permute-done((bf16[512,1024]{1,0:T(8,128)(2,1)}, bf16[512,1024]{1,0:T(8,128)(2,1)}, u32[]{:S(2)}, u32[]{:S(2)}) %collective-permute-start.14) | collective-permute-done | bytes 1048608 | tf_op jit(solution)/shard_map/ppermute | solution.py:499
  329.4 13.7 %fusion.10 = f32[2048,1408]{0,1:T(8,128)} fusion(bf16[1024,2112]{0,1:T(8,128)(2,1)} %all-gather.8.cloned.1.call-done, bf16[512,1024]{1,0:T(8,128)(2,1)} %collective-permute-done.19, bf16[512,1024]{1,0:T(8,128)(2,1)} %collective-permute-done.18, bf16[512,1024]{1,0:T(8,128)(2,1)} %collective-permute-done.17, bf16[512,1024]{1,0:T(8,128)(2,1)} %multiply_convert_fusion.3), kind=kOutput, calls=%fused_computation.35 | convolution fusion | flops 5922357248 | bytes 18612224 | tf_op jit(solution)/shard_map/dot_general | solution.py:558
  343.1 11.7 %multiply_convert_fusion.2 = (bf16[2048,704]{0,1:T(8,128)(2,1)S(1)}, bf16[2048,704]{0,1:T(8,128)(2,1)S(1)}, bf16[2048,704]{0,1:T(8,128)(2,1)}) fusion(f32[2048,1408]{0,1:T(8,128)} %fusion.10, f32[2048]{0:T(1024)S(1)} %convert_reduce_fusion.1, bf16[1024,2112]{0,1:T(8,128)(2,1)S(1)} %copy-done.25, bf16[512,1024]{1,0:T(8,128)(2,1)} %collective-permute-done.15, ...), kind=kOutput, calls=%fused_computation.6 | convolution fusion | flops 2994077696 | bytes 25829376 | tf_op jit(solution)/shard_map/dot_general | solution.py:558
  357.8 7.4 convolution_convert_fusion.3
  369.7 6.5 convolution_convert_fusion.5
  379.3 10.4 %convolution_convert_fusion = bf16[1024,1408]{1,0:T(8,128)(2,1)S(1)} fusion(bf16[2048,1408]{0,1:T(8,128)(2,1)} %pad_maximum_fusion, bf16[512,1024]{1,0:T(8,128)(2,1)} %collective-permute-done.19, bf16[512,1024]{1,0:T(8,128)(2,1)} %collective-permute-done.18, bf16[512,1024]{1,0:T(8,128)(2,1)} %collective-permute-done.17, ...), kind=kOutput, calls=%fused_computation.22 | convolution fusion | flops 5923799040 | bytes 12845056 | tf_op jit(solution)/shard_map/dot_general | solution.py:558
  395.4 7.8 %convolution_convert_fusion.2 = bf16[2048,1024]{1,0:T(8,128)(2,1)} fusion(bf16[2048,704]{0,1:T(8,128)(2,1)} %get-tuple-element.38, bf16[1024,2112]{0,1:T(8,128)(2,1)} %all-gather.8.cloned.1.call-done), kind=kOutput, calls=%fused_computation.24 | convolution fusion | flops 2954887168 | bytes 8519680 | tf_op jit(solution)/shard_map/dot_general | solution.py:558
  403.3 15.0 %collective-permute-done.22 = bf16[512,1024]{1,0:T(8,128)(2,1)} collective-permute-done((bf16[512,1024]{1,0:T(8,128)(2,1)}, bf16[512,1024]{1,0:T(8,128)(2,1)}, u32[]{:S(2)}, u32[]{:S(2)}) %collective-permute-start.22) | collective-permute-done | bytes 1048608 | tf_op jit(solution)/shard_map/ppermute | solution.py:499
  424.8 24.1 %collective-permute-done.24 = bf16[512,1024]{1,0:T(8,128)(2,1)S(1)} collective-permute-done((bf16[512,1024]{1,0:T(8,128)(2,1)S(1)}, bf16[512,1024]{1,0:T(8,128)(2,1)S(1)}, u32[]{:S(2)}, u32[]{:S(2)}) %collective-permute-start.24) | collective-permute-done | bytes 1048608 | tf_op jit(solution)/shard_map/ppermute | solution.py:499
  461.8 6.5 fusion.73.dgated_ref
  468.2 76.9 %mixer_backward.1 = (bf16[2048,1664]{1,0:T(8,128)(2,1)}, f32[32,1024]{1,0:T(8,128)}, f32[8,256]{1,0:T(8,128)}, f32[16,128]{1,0:T(8,128)}) custom-call(s32[3]{0:T(128)} %select_reduce_fusion.ends_ref, f32[2048,1664]{1,0:T(8,128)} %fusion.71.proj_ref.halo_ref, f32[2048,1664]{1,0:T(8,128)} %fusion.71.proj_ref.halo_ref, f32[4,1024]{1,0:T(4,128)} %bitcast.138, ...), custom_call_target="tpu_custom_call" | custom-call | tf_op jit(solution)/shard_map/mixer_backward/pallas_call | solution.py:439
  545.2 11.4 %convolution_convert_fusion.1 = bf16[1024,1664]{1,0:T(8,128)(2,1)S(1)} fusion(bf16[2048,1024]{1,0:T(8,128)(2,1)S(1)} %bitcast.154, bf16[2048,1664]{1,0:T(8,128)(2,1)} %get-tuple-element.50), kind=kOutput, calls=%fused_computation.23 | convolution fusion | flops 6981025792 | bytes 14417920 | tf_op jit(solution)/shard_map/dot_general | solution.py:558
  558.7 6.5 concatenate.48
  565.3 11.0 %convolution_convert_fusion.4 = bf16[2048,1024]{1,0:T(8,128)(2,1)S(1)} fusion(bf16[2048,1664]{1,0:T(8,128)(2,1)} %get-tuple-element.50, bf16[1024,1664]{1,0:T(8,128)(2,1)} %all-gather.4.cloned.1.call-done), kind=kOutput, calls=%fused_computation.26 | convolution fusion | flops 6981419008 | bytes 14417920 | tf_op jit(solution)/shard_map/dot_general | solution.py:558
  590.0 21.4 %collective-permute-done.31 = bf16[512,1024]{1,0:T(8,128)(2,1)S(1)} collective-permute-done((bf16[512,1024]{1,0:T(8,128)(2,1)S(1)}, bf16[512,1024]{1,0:T(8,128)(2,1)S(1)}, u32[]{:S(2)}, u32[]{:S(2)}) %collective-permute-start.31) | collective-permute-done | bytes 1048608 | tf_op jit(solution)/shard_map/ppermute | solution.py:499
  621.6 24.8 %collective-permute-done.28 = bf16[512,1024]{1,0:T(8,128)(2,1)S(1)} collective-permute-done((bf16[512,1024]{1,0:T(8,128)(2,1)S(1)}, bf16[512,1024]{1,0:T(8,128)(2,1)S(1)}, u32[]{:S(2)}, u32[]{:S(2)}) %collective-permute-start.28) | collective-permute-done | bytes 1048608 | tf_op jit(solution)/shard_map/ppermute | solution.py:499
  649.3 9.7 %all-to-all-done.3 = bf16[8,64,1024]{2,1,0:T(8,128)(2,1)} async-done(((bf16[8,64,1024]{2,1,0:T(8,128)(2,1)}), bf16[8,64,1024]{2,1,0:T(8,128)(2,1)}, u32[]{:S(2)}, u32[]{:S(2)}) %all-to-all-start.3) | async-done | bytes 1048608 | tf_op jit(solution)/shard_map/all_to_all | solution.py:599
  669.8 18.6 %collective-permute-done.37 = f32[8,384]{1,0:T(8,128)S(1)} collective-permute-done((f32[8,384]{1,0:T(8,128)S(1)}, f32[8,384]{1,0:T(8,128)S(1)}, u32[]{:S(2)}, u32[]{:S(2)}) %collective-permute-start.37) | collective-permute-done | bytes 12320 | tf_op jit(solution)/shard_map/ppermute | solution.py:499
  688.4 6.0 collective-permute-done.38
  699.9 7.0 collective-permute-done.33
  711.8 32.3 %reduce-scatter.4.cloned.1.call-done = bf16[128,1664]{1,0:T(8,128)(2,1)} async-done(((bf16[1024,1664]{1,0:T(8,128)(2,1)}), bf16[128,1664]{1,0:T(8,128)(2,1)}) %reduce-scatter.4.cloned.1.call-update) | async-done | bytes 426000 | tf_op jit(solution)/shard_map/reduce_scatter | solution.py:553
  744.1 6.3 collective-permute-start.32
  762.6 7.4 collective-permute-done.32
  (264 shorter events, 184.8 us)
Async XLA Ops:
  7.2 137.8 %all-gather.4.cloned.1.call-start = ((), (), s32[]{:S(2)}) async-start(), calls=%async_computation.7 | async-start | bytes 3833856 | tf_op jit(solution)/shard_map/all_gather | solution.py:548
  10.6 25.1 %collective-permute-start.8 = (bf16[128,1664]{1,0:T(8,128)(2,1)S(1)}, bf16[128,1664]{1,0:T(8,128)(2,1)S(1)}, u32[]{:S(2)}, u32[]{:S(2)}) collective-permute-start(bf16[128,1664]{1,0:T(8,128)(2,1)S(1)} %concatenate.40), channel_id=1, source_target_pairs={{0,0},{1,4},{2,8},{3,12},{4,1},{5,5},{6,9},{7,13},{8,2},{9,6},{10,... | collective-permute-start | bytes 1277960 | tf_op jit(solution)/shard_map/ppermute | solution.py:504
  36.4 174.2 %all-gather.6.cloned.1.call-start = ((), (), s32[]{:S(2)}) async-start(), calls=%async_computation.8 | async-start | bytes 1179648 | tf_op jit(solution)/shard_map/all_gather | solution.py:548
  80.8 25.8 %collective-permute-start.6 = (bf16[512,1024]{1,0:T(8,128)(2,1)S(1)}, bf16[512,1024]{1,0:T(8,128)(2,1)S(1)}, u32[]{:S(2)}, u32[]{:S(2)}) collective-permute-start(bf16[512,1024]{1,0:T(8,128)(2,1)S(1)} %fusion.14), channel_id=1, source_target_pairs={{0,8},{4,12},{8,0},{12,4},{1,9},{5,13},{9,1},{13,5},{2,10},{6,14},... | collective-permute-start | bytes 3145736 | tf_op jit(solution)/shard_map/ppermute | solution.py:499
  81.8 24.8 %collective-permute-start = (s32[512]{0:T(512)S(1)}, s32[512]{0:T(512)S(1)}, u32[]{:S(2)}, u32[]{:S(2)}) collective-permute-start(s32[512]{0:T(512)S(1)} %copy-done.28), channel_id=1, source_target_pairs={{0,0},{1,4},{2,8},{3,12},{4,1},{5,5},{6,9},{7,13},{8,2},{9,6},{10,... | collective-permute-start | bytes 6152 | tf_op jit(solution)/shard_map/ppermute | solution.py:504
  84.6 27.5 %collective-permute-start.4 = (s32[1,3]{1,0:T(1,128)S(1)}, s32[1,3]{1,0:T(1,128)S(1)}, u32[]{:S(2)}, u32[]{:S(2)}) collective-permute-start(s32[1,3]{1,0:T(1,128)S(1)} %copy-done.31), channel_id=1, source_target_pairs={{0,0},{1,4},{2,8},{3,12},{4,1},{5,5},{6,9},{7,13},{8,2},{9,6},{10,... | collective-permute-start | bytes 44 | tf_op jit(solution)/shard_map/ppermute | solution.py:504
  91.6 46.4 %collective-permute-start.5 = (bf16[512,1024]{1,0:T(8,128)(2,1)S(1)}, bf16[512,1024]{1,0:T(8,128)(2,1)}, u32[]{:S(2)}, u32[]{:S(2)}) collective-permute-start(bf16[512,1024]{1,0:T(8,128)(2,1)S(1)} %fusion.14), channel_id=1, source_target_pairs={{0,4},{4,0},{8,12},{12,8},{1,5},{5,1},{9,13},{13,9},{2,6},{6,2},{1... | collective-permute-start | bytes 3145736 | tf_op jit(solution)/shard_map/ppermute | solution.py:499
  106.6 31.4 %collective-permute-start.7 = (bf16[512,1024]{1,0:T(8,128)(2,1)S(1)}, bf16[512,1024]{1,0:T(8,128)(2,1)}, u32[]{:S(2)}, u32[]{:S(2)}) collective-permute-start(bf16[512,1024]{1,0:T(8,128)(2,1)S(1)} %collective-permute-done.6), channel_id=1, source_target_pairs={{0,4},{4,0},{8,12},{12,8},{1,5},{5,1},{9,13},{13,9},{2,6},{6,2},{1... | collective-permute-start | bytes 3145736 | tf_op jit(solution)/shard_map/ppermute | solution.py:499
  114.4 22.4 %collective-permute-start.9 = (bf16[128,512]{1,0:T(8,128)(2,1)S(1)}, bf16[128,512]{1,0:T(8,128)(2,1)S(1)}, u32[]{:S(2)}, u32[]{:S(2)}) collective-permute-start(bf16[128,512]{1,0:T(8,128)(2,1)S(1)} %bitcast.140), channel_id=1, source_target_pairs={{0,0},{1,4},{2,8},{3,12},{4,1},{5,5},{6,9},{7,13},{8,2},{9,6},{10,... | collective-permute-start | bytes 393224 | tf_op jit(solution)/shard_map/ppermute | solution.py:504
  116.6 102.3 %collective-permute-start.16 = (bf16[128,2112]{0,1:T(8,128)(2,1)}, bf16[128,2112]{0,1:T(8,128)(2,1)}, u32[]{:S(2)}, u32[]{:S(2)}) collective-permute-start(bf16[128,2112]{0,1:T(8,128)(2,1)} %pad_maximum_fusion.10), channel_id=1, source_target_pairs={{0,0},{1,4},{2,8},{3,12},{4,1},{5,5},{6,9},{7,13},{8,2},{9,6},{10,... | collective-permute-start | bytes 1622024 | tf_op jit(solution)/shard_map/ppermute | solution.py:504
  137.4 192.0 %all-gather.8.cloned.1.call-start = ((), (), s32[]{:S(2)}) async-start(), calls=%async_computation.9 | async-start | bytes 4866048 | tf_op jit(solution)/shard_map/all_gather | solution.py:548
  229.7 48.0 %collective-permute-start.12 = (f32[512,1024]{1,0:T(8,128)}, f32[512,1024]{1,0:T(8,128)}, u32[]{:S(2)}, u32[]{:S(2)}) collective-permute-start(f32[512,1024]{1,0:T(8,128)} %slice_add_fusion), channel_id=1, source_target_pairs={{0,8},{4,12},{8,0},{12,4},{1,9},{5,13},{9,1},{13,5},{2,10},{6,14},... | collective-permute-start | bytes 6291464 | tf_op jit(solution)/shard_map/ppermute | solution.py:499
  232.6 49.9 %all-to-all-start.1 = ((bf16[8,64,1024]{2,1,0:T(8,128)(2,1)}), bf16[8,64,1024]{2,1,0:T(8,128)(2,1)}, u32[]{:S(2)}, u32[]{:S(2)}) async-start(bf16[8,64,1024]{2,1,0:T(8,128)(2,1)} %bitcast.130), calls=%async_computation.1 | async-start | bytes 2097152 | tf_op jit(solution)/shard_map/all_to_all | solution.py:599
  236.9 459.1 %reduce-scatter.6.cloned.1.call-start = ((), (), s32[]{:S(2)}) async-start(), calls=%async_computation.11 | async-start | bytes 1179648 | tf_op jit(solution)/shard_map/reduce_scatter | solution.py:553
  282.2 26.4 %collective-permute-start.18 = (bf16[512,1024]{1,0:T(8,128)(2,1)}, bf16[512,1024]{1,0:T(8,128)(2,1)}, u32[]{:S(2)}, u32[]{:S(2)}) collective-permute-start(bf16[512,1024]{1,0:T(8,128)(2,1)} %multiply_convert_fusion.3), channel_id=1, source_target_pairs={{0,8},{4,12},{8,0},{12,4},{1,9},{5,13},{9,1},{13,5},{2,10},{6,14},... | collective-permute-start | bytes 3145736 | tf_op jit(solution)/shard_map/ppermute | solution.py:499
  282.5 46.9 %collective-permute-start.14 = (bf16[512,1024]{1,0:T(8,128)(2,1)}, bf16[512,1024]{1,0:T(8,128)(2,1)}, u32[]{:S(2)}, u32[]{:S(2)}) collective-permute-start(bf16[512,1024]{1,0:T(8,128)(2,1)} %bitcast.21), channel_id=1, source_target_pairs={{0,8},{4,12},{8,0},{12,4},{1,9},{5,13},{9,1},{13,5},{2,10},{6,14},... | collective-permute-start | bytes 3145736 | tf_op jit(solution)/shard_map/ppermute | solution.py:499
  284.3 45.1 %collective-permute-start.17 = (bf16[512,1024]{1,0:T(8,128)(2,1)}, bf16[512,1024]{1,0:T(8,128)(2,1)}, u32[]{:S(2)}, u32[]{:S(2)}) collective-permute-start(bf16[512,1024]{1,0:T(8,128)(2,1)} %multiply_convert_fusion.3), channel_id=1, source_target_pairs={{0,4},{4,0},{8,12},{12,8},{1,5},{5,1},{9,13},{13,9},{2,6},{6,2},{1... | collective-permute-start | bytes 3145736 | tf_op jit(solution)/shard_map/ppermute | solution.py:499
  308.7 20.8 %collective-permute-start.19 = (bf16[512,1024]{1,0:T(8,128)(2,1)}, bf16[512,1024]{1,0:T(8,128)(2,1)}, u32[]{:S(2)}, u32[]{:S(2)}) collective-permute-start(bf16[512,1024]{1,0:T(8,128)(2,1)} %collective-permute-done.18), channel_id=1, source_target_pairs={{0,4},{4,0},{8,12},{12,8},{1,5},{5,1},{9,13},{13,9},{2,6},{6,2},{1... | collective-permute-start | bytes 3145736 | tf_op jit(solution)/shard_map/ppermute | solution.py:499
  311.6 31.5 %collective-permute-start.13 = (bf16[512,1024]{1,0:T(8,128)(2,1)}, bf16[512,1024]{1,0:T(8,128)(2,1)}, u32[]{:S(2)}, u32[]{:S(2)}) collective-permute-start(bf16[512,1024]{1,0:T(8,128)(2,1)} %bitcast.21), channel_id=1, source_target_pairs={{0,4},{4,0},{8,12},{12,8},{1,5},{5,1},{9,13},{13,9},{2,6},{6,2},{1... | collective-permute-start | bytes 3145736 | tf_op jit(solution)/shard_map/ppermute | solution.py:499
  379.2 24.0 %collective-permute-start.20 = (bf16[512,1024]{1,0:T(8,128)(2,1)}, bf16[512,1024]{1,0:T(8,128)(2,1)S(1)}, u32[]{:S(2)}, u32[]{:S(2)}) collective-permute-start(bf16[512,1024]{1,0:T(8,128)(2,1)} %get-tuple-element.137), channel_id=1, source_target_pairs={{0,4},{4,0},{8,12},{12,8},{1,5},{5,1},{9,13},{13,9},{2,6},{6,2},{1... | collective-permute-start | bytes 3145736 | tf_op jit(solution)/shard_map/ppermute | solution.py:499
  392.4 25.9 %collective-permute-start.22 = (bf16[512,1024]{1,0:T(8,128)(2,1)}, bf16[512,1024]{1,0:T(8,128)(2,1)}, u32[]{:S(2)}, u32[]{:S(2)}) collective-permute-start(bf16[512,1024]{1,0:T(8,128)(2,1)} %add_convert_fusion.2), channel_id=1, source_target_pairs={{0,8},{4,12},{8,0},{12,4},{1,9},{5,13},{9,1},{13,5},{2,10},{6,14},... | collective-permute-start | bytes 3145736 | tf_op jit(solution)/shard_map/ppermute | solution.py:499
  424.2 24.8 %collective-permute-start.24 = (bf16[512,1024]{1,0:T(8,128)(2,1)S(1)}, bf16[512,1024]{1,0:T(8,128)(2,1)S(1)}, u32[]{:S(2)}, u32[]{:S(2)}) collective-permute-start(bf16[512,1024]{1,0:T(8,128)(2,1)S(1)} %get-tuple-element.39), channel_id=1, source_target_pairs={{0,8},{4,12},{8,0},{12,4},{1,9},{5,13},{9,1},{13,5},{2,10},{6,14},... | collective-permute-start | bytes 3145736 | tf_op jit(solution)/shard_map/ppermute | solution.py:499
  424.8 24.1 %collective-permute-start.23 = (bf16[512,1024]{1,0:T(8,128)(2,1)S(1)}, bf16[512,1024]{1,0:T(8,128)(2,1)S(1)}, u32[]{:S(2)}, u32[]{:S(2)}) collective-permute-start(bf16[512,1024]{1,0:T(8,128)(2,1)S(1)} %get-tuple-element.39), channel_id=1, source_target_pairs={{0,4},{4,0},{8,12},{12,8},{1,5},{5,1},{9,13},{13,9},{2,6},{6,2},{1... | collective-permute-start | bytes 3145736 | tf_op jit(solution)/shard_map/ppermute | solution.py:499
  460.6 247.3 %reduce-scatter.8.cloned.1.call-start = ((), (), s32[]{:S(2)}) async-start(), calls=%async_computation.12 | async-start | bytes 5013504 | tf_op jit(solution)/shard_map/reduce_scatter | solution.py:553
  461.1 283.0 %reduce-scatter.4.cloned.1.call-start = ((), (), s32[]{:S(2)}) async-start(), calls=%async_computation.10 | async-start | bytes 3833856 | tf_op jit(solution)/shard_map/reduce_scatter | solution.py:553
  586.1 25.4 %collective-permute-start.31 = (bf16[512,1024]{1,0:T(8,128)(2,1)S(1)}, bf16[512,1024]{1,0:T(8,128)(2,1)S(1)}, u32[]{:S(2)}, u32[]{:S(2)}) collective-permute-start(bf16[512,1024]{1,0:T(8,128)(2,1)S(1)} %fusion.22), channel_id=1, source_target_pairs={{0,8},{4,12},{8,0},{12,4},{1,9},{5,13},{9,1},{13,5},{2,10},{6,14},... | collective-permute-start | bytes 3145736 | tf_op jit(solution)/shard_map/ppermute | solution.py:499
  590.0 28.7 %collective-permute-start.27 = (bf16[512,1024]{1,0:T(8,128)(2,1)}, bf16[512,1024]{1,0:T(8,128)(2,1)}, u32[]{:S(2)}, u32[]{:S(2)}) collective-permute-start(bf16[512,1024]{1,0:T(8,128)(2,1)} %get-tuple-element.136), channel_id=1, source_target_pairs={{0,4},{4,0},{8,12},{12,8},{1,5},{5,1},{9,13},{13,9},{2,6},{6,2},{1... | collective-permute-start | bytes 3145736 | tf_op jit(solution)/shard_map/ppermute | solution.py:499
  614.4 44.6 %all-to-all-start.3 = ((bf16[8,64,1024]{2,1,0:T(8,128)(2,1)}), bf16[8,64,1024]{2,1,0:T(8,128)(2,1)}, u32[]{:S(2)}, u32[]{:S(2)}) async-start(bf16[8,64,1024]{2,1,0:T(8,128)(2,1)} %bitcast.116), calls=%async_computation.3 | async-start | bytes 2097152 | tf_op jit(solution)/shard_map/all_to_all | solution.py:599
  620.7 25.6 %collective-permute-start.28 = (bf16[512,1024]{1,0:T(8,128)(2,1)S(1)}, bf16[512,1024]{1,0:T(8,128)(2,1)S(1)}, u32[]{:S(2)}, u32[]{:S(2)}) collective-permute-start(bf16[512,1024]{1,0:T(8,128)(2,1)S(1)} %add_convert_fusion.1), channel_id=1, source_target_pairs={{0,8},{4,12},{8,0},{12,4},{1,9},{5,13},{9,1},{13,5},{2,10},{6,14},... | collective-permute-start | bytes 3145736 | tf_op jit(solution)/shard_map/ppermute | solution.py:499
  659.0 94.4 %all-to-all-start.2 = ((bf16[8,64,1024]{2,1,0:T(8,128)(2,1)}), bf16[8,64,1024]{2,1,0:T(8,128)(2,1)S(1)}, u32[]{:S(2)}, u32[]{:S(2)}) async-start(bf16[8,64,1024]{2,1,0:T(8,128)(2,1)} %bitcast.31), calls=%async_computation.2 | async-start | bytes 2097152 | tf_op jit(solution)/shard_map/all_to_all | solution.py:599
  709.9 51.0 %collective-permute-start.34 = (bf16[128,2112]{0,1:T(8,128)(2,1)}, bf16[128,2112]{0,1:T(8,128)(2,1)S(1)}, u32[]{:S(2)}, u32[]{:S(2)}) collective-permute-start(bf16[128,2112]{0,1:T(8,128)(2,1)} %copy.98), channel_id=1, source_target_pairs={{0,0},{1,4},{2,8},{3,12},{4,1},{5,5},{6,9},{7,13},{8,2},{9,6},{10,... | collective-permute-start | bytes 1622024 | tf_op jit(solution)/shard_map/ppermute | solution.py:504
  744.1 25.9 %collective-permute-start.32 = (bf16[128,1664]{1,0:T(8,128)(2,1)}, bf16[128,1664]{1,0:T(8,128)(2,1)S(1)}, u32[]{:S(2)}, u32[]{:S(2)}) collective-permute-start(bf16[128,1664]{1,0:T(8,128)(2,1)} %reduce-scatter.4.cloned.1.call-done), channel_id=1, source_target_pairs={{0,0},{1,4},{2,8},{3,12},{4,1},{5,5},{6,9},{7,13},{8,2},{9,6},{10,... | collective-permute-start | bytes 1277960 | tf_op jit(solution)/shard_map/ppermute | solution.py:504
  (52 other events, 1492.1 us)
Sparse Core Ops, SparseCore 0:
  36.5 77.5 all-gather.3
  137.6 38.5 all-gather.5
  219.0 93.1 all-gather.7
  460.7 61.8 reduce-scatter.5
  526.5 90.6 reduce-scatter.7
  620.7 123.4 reduce-scatter.3

commit v2 on v1

--- a/solution.py
+++ b/solution.py
@@ -101,21 +101,22 @@
 
 
 def forward_kernel(
-    ends_ref, proj_ref, taps_ref, rate_ref, shift_ref, gain_ref,
-    gated_ref, o_ref, u_ref, s_ref, t_ref, qe_ref, m_ref,
-    xs, state, *, heads, rows, taps,
+    ends_ref, proj_ref, before_ref, taps_ref, rate_ref, shift_ref, gain_ref, enter_ref,
+    gated_ref, o_ref, u_ref, s_ref, t_ref, qe_ref, m_ref, state,
+    xs, *, heads, rows, taps, start,
 ):
     i = pl.program_id(0)
     wide = 2 * DK + DV
     full = wide + DV
     ends = [ends_ref[k] for k in range(SEQS)]
-    base = i * rows
+    base = start + i * rows
     c = CHUNK
 
     @pl.when(i == 0)
     def _():
-        xs[0:8, :] = jnp.zeros((8, heads * wide), f32)
-        state[...] = jnp.zeros_like(state)
+        for h in range(heads):
+            xs[0:8, h * wide : (h + 1) * wide] = before_ref[:, h * full : h * full + wide]
+        state[...] = enter_ref[...]
 
     @pl.when(i > 0)
     def _():
@@ -190,23 +191,23 @@
 
 
 def backward_kernel(
-    ends_ref, proj_ref, halo_ref, taps_ref, rate_ref, shift_ref, gain_ref,
-    dgated_ref, o_ref, u_ref, s_ref, t_ref, qe_ref, m_ref,
-    dproj_ref, dtaps_ref, dgain_ref, ddecay_ref,
-    xs, ds, dstate, *, heads, rows, taps, blocks,
+    ends_ref, proj_ref, halo_ref, before_ref, taps_ref, rate_ref, shift_ref, gain_ref,
+    dgated_ref, o_ref, u_ref, s_ref, t_ref, qe_ref, m_ref, leave_ref, later_ref,
+    dproj_ref, dtaps_ref, dgain_ref, ddecay_ref, dstate, first_ref,
+    xs, ds, *, heads, rows, taps, blocks, start,
 ):
     step = pl.program_id(0)
     i = blocks - 1 - step
     wide = 2 * DK + DV
     full = wide + DV
     ends = [ends_ref[k] for k in range(SEQS)]
-    base = i * rows
+    base = start + i * rows
     c = CHUNK
 
     @pl.when(step == 0)
     def _():
-        ds[...] = jnp.zeros_like(ds)
-        dstate[...] = jnp.zeros_like(dstate)
+        ds[rows : rows + 8, :] = later_ref[...]
+        dstate[...] = leave_ref[...]
         dtaps_ref[...] = jnp.zeros_like(dtaps_ref)
         dgain_ref[...] = jnp.zeros_like(dgain_ref)
         ddecay_ref[...] = jnp.zeros_like(ddecay_ref)
@@ -216,7 +217,8 @@
         ds[rows : rows + 8, :] = ds[0:8, :]
 
     for h in range(heads):
-        xs[0:8, h * wide : (h + 1) * wide] = halo_ref[:, h * full : h * full + wide]
+        cols = slice(h * full, h * full + wide)
+        xs[0:8, h * wide : (h + 1) * wide] = jnp.where(i == 0, before_ref[:, cols], halo_ref[:, cols])
         xs[8:, h * wide : (h + 1) * wide] = proj_ref[:, h * full : h * full + wide]
     small = proj_ref[:, heads * full :]
     beta_all = sigmoid(small)
@@ -318,9 +320,9 @@
             strict_low, jnp.where(lane == 0, dtail, 0.0)
         )
         dld = jnp.sum(straddle, axis=-1, keepdims=True) + both[:, 0:1]
-        dq_all[h][b] = carry * x["f"] + DOT_B(dqk, k)
+        dq_all[h][b] = carry * x["f"] + DOT_G(dqk, k)
         dk_all[h][b] = (
-            x["tail"] * x["j"] - (carry * beta) * hh + DOT_B(dqk, q, 0, 0) + DOT_B(dkk, k) + DOT_B(dkk, k, 0, 0)
+            x["tail"] * x["j"] - (carry * beta) * hh + DOT_G(dqk, q, 0, 0) + DOT_G(dkk, k) + DOT_G(dkk, k, 0, 0)
         )
         dv_all[h][b] = beta * dr
         dsmall[b][h] = (dbeta, dld)
@@ -362,6 +364,7 @@
                 (own * (xs[8 - j : 8 - j + rows, sl] * masks[j - 1])).reshape(rows // 8, 8, wide), axis=0
             )
         dproj_ref[:, h * full : h * full + wide] = total.astype(bf16)
+    first_ref[...] = ds[0:8, :]
 
 
 DOT_QK = dot3
@@ -372,9 +375,10 @@
 DOT_S = dot3
 DOT_O = dot3
 DOT_B = dot3
-
-
-def mixer_forward(ends, proj, taps, rate, shift, gain, *, heads, rows):
+DOT_G = dot1
+
+
+def mixer_forward(ends, proj, before, before_at, taps, rate, shift, gain, enter, *, heads, rows, start):
     total, width = proj.shape
     blocks = total // rows
     n = rows // CHUNK
@@ -383,7 +387,8 @@
     quad = lambda i, e: (i, 0, 0, 0)
     wide = 2 * DK + DV
     chunks = total // CHUNK
-    kernel = functools.partial(forward_kernel, heads=heads, rows=rows, taps=taps.shape[0])
+    kernel = functools.partial(forward_kernel, heads=heads, rows=rows, taps=taps.shape[0], start=start)
+    wide_rows = pl.BlockSpec((rows, heads * DV), row)
     return pl.pallas_call(
         kernel,
         grid_spec=pltpu.PrefetchScalarGridSpec(
@@ -391,24 +396,24 @@
             grid=(blocks,),
             in_specs=[
                 pl.BlockSpec((rows, width), row),
+                pl.BlockSpec((8, width), lambda i, e: (before_at, 0)),
                 pl.BlockSpec(taps.shape, same),
                 pl.BlockSpec(rate.shape, same),
                 pl.BlockSpec(shift.shape, same),
                 pl.BlockSpec(gain.shape, same),
+                pl.BlockSpec(enter.shape, lambda i, e: (0, 0, 0)),
             ],
             out_specs=[
-                pl.BlockSpec((rows, heads * DV), row),
-                pl.BlockSpec((rows, heads * DV), row),
-                pl.BlockSpec((rows, heads * DV), row),
+                wide_rows,
+                wide_rows,
+                wide_rows,
                 pl.BlockSpec((n, heads, DK, DV), quad),
                 pl.BlockSpec((n, heads, CHUNK, CHUNK), quad),
                 pl.BlockSpec((n, heads, CHUNK, DK), quad),
                 pl.BlockSpec((n, heads, DK, DK), quad),
+                pl.BlockSpec(enter.shape, lambda i, e: (0, 0, 0)),
             ],
-            scratch_shapes=[
-                pltpu.VMEM((rows + 8, heads * wide), f32),
-                pltpu.VMEM((heads, DK, DV), f32),
-            ],
+            scratch_shapes=[pltpu.VMEM((rows + 8, heads * wide), f32)],
         ),
         out_shape=[
             jax.ShapeDtypeStruct((total, heads * DV), bf16),
@@ -418,15 +423,21 @@
             jax.ShapeDtypeStruct((chunks, heads, CHUNK, CHUNK), f32),
             jax.ShapeDtypeStruct((chunks, heads, CHUNK, DK), f32),
             jax.ShapeDtypeStruct((chunks, heads, DK, DK), f32),
+            jax.ShapeDtypeStruct(enter.shape, f32),
         ],
         compiler_params=pltpu.CompilerParams(
             dimension_semantics=("arbitrary",), vmem_limit_bytes=56 * 1024 * 1024
         ),
+        cost_estimate=pl.CostEstimate(
+            flops=total * heads * 6_000_000, bytes_accessed=total * heads * 9_000, transcendentals=total * heads * 2_000
+        ),
         name="mixer_forward",
-    )(ends, proj, taps, rate, shift, gain)
-
-
-def mixer_backward(ends, proj, taps, rate, shift, gain, dgated, saved, *, heads, rows):
+    )(ends, proj, before, taps, rate, shift, gain, enter)
+
+
+def mixer_backward(
+    ends, proj, before, before_at, taps, rate, shift, gain, dgated, saved, leave, later, *, heads, rows, start
+):
     total, width = proj.shape
     blocks = total // rows
     n = rows // CHUNK
@@ -435,7 +446,10 @@
     same = lambda s, e: (0, 0)
     quad = lambda s, e: (blocks - 1 - s, 0, 0, 0)
     wide = 2 * DK + DV
-    kernel = functools.partial(backward_kernel, heads=heads, rows=rows, taps=taps.shape[0], blocks=blocks)
+    kernel = functools.partial(
+        backward_kernel, heads=heads, rows=rows, taps=taps.shape[0], blocks=blocks, start=start
+    )
+    wide_rows = pl.BlockSpec((rows, heads * DV), row)
     return pl.pallas_call(
         kernel,
         grid_spec=pltpu.PrefetchScalarGridSpec(
@@ -444,44 +458,54 @@
             in_specs=[
                 pl.BlockSpec((rows, width), row),
                 pl.BlockSpec((8, width), halo),
+                pl.BlockSpec((8, width), lambda s, e: (before_at, 0)),
                 pl.BlockSpec(taps.shape, same),
                 pl.BlockSpec(rate.shape, same),
                 pl.BlockSpec(shift.shape, same),
                 pl.BlockSpec(gain.shape, same),
-                pl.BlockSpec((rows, heads * DV), row),
-                pl.BlockSpec((rows, heads * DV), row),
-                pl.BlockSpec((rows, heads * DV), row),
+                wide_rows,
+                wide_rows,
+                wide_rows,
                 pl.BlockSpec((n, heads, DK, DV), quad),
                 pl.BlockSpec((n, heads, CHUNK, CHUNK), quad),
                 pl.BlockSpec((n, heads, CHUNK, DK), quad),
                 pl.BlockSpec((n, heads, DK, DK), quad),
+                pl.BlockSpec(leave.shape, lambda s, e: (0, 0, 0)),
+                pl.BlockSpec(later.shape, same),
             ],
             out_specs=[
                 pl.BlockSpec((rows, width), row),
-                pl.BlockSpec((32, heads * wide), same),
+                pl.BlockSpec((8 * taps.shape[0], heads * wide), same),
                 pl.BlockSpec((8, DV), same),
                 pl.BlockSpec((16, 128), same),
+                pl.BlockSpec(leave.shape, lambda s, e: (0, 0, 0)),
+                pl.BlockSpec(later.shape, same),
             ],
             scratch_shapes=[
                 pltpu.VMEM((rows + 8, heads * wide), f32),
                 pltpu.VMEM((rows + 8, heads * wide), f32),
-                pltpu.VMEM((heads, DK, DV), f32),
             ],
         ),
         out_shape=[
             jax.ShapeDtypeStruct((total, width), bf16),
-            jax.ShapeDtypeStruct((32, heads * wide), f32),
+            jax.ShapeDtypeStruct((8 * taps.shape[0], heads * wide), f32),
             jax.ShapeDtypeStruct((8, DV), f32),
             jax.ShapeDtypeStruct((16, 128), f32),
+            jax.ShapeDtypeStruct(leave.shape, f32),
+            jax.ShapeDtypeStruct(later.shape, f32),
         ],
         compiler_params=pltpu.CompilerParams(
             dimension_semantics=("arbitrary",), vmem_limit_bytes=56 * 1024 * 1024
         ),
+        cost_estimate=pl.CostEstimate(
+            flops=total * heads * 1_000_000, bytes_accessed=total * heads * 9_000, transcendentals=total * heads * 2_000
+        ),
         name="mixer_backward",
-    )(ends, proj, proj, taps, rate, shift, gain, dgated, *saved)
+    )(ends, proj, proj, before, taps, rate, shift, gain, dgated, *saved, leave, later)
 
 
 BLOCK_ROWS = 256
+RUNS = 2
 
 
 def rms_scale(values):
@@ -508,25 +532,42 @@
     return [1 << k for k in range(size.bit_length() - 1)]
 
 
+def reversed_bits(n):
+    order = [0]
+    for bit in reversed(bits(n)):
+        order = order + [k ^ bit for k in order]
+    return order
+
+
+def gather_first(x):
+    return jnp.concatenate([x, swap(x, "lo", bits(lax.axis_size("lo"))[-1])], axis=0)
+
+
+def gather_last(x):
+    for bit in reversed(bits(lax.axis_size("lo"))[:-1]):
+        x = jnp.concatenate([x, swap(x, "lo", bit)], axis=0)
+    return x
+
+
 def gather_rows(x):
-    pieces = {0: x}
-    for bit in reversed(bits(lax.axis_size("lo"))):
-        pieces.update({k ^ bit: swap(p, "lo", bit) for k, p in list(pieces.items())})
-    return jnp.concatenate([pieces[k] for k in sorted(pieces)], axis=0)
-
-
-def scatter_sum(x):
-    n = lax.axis_size("lo")
-    rows = x.shape[0] // n
-    held = {k: x[k * rows : (k + 1) * rows] for k in range(n)}
-    for bit in bits(n):
-        sent = [k for k in held if k & bit]
-        sums = {}
-        for k in sent:
-            got = swap(held[k].astype(x.dtype), "lo", bit)
-            sums[k ^ bit] = held[k ^ bit].astype(f32) + got.astype(f32)
-        held = sums
-    return held[0]
+    return gather_last(gather_first(x))
+
+
+def halve(x, bit, kind):
+    half = x.shape[0] // 2
+    return x[:half].astype(f32) + swap(x[half:].astype(kind), "lo", bit).astype(f32)
+
+
+def scatter_first(x):
+    kind = x.dtype
+    for bit in bits(lax.axis_size("lo"))[:-1]:
+        x = halve(x, bit, kind)
+    half = x.shape[0] // 2
+    return x[:half], x[half:].astype(kind)
+
+
+def scatter_last(kept, sent):
+    return kept + swap(sent, "lo", bits(lax.axis_size("lo"))[-1]).astype(f32)
 
 
 def sum_everywhere(x):
@@ -545,7 +586,7 @@
 
 
 def widen(columns):
-    return lax.all_gather(exchange_roles(columns), ("hi", "tensor"), axis=0, tiled=True)
+    return lax.all_gather(columns, ("hi", "tensor"), axis=0, tiled=True)
 
 
 def narrow(columns):
@@ -591,134 +632,225 @@
     spread = ("hi", "tensor")
     width = lax.axis_size("hi")
     span = jnp.arange(local_rows, dtype=jnp.int32)
+    part_rows = width * per_peer
 
     send_rank = rank_of(token_return // group_rows * local_rows + token_return % local_rows)
     send_hot = (span[:, None] == send_rank[None, :]).astype(bf16)
 
     def across(rows):
-        moved = lax.all_to_all(
-            rows.reshape(groups, per_peer, model_width), spread, split_axis=0, concat_axis=0, tiled=True
-        )
-        return moved.reshape(local_rows, model_width)
+        return lax.all_to_all(rows, spread, split_axis=0, concat_axis=0, tiled=True)
 
     def pack(rows):
-        return across(product(send_hot, rows, dtype=bf16))
-
-    def unpack(rows):
-        return product(send_hot, across(rows), 0, 0, bf16)
-
+        return across(product(send_hot, rows, dtype=bf16).reshape(groups, per_peer, model_width))
+
+    def by_part(rows):
+        rows = jnp.transpose(rows.reshape(width, splits, per_peer, model_width), (1, 0, 2, 3))
+        return rows.reshape(local_rows, model_width)
+
+    def send_back(rows):
+        rows = jnp.transpose(rows.reshape(splits, width, per_peer, model_width), (1, 0, 2, 3))
+        return across(rows.reshape(groups, per_peer, model_width))
+
+    def unpack(got):
+        return product(send_hot, got.reshape(local_rows, model_width), 0, 0, bf16)
+
+    pieces = jnp.array(reversed_bits(splits), jnp.int32)
     orders = gather_rows(exchange_roles(token_order)).reshape(splits, local_rows)
-    orders = jnp.take(orders, jnp.arange(splits, dtype=jnp.int32) ^ me, axis=0)
+    parts = jnp.arange(splits, dtype=jnp.int32)
+    stand = jnp.sum(jnp.where(pieces[None, :] == (parts ^ me)[:, None], parts[None, :], 0), axis=1)
+    orders = jnp.sum(jnp.where((stand[:, None] == parts[None, :])[:, :, None], orders[None], 0), axis=1)
     given = orders // group_rows
     place_of = rank_of(given * local_rows + span[None, :]) % per_peer
-    held_at = (((given % splits) ^ me) * width + given // splits) * per_peer + place_of
+    piece_of = jnp.sum(jnp.where((given % splits)[..., None] == parts, stand, 0), axis=-1)
+    held_at = (piece_of * width + given // splits) * per_peer + place_of
     order_hot = (held_at[:, :, None] == span[None, None, :]).astype(bf16)
-
-    def to_sequence(rows):
-        parts = rows.reshape(splits * width, splits, per_peer, -1)
-        parts = jnp.transpose(parts, (1, 0, 2, 3)).reshape(splits, local_rows, -1)
+    run_parts = splits // RUNS
+    run_rows = run_parts * local_rows
+
+    def order_of(run):
+        return order_hot[run * run_parts : (run + 1) * run_parts]
+
+    def to_sequence(run, rows):
+        rows = rows.reshape(splits, run_parts, part_rows, -1)
+        rows = jnp.transpose(rows, (1, 0, 2, 3)).reshape(run_parts, local_rows, -1)
         return lax.dot_general(
-            order_hot, parts, (((2,), (1,)), ((0,), (0,))), preferred_element_type=f32
-        ).astype(bf16).reshape(group_rows, -1)
-
-    def from_sequence(rows):
-        parts = lax.dot_general(
-            order_hot, rows.reshape(splits, local_rows, -1), (((1,), (1,)), ((0,), (0,))), preferred_element_type=f32
-        ).astype(bf16).reshape(splits, splits * width, per_peer, -1)
-        return jnp.transpose(parts, (1, 0, 2, 3)).reshape(group_rows, -1)
+            order_of(run), rows, (((2,), (1,)), ((0,), (0,))), preferred_element_type=f32
+        ).astype(bf16).reshape(run_rows, -1)
+
+    def from_sequence(run, rows):
+        rows = lax.dot_general(
+            order_of(run), rows.reshape(run_parts, local_rows, -1), (((1,), (1,)), ((0,), (0,))),
+            preferred_element_type=f32,
+        ).astype(bf16).reshape(run_parts, splits, part_rows, -1)
+        return jnp.transpose(rows, (1, 0, 2, 3)).reshape(run_rows, -1)
 
     own_lengths = exchange_roles(lengths)
     ends = jnp.sum(jnp.where(jnp.tri(SEQS, dtype=bool), own_lengths, 0), axis=1).astype(jnp.int32)
+    small_at = proj_width
+    conv_at = small_at + heads * w_ba.shape[2]
     spare = 128 - heads * w_ba.shape[2] - taps
     mix_all = widen(
-        jnp.concatenate(
+        exchange_roles(jnp.concatenate(
             [
                 w_mix.reshape(weight_rows, proj_width).astype(bf16),
                 w_ba.reshape(weight_rows, -1).astype(bf16),
                 conv_w.reshape(weight_rows, taps).astype(bf16),
                 jnp.zeros((weight_rows, spare), bf16),
+                w_out.reshape(weight_rows, heads * DV).astype(bf16),
             ],
             axis=1,
-        )
-    )
-    packed_in = pack(tokens)
-    out_all = widen(after(w_out.reshape(weight_rows, heads * DV).astype(bf16), packed_in))
-    ffn_all = widen(
-        after(
-            jnp.concatenate(
-                [w_gate_up.reshape(weight_rows, 2 * units).astype(bf16), w_down.astype(bf16)], axis=1
-            ),
-            packed_in,
-        )
-    )
+        ))
+    )
+    packed_in = by_part(pack(tokens))
+    runs = range(RUNS)
+    own_rows = local_rows // RUNS
+
+    def split(rows):
+        return [rows[r * own_rows : (r + 1) * own_rows] for r in runs]
 
     input_f32 = packed_in.astype(f32)
     input_scale = rms_scale(input_f32)
-    gathered = gather_rows((input_f32 * input_scale * gain_attn).astype(bf16))
-    packed_grad = pack(after(cotangent, gathered))
-    normed_seq = to_sequence(gathered)
-
-    small_at = proj_width
-    conv_at = small_at + heads * w_ba.shape[2]
+    input_runs = split(input_f32)
+    gathered = [gather_rows(x) for x in split((input_f32 * input_scale * gain_attn).astype(bf16))]
+    cotangent, w_down, w_gate_up = after((cotangent, w_down, w_gate_up), *gathered)
+    packed_grad = pack(cotangent)
+    ffn_own = exchange_roles(
+        jnp.concatenate([w_gate_up.reshape(weight_rows, 2 * units).astype(bf16), w_down.astype(bf16)], axis=1)
+    )
+    ffn_all = widen(ffn_own)
+    w_pair, w_last = ffn_all[:, : 2 * units], ffn_all[:, 2 * units :]
+    out_all = mix_all[:, small_at + 128 :]
+    mix_all = mix_all[:, : small_at + 128]
+
     conv_all = mix_all[:, conv_at : conv_at + taps].reshape(-1, heads, taps).astype(f32)
     tap_rows = jnp.transpose(conv_all, (2, 1, 0)).reshape(taps, heads * conv_width)
-    projected = product(normed_seq, mix_all)
     head_start = me * heads
     lanes = jnp.zeros((1, 128), f32)
     rate_row = lanes.at[0, 1 : 2 * heads : 2].set(lax.dynamic_slice_in_dim(decay_log, head_start, heads))
     shift_row = lanes.at[0, 1 : 2 * heads : 2].set(lax.dynamic_slice_in_dim(decay_bias, head_start, heads))
     gain_row = gain_out[None]
-    saved = mixer_forward(
-        ends, projected, tap_rows, rate_row, shift_row, gain_row, heads=heads, rows=BLOCK_ROWS
-    )
-    grad_all = gather_rows(packed_grad)
-    gated = saved[0]
-    middle = input_f32 + scatter_sum(product(from_sequence(gated), out_all, 1, 1))
-    mid_scale = rms_scale(middle)
-    normed_mid_all = gather_rows((middle * mid_scale * gain_ffn).astype(bf16))
-
-    in_sequence = jnp.arange(group_rows, dtype=jnp.int32).reshape(splits, local_rows, 1) < ends[SEQS - 1]
-    live = from_sequence(jnp.broadcast_to(in_sequence, (splits, local_rows, 128)).astype(bf16))[:, :1].astype(f32)
-    w_pair = ffn_all[:, : 2 * units]
-    w_last = ffn_all[:, 2 * units :]
-    grad_hidden = product(grad_all, w_last) * live
-    gate_up = product(normed_mid_all, w_pair)
-    gate, up = gate_up[:, :units], gate_up[:, units:]
-    s = sigmoid(gate)
-    hidden = (gate * s * up * live).astype(bf16)
-    grad_pair = jnp.concatenate(
-        [grad_hidden * up * (s * (1.0 + gate * (1.0 - s))), grad_hidden * (gate * s)], axis=1
-    ).astype(bf16)
-    grad_norm_terms = product(grad_pair, w_pair, 1, 1, bf16)
-    grad_norm_mid = scatter_sum(grad_norm_terms)
-    hidden, grad_pair = after((hidden, grad_pair), grad_norm_terms)
-    grad_ffn = jnp.concatenate(
-        [product(normed_mid_all, grad_pair, 0, 0, bf16), product(grad_all, hidden, 0, 0, bf16)], axis=1
-    )
-    layer_terms = product(hidden, w_last, 1, 1, bf16)
-    grad_mid_norm, grad_gain_ffn = norm_back(middle, mid_scale, gain_ffn, grad_norm_mid)
-    grad_middle = packed_grad.astype(f32) + grad_mid_norm
-    grad_middle_all = gather_rows(after(grad_middle.astype(bf16), grad_ffn, layer_terms))
-    grad_ffn = narrow(grad_ffn)
-
-    grad_middle_seq = to_sequence(grad_middle_all)
-    grad_gated = product(grad_middle_seq, out_all)
-    grad_out_w = product(grad_middle_seq, gated, 0, 0, bf16)
-    grad_gated, layer_terms = after((grad_gated, layer_terms), grad_out_w)
-    grad_out_w = narrow(grad_out_w)
-    layer_out = unpack((middle + scatter_sum(layer_terms)).astype(bf16))
-    grad_proj, grad_taps, grad_gain_out, grad_decay = mixer_backward(
-        ends, projected, tap_rows, rate_row, shift_row, gain_row, grad_gated, saved[1:],
-        heads=heads, rows=BLOCK_ROWS,
-    )
+    constants = (tap_rows, rate_row, shift_row, gain_row)
+
+    state = jnp.zeros((heads, DK, DV), f32)
+
+    def ahead(r):
+        return (projected[r - 1], run_rows // 8 - 1) if r else (projected[r], 0)
+
+    def mix_forward(r, state):
+        return mixer_forward(
+            ends, projected[r], *ahead(r), *constants, state, heads=heads, rows=BLOCK_ROWS, start=r * run_rows
+        )
+
+    def feed_forward(r, normed_mid):
+        place = (r * run_parts + jnp.arange(run_parts, dtype=jnp.int32))[:, None, None] * local_rows
+        alive = (place + span[None, :, None] < ends[SEQS - 1]).astype(bf16)
+        live = from_sequence(r, jnp.broadcast_to(alive, (run_parts, local_rows, 128)))[:, :1].astype(f32)
+        grad_hidden = product(grad_all[r], w_last) * live
+        gate_up = product(normed_mid, w_pair)
+        gate, up = gate_up[:, :units], gate_up[:, units:]
+        s = sigmoid(gate)
+        hidden = (gate * s * up * live).astype(bf16)
+        grad_pair = jnp.concatenate(
+            [grad_hidden * up * (s * (1.0 + gate * (1.0 - s))), grad_hidden * (gate * s)], axis=1
+        ).astype(bf16)
+        return hidden, grad_pair, product(grad_pair, w_pair, 1, 1, bf16)
+
+    def normed_of(middle):
+        scale = rms_scale(middle)
+        return scale, (middle * scale * gain_ffn).astype(bf16)
+
+    constants = (tap_rows, rate_row, shift_row, gain_row)
+    seq_0 = to_sequence(0, gathered[0])
+    projected = [after(product(seq_0, mix_all), ffn_own)]
+    *saved_0, state = mix_forward(0, state)
+    terms_0 = product(from_sequence(0, saved_0[0]), out_all, 1, 1)
+    seq_1 = to_sequence(1, after(gathered[1], terms_0))
+    projected.append(product(seq_1, mix_all))
+    grad_runs = split(by_part(after(packed_grad, terms_0)))
+    kept_0, sent_0 = scatter_first(terms_0)
+    grad_first = [gather_first(x) for x in grad_runs]
+    projected[1], kept_0, sent_0, grad_first = lax.optimization_barrier((projected[1], kept_0, sent_0, grad_first))
+    grad_all = [gather_last(x) for x in grad_first]
+    *saved_1, state = mix_forward(1, state)
+    middle_0 = input_runs[0] + after(scatter_last(kept_0, sent_0), saved_1[0])
+    scale_0, normed_mid_0 = normed_of(middle_0)
+    terms_1 = product(from_sequence(1, saved_1[0]), out_all, 1, 1)
+    first_0 = gather_first(normed_mid_0)
+    kept_1, sent_1 = scatter_first(terms_1)
+    kept_1, sent_1, first_0 = lax.optimization_barrier((kept_1, sent_1, first_0))
+    normed_mid_0 = gather_last(first_0)
+
+    hidden_0, pair_0, grad_terms_0 = feed_forward(0, normed_mid_0)
+    middle_1 = input_runs[1] + after(scatter_last(kept_1, sent_1), grad_terms_0)
+    scale_1, normed_mid_1 = normed_of(middle_1)
+    first_1 = gather_first(normed_mid_1)
+    grad_kept_0, grad_sent_0 = scatter_first(grad_terms_0)
+    grad_kept_0, grad_sent_0, first_1 = lax.optimization_barrier((grad_kept_0, grad_sent_0, first_1))
+    normed_mid_1 = gather_last(first_1)
+    hidden_1, pair_1, grad_terms_1 = feed_forward(1, normed_mid_1)
+    grad_kept_1, grad_sent_1 = scatter_first(grad_terms_1)
+    grad_kept_1, grad_sent_1, grad_terms_0_sum = lax.optimization_barrier(
+        (grad_kept_1, grad_sent_1, scatter_last(grad_kept_0, grad_sent_0))
+    )
+    hidden_0, pair_0, hidden_1, pair_1 = after((hidden_0, pair_0, hidden_1, pair_1), grad_sent_1)
+    grad_pairs = product(normed_mid_0, pair_0, 0, 0) + product(normed_mid_1, pair_1, 0, 0)
+    grad_terms_1_sum = after(scatter_last(grad_kept_1, grad_sent_1), grad_pairs)
+    back_1, gain_1 = norm_back(middle_1, scale_1, gain_ffn, grad_terms_1_sum)
+    grad_middle_1 = grad_runs[1].astype(f32) + back_1
+    first_1 = gather_first(grad_middle_1.astype(bf16))
+    hidden_0, hidden_1 = after((hidden_0, hidden_1), grad_middle_1)
+    grad_last = product(grad_all[0], hidden_0, 0, 0) + product(grad_all[1], hidden_1, 0, 0)
+    layer_terms = [product(h, w_last, 1, 1, bf16) for h in (hidden_0, hidden_1)]
+    back_0, gain_0 = norm_back(middle_0, scale_0, gain_ffn, after(grad_terms_0_sum, grad_middle_1))
+    grad_gain_ffn = gain_0 + gain_1
+    grad_middle_0 = grad_runs[0].astype(f32) + back_0
+    first_1, grad_last, layer_terms, grad_low_0 = lax.optimization_barrier(
+        (first_1, grad_last, layer_terms, grad_middle_0.astype(bf16))
+    )
+    grad_mid_seq_1 = to_sequence(1, gather_last(first_1))
+    grad_ffn = narrow(jnp.concatenate([grad_pairs.astype(bf16), grad_last.astype(bf16)], axis=1))
+
+    def mix_backward(r, grad_gated, saved, leave, later):
+        return mixer_backward(
+            ends, projected[r], *ahead(r), *constants, grad_gated, saved[1:], leave, later,
+            heads=heads, rows=BLOCK_ROWS, start=r * run_rows,
+        )
+
+    leave = jnp.zeros((heads, DK, DV), f32)
+    later = jnp.zeros((8, heads * conv_width), f32)
+    first_0 = gather_first(grad_low_0)
+    layer_parts = [scatter_first(x) for x in layer_terms]
+    grad_gated_1 = product(grad_mid_seq_1, out_all)
+    grad_proj_1, *sums_1, leave, later = mix_backward(
+        1, after(grad_gated_1, grad_low_0, layer_parts), saved_1, leave, later
+    )
+    grad_mid_seq_0 = to_sequence(0, gather_last(after(first_0, grad_proj_1)))
+    grad_gated_0 = product(grad_mid_seq_0, out_all)
+    grad_out_w = product(grad_mid_seq_0, saved_0[0], 0, 0) + product(grad_mid_seq_1, saved_1[0], 0, 0)
+    normed_kept_1, normed_sent_1 = scatter_first(from_sequence(1, product(grad_proj_1, mix_all, 1, 1, bf16)))
+    layer_sums = [scatter_last(*x) for x in layer_parts]
+    layer_rows = [(m + x).astype(bf16) for m, x in zip((middle_0, middle_1), layer_sums)]
+    grad_out_w = grad_out_w.astype(bf16)
+    grad_gated_0, normed_kept_1, normed_sent_1, layer_rows, grad_out_w, grad_ffn = lax.optimization_barrier(
+        (grad_gated_0, normed_kept_1, normed_sent_1, layer_rows, grad_out_w, grad_ffn)
+    )
+    layer_back = send_back(jnp.concatenate(layer_rows, axis=0))
+    grad_proj_0, *sums_0, leave, later = mix_backward(0, grad_gated_0, saved_0, leave, later)
+    grad_proj_0, layer_back = lax.optimization_barrier((grad_proj_0, layer_back))
+    grad_taps, grad_gain_out, grad_decay = [a + b for a, b in zip(sums_0, sums_1)]
     grad_conv = jnp.sum(grad_taps.reshape(taps, 8, heads, conv_width), axis=1)
-    grad_conv = jnp.transpose(grad_conv, (2, 1, 0)).reshape(-1, taps).astype(bf16)
-    grad_mix = product(normed_seq, grad_proj, 0, 0, bf16)
-    grad_mix = jnp.concatenate([grad_mix[:, :conv_at], grad_conv, grad_mix[:, conv_at + taps :]], axis=1)
-    grad_normed = scatter_sum(from_sequence(product(after(grad_proj, grad_mix), mix_all, 1, 1, bf16)))
+    grad_conv = jnp.transpose(grad_conv, (2, 1, 0)).reshape(-1, taps)
+    grad_mix = product(seq_0, grad_proj_0, 0, 0) + product(seq_1, grad_proj_1, 0, 0)
+    grad_mix = (grad_mix + jnp.pad(grad_conv, ((0, 0), (conv_at, spare)))).astype(bf16)
+    grad_mix = jnp.concatenate([grad_mix, grad_out_w], axis=1)
+    normed_terms_0 = from_sequence(0, product(after(grad_proj_0, grad_mix), mix_all, 1, 1, bf16))
     grad_mix = narrow(grad_mix)
+    normed_sum_1 = scatter_last(normed_kept_1, normed_sent_1)
+    grad_normed = jnp.concatenate([scatter_last(*scatter_first(normed_terms_0)), normed_sum_1], axis=0)
     grad_input_norm, grad_gain_attn = norm_back(input_f32, input_scale, gain_attn, grad_normed)
-    input_grad = unpack((grad_middle + grad_input_norm).astype(bf16))
+    grad_middle = jnp.concatenate([grad_middle_0, grad_middle_1], axis=0)
+    input_grad = unpack(send_back((grad_middle + grad_input_norm).astype(bf16)))
+    layer_out = unpack(layer_back)
 
     head_total = decay_log.shape[0]
     decay_sums = jnp.sum(grad_decay.reshape(2, 8, 128), axis=1)[:, 1 : 2 * heads : 2]
@@ -738,7 +870,7 @@
         grad_mix[:, :small_at].reshape(w_mix.shape),
         grad_mix[:, small_at:conv_at].reshape(w_ba.shape),
         grad_mix[:, conv_at : conv_at + taps].reshape(conv_w.shape),
-        grad_out_w.reshape(w_out.shape),
+        grad_mix[:, small_at + 128 :].reshape(w_out.shape),
         grad_ffn[:, : 2 * units].reshape(w_gate_up.shape),
         grad_ffn[:, 2 * units :],
         *sums,

time: 785 us -> 728 us (0.927)
  waiting for transfers between devices: 318 us -> 270 us
  blocking collectives: 41.4 us -> 0 us
  starting transfers between devices: 58.4 us -> 69.7 us
  matrix products: 128 us -> 138 us
    ppermute x32 -> x39, waiting for transfers between devices: 220 us -> 124 us  [swap(): return lax.ppermute(x, axis, [(i, i ^ bit) for i in range(size)])]
    all_to_all x1 -> x0, blocking collectives: 41.4 us -> none  [across(): lax.all_to_all(rows.reshape(groups, per_peer, model_width), spread, split...]
    ppermute x8 -> x6, waiting for transfers between devices: 55.4 us -> 82.4 us  [exchange_roles(): lax.ppermute(x, ('lo', 'tensor'), [(a * n + b, b * n + a) for a in range(...]
    all_to_all x3 -> x4, waiting for transfers between devices: 9.67 us -> 34.3 us  [across(): return lax.all_to_all(rows, spread, split_axis=0, concat_axis=0, tiled=True)]
    ppermute x32 -> x39, starting transfers between devices: 15.8 us -> 28.1 us  [swap(): return lax.ppermute(x, axis, [(i, i ^ bit) for i in range(size)])]
    concatenate x5 -> x21, other arithmetic: 7.73 us -> 18.6 us  [the longest x9 6.53 us: gather_first(): jnp.concatenate([x, swap(x, 'lo', bits(lax.axis_size('lo'))[-1])], axis=0)]
    dot_general x5 -> x10, matrix products: 13.5 us -> 21.7 us  [the longest x6 12.7 us: from_sequence(): lax.dot_general(order_of(run), rows.reshape(run_parts, local_rows, -1), (...]
    ppermute x8 -> x6, starting transfers between devices: 29.8 us -> 22.7 us  [exchange_roles(): lax.ppermute(x, ('lo', 'tensor'), [(a * n + b, b * n + a) for a in range(...]
  transfers between devices with their start and end apart: 49 -> 53, of which waited for: 25 -> 23; matrix products, arithmetic and copies ran while one was open for 20% -> 28% of each run, Pallas kernels for 16% -> 18%
where the time goes in v2:
time: 728 us; the launch traced here: 718 us
  waiting for transfers between devices  270 us (37%)
  matrix products  138 us (19%)
  Pallas kernels  126 us (17%)
  starting transfers between devices  69.7 us (10%)
  other arithmetic  51.2 us (7%)
  local copies, waits for them, and re-layouts  48.5 us (7%)
  between operations  15.6 us (2%)
    ppermute x39, waiting for transfers between devices, swap(): return lax.ppermute(x, axis, [(i, i ^ bit) for i in range(size)])  124 us
    dot_general x28, matrix products, product(): lax.dot_general(a, b, (((ca,), (cb,)), ((), ())), preferred_element_type=...  116 us
    ppermute x6, waiting for transfers between devices, exchange_roles(): lax.ppermute(x, ('lo', 'tensor'), [(a * n + b, b * n + a) for a in range(...  82.4 us
    pallas_call x2, Pallas kernels, mixer_backward(): pl.pallas_call(kernel, grid_spec=pltpu.PrefetchScalarGridSpec(num_scalar_...  73.8 us
    pallas_call x2, Pallas kernels, mixer_forward(): pl.pallas_call(kernel, grid_spec=pltpu.PrefetchScalarGridSpec(num_scalar_...  52.2 us
    all_to_all x4, waiting for transfers between devices, across(): return lax.all_to_all(rows, spread, split_axis=0, concat_axis=0, tiled=True)  34.3 us
    reduce_scatter x2, waiting for transfers between devices, narrow(): lax.psum_scatter(columns.astype(bf16), ('hi', 'tensor'), scatter_dimensio...  28.7 us
    ppermute x39, starting transfers between devices, swap(): return lax.ppermute(x, axis, [(i, i ^ bit) for i in range(size)])  28.1 us
  transfers between devices with their start and end apart: 53, of which 23 were waited for; matrix products, arithmetic and copies ran while one was open for 28% of the time, Pallas kernels for 18%

profile of v2, /device:TPU:2, one launch (start us, length us, event | category | flops | bytes accessed | tf_op | source)
XLA Modules:
  0.0 718.5 jit_solution(15796719794887137905)
XLA Ops:
  15.4 26.2 %collective-permute-done.6 = bf16[128,2176]{1,0:T(8,128)(2,1)S(1)} collective-permute-done((bf16[128,2176]{1,0:T(8,128)(2,1)S(1)}, bf16[128,2176]{1,0:T(8,128)(2,1)S(1)}, u32[]{:S(2)}, u32[]{:S(2)}) %collective-permute-start.6) | collective-permute-done | bytes 557088 | tf_op jit(solution)/shard_map/ppermute | solution.py:528
  55.9 34.3 %all-to-all-done = bf16[8,64,1024]{2,1,0:T(8,128)(2,1)S(1)} async-done(((bf16[8,64,1024]{2,1,0:T(8,128)(2,1)}), bf16[8,64,1024]{2,1,0:T(8,128)(2,1)S(1)}, u32[]{:S(2)}, u32[]{:S(2)}) %all-to-all-start) | async-done | bytes 1048608 | tf_op jit(solution)/shard_map/all_to_all | solution.py:641
  101.0 20.3 %collective-permute-done.2 = s32[512]{0:T(512)S(1)} collective-permute-done((s32[512]{0:T(512)S(1)}, s32[512]{0:T(512)S(1)}, u32[]{:S(2)}, u32[]{:S(2)}) %collective-permute-start.2) | collective-permute-done | bytes 2080 | tf_op jit(solution)/shard_map/ppermute | solution.py:523
  138.2 5.5 all-to-all-start.1
  148.1 9.4 %fusion.18.proj_ref.before_ref.halo_ref = f32[1024,1664]{1,0:T(8,128)} fusion(bf16[1024,1024]{1,0:T(8,128)(2,1)} %bitcast.263, bf16[1024,2176]{1,0:T(8,128)(2,1)} %all-gather.3.cloned.1.call-done), kind=kOutput, calls=%fused_computation.36 | convolution fusion | flops 3489660928 | bytes 12320768 | tf_op jit(solution)/shard_map/dot_general | solution.py:599
  157.5 15.3 %collective-permute-done.9 = bf16[128,2112]{0,1:T(8,128)(2,1)} collective-permute-done((bf16[128,2112]{0,1:T(8,128)(2,1)}, bf16[128,2112]{0,1:T(8,128)(2,1)}, u32[]{:S(2)}, u32[]{:S(2)}) %collective-permute-start.9) | collective-permute-done | bytes 540704 | tf_op jit(solution)/shard_map/ppermute | solution.py:528
  177.2 26.1 %mixer_forward.2 = (bf16[1024,512]{1,0:T(8,128)(2,1)}, f32[1024,512]{1,0:T(8,128)}, f32[1024,512]{1,0:T(8,128)}, f32[8,2,128,256]{3,2,1,0:T(8,128)}, f32[8,2,128...) custom-call(s32[3]{0:T(128)} %select_reduce_fusion.3.ends_ref, ...), custom_call_target="tpu_custom_call" | custom-call | flops 12288000000 | bytes 18432000 | tf_op jit(solution)/shard_map/mixer_forward/pallas_call | solution.py:392
  218.4 6.1 fusion.16.proj_ref.halo_ref
  224.5 5.1 collective-permute-done.11
  229.7 10.8 %collective-permute-done.12 = bf16[256,1024]{1,0:T(8,128)(2,1)S(1)} collective-permute-done((bf16[256,1024]{1,0:T(8,128)(2,1)S(1)}, bf16[256,1024]{1,0:T(8,128)(2,1)S(1)}, u32[]{:S(2)}, u32[]{:S(2)}) %collective-permute-start.12) | collective-permute-done | bytes 524320 | tf_op jit(solution)/shard_map/ppermute | solution.py:523
  244.9 26.1 %mixer_forward.3 = (bf16[1024,512]{1,0:T(8,128)(2,1)}, f32[1024,512]{1,0:T(8,128)}, f32[1024,512]{1,0:T(8,128)}, f32[8,2,128,256]{3,2,1,0:T(8,128)}, f32[8,2,128...) custom-call(s32[3]{0:T(128)} %select_reduce_fusion.3.ends_ref, ...), custom_call_target="tpu_custom_call" | custom-call | flops 12288000000 | bytes 18432000 | tf_op jit(solution)/shard_map/mixer_forward/pallas_call | solution.py:392
  279.9 12.4 %collective-permute-done.15 = bf16[256,1024]{1,0:T(8,128)(2,1)S(1)} collective-permute-done((bf16[256,1024]{1,0:T(8,128)(2,1)S(1)}, bf16[256,1024]{1,0:T(8,128)(2,1)S(1)}, u32[]{:S(2)}, u32[]{:S(2)}) %collective-permute-start.15) | collective-permute-done | bytes 524320 | tf_op jit(solution)/shard_map/ppermute | solution.py:523
  300.7 5.8 fusion.60
  313.9 8.9 %collective-permute-done.16 = f32[256,1024]{1,0:T(8,128)} collective-permute-done((f32[256,1024]{1,0:T(8,128)}, f32[256,1024]{1,0:T(8,128)}, u32[]{:S(2)}, u32[]{:S(2)}) %collective-permute-start.16) | collective-permute-done | bytes 1048608 | tf_op jit(solution)/shard_map/ppermute | solution.py:523
  326.4 11.8 %collective-permute-done.21 = bf16[256,1024]{1,0:T(8,128)(2,1)S(1)} collective-permute-done((bf16[256,1024]{1,0:T(8,128)(2,1)S(1)}, bf16[256,1024]{1,0:T(8,128)(2,1)S(1)}, u32[]{:S(2)}, u32[]{:S(2)}) %collective-permute-start.21) | collective-permute-done | bytes 524320 | tf_op jit(solution)/shard_map/ppermute | solution.py:523
  342.3 5.0 fusion.57
  347.2 4.8 multiply_convert_fusion.3
  360.2 5.3 fusion.114
  365.5 6.5 convolution_add_fusion
  395.3 12.8 %collective-permute-done.27 = bf16[256,1024]{1,0:T(8,128)(2,1)S(1)} collective-permute-done((bf16[256,1024]{1,0:T(8,128)(2,1)S(1)}, bf16[256,1024]{1,0:T(8,128)(2,1)S(1)}, u32[]{:S(2)}, u32[]{:S(2)}) %collective-permute-start.27) | collective-permute-done | bytes 524320 | tf_op jit(solution)/shard_map/ppermute | solution.py:523
  422.1 36.7 %mixer_backward.2 = (bf16[1024,1664]{1,0:T(8,128)(2,1)}, f32[32,1024]{1,0:T(8,128)}, f32[8,256]{1,0:T(8,128)}, f32[16,128]{1,0:T(8,128)}, f32[2,128,256]{2,1,0:T(8,128)}, /*index=5*/f32[8,1024]{1,0:T(8,128)}) custom-call(s32[3]{0:T(128)} %select_reduce_fusion.3.ends_ref, f32[1024,1664]{1,0:T(8,128)} %fusion.16.proj_ref.halo_ref, ...), custom_call_target="tpu_custom_call" | custom-call | flops 2048000000 | bytes 18432000 | tf_op jit(solution)/shard_map/mixer_backward/pallas_call | solution.py:453
  458.9 7.0 fusion.44
  496.6 18.7 %collective-permute-done.35 = bf16[128,2112]{0,1:T(8,128)(2,1)S(1)} collective-permute-done((bf16[128,2112]{0,1:T(8,128)(2,1)}, bf16[128,2112]{0,1:T(8,128)(2,1)S(1)}, u32[]{:S(2)}, u32[]{:S(2)}) %collective-permute-start.35) | collective-permute-done | bytes 540704 | tf_op jit(solution)/shard_map/ppermute | solution.py:528
  520.1 37.1 %mixer_backward.3 = (bf16[1024,1664]{1,0:T(8,128)(2,1)}, f32[32,1024]{1,0:T(8,128)}, f32[8,256]{1,0:T(8,128)}, f32[16,128]{1,0:T(8,128)}, f32[2,128,256]{2,1,0:T(8,128)}, /*index=5*/f32[8,1024]{1,0:T(8,128)}) custom-call(s32[3]{0:T(128)} %select_reduce_fusion.3.ends_ref, f32[1024,1664]{1,0:T(8,128)} %fusion.18.proj_ref.before_ref.halo_ref, ...), custom_call_target="tpu_custom_call" | custom-call | flops 2048000000 | bytes 18432000 | tf_op jit(solution)/shard_map/mixer_backward/pallas_call | solution.py:453
  559.3 6.9 fusion.117
  573.6 7.0 fusion.47
  588.0 11.3 %collective-permute-done.38 = bf16[256,1024]{1,0:T(8,128)(2,1)S(1)} collective-permute-done((bf16[256,1024]{1,0:T(8,128)(2,1)S(1)}, bf16[256,1024]{1,0:T(8,128)(2,1)S(1)}, u32[]{:S(2)}, u32[]{:S(2)}) %collective-permute-start.38) | collective-permute-done | bytes 524320 | tf_op jit(solution)/shard_map/ppermute | solution.py:523
  599.4 9.8 %collective-permute-done.37 = bf16[256,1024]{1,0:T(8,128)(2,1)S(1)} collective-permute-done((bf16[256,1024]{1,0:T(8,128)(2,1)S(1)}, bf16[256,1024]{1,0:T(8,128)(2,1)S(1)}, u32[]{:S(2)}, u32[]{:S(2)}) %collective-permute-start.37) | collective-permute-done | bytes 524320 | tf_op jit(solution)/shard_map/ppermute | solution.py:523
  613.1 6.0 all-to-all-start.3
  626.5 9.0 %collective-permute-done.42 = f32[8,384]{1,0:T(8,128)S(1)} collective-permute-done((f32[8,384]{1,0:T(8,128)S(1)}, f32[8,384]{1,0:T(8,128)S(1)}, u32[]{:S(2)}, u32[]{:S(2)}) %collective-permute-start.42) | collective-permute-done | bytes 12320 | tf_op jit(solution)/shard_map/ppermute | solution.py:523
  648.2 28.7 %reduce-scatter.5.cloned.1.call-done = bf16[128,2176]{1,0:T(8,128)(2,1)} async-done(((bf16[1024,2176]{1,0:T(8,128)(2,1)}), bf16[128,2176]{1,0:T(8,128)(2,1)}) %reduce-scatter.5.cloned.1.call-update) | async-done | bytes 557072 | tf_op jit(solution)/shard_map/reduce_scatter | solution.py:594
  685.8 22.1 %collective-permute-done.39 = bf16[128,2176]{1,0:T(8,128)(2,1)S(1)} collective-permute-done((bf16[128,2176]{1,0:T(8,128)(2,1)}, bf16[128,2176]{1,0:T(8,128)(2,1)S(1)}, u32[]{:S(2)}, u32[]{:S(2)}) %collective-permute-start.39) | collective-permute-done | bytes 557088 | tf_op jit(solution)/shard_map/ppermute | solution.py:528
  (426 shorter events, 243.9 us)
Async XLA Ops:
  7.2 140.9 %all-gather.3.cloned.1.call-start = ((), (), s32[]{:S(2)}) async-start(), calls=%async_computation.6 | async-start | bytes 5013504 | tf_op jit(solution)/shard_map/all_gather | solution.py:589
  10.9 30.7 %collective-permute-start.6 = (bf16[128,2176]{1,0:T(8,128)(2,1)S(1)}, bf16[128,2176]{1,0:T(8,128)(2,1)S(1)}, u32[]{:S(2)}, u32[]{:S(2)}) collective-permute-start(bf16[128,2176]{1,0:T(8,128)(2,1)S(1)} %concatenate.101), channel_id=1, source_target_pairs={{0,0},{1,4},{2,8},{3,12},{4,1},{5,5},{6,9},{7,13},{8,2},{9,6},{10,... | collective-permute-start | bytes 1671176 | tf_op jit(solution)/shard_map/ppermute | solution.py:528
  44.4 45.8 %all-to-all-start = ((bf16[8,64,1024]{2,1,0:T(8,128)(2,1)}), bf16[8,64,1024]{2,1,0:T(8,128)(2,1)S(1)}, u32[]{:S(2)}, u32[]{:S(2)}) async-start(bf16[8,64,1024]{2,1,0:T(8,128)(2,1)} %bitcast.1), calls=%async_computation | async-start | bytes 2097152 | tf_op jit(solution)/shard_map/all_to_all | solution.py:641
  48.0 52.4 %collective-permute-start = (s32[1,3]{1,0:T(1,128)S(1)}, s32[1,3]{1,0:T(1,128)S(1)}, u32[]{:S(2)}, u32[]{:S(2)}) collective-permute-start(s32[1,3]{1,0:T(1,128)S(1)} %copy-done.53), channel_id=1, source_target_pairs={{0,0},{1,4},{2,8},{3,12},{4,1},{5,5},{6,9},{7,13},{8,2},{9,6},{10,... | collective-permute-start | bytes 44 | tf_op jit(solution)/shard_map/ppermute | solution.py:528
  51.0 49.3 %collective-permute-start.1 = (s32[512]{0:T(512)S(1)}, s32[512]{0:T(512)S(1)}, u32[]{:S(2)}, u32[]{:S(2)}) collective-permute-start(s32[512]{0:T(512)S(1)} %copy-done.50), channel_id=1, source_target_pairs={{0,0},{1,4},{2,8},{3,12},{4,1},{5,5},{6,9},{7,13},{8,2},{9,6},{10,... | collective-permute-start | bytes 6152 | tf_op jit(solution)/shard_map/ppermute | solution.py:528
  95.8 25.5 %collective-permute-start.4 = (bf16[256,1024]{1,0:T(8,128)(2,1)S(1)}, bf16[256,1024]{1,0:T(8,128)(2,1)}, u32[]{:S(2)}, u32[]{:S(2)}) collective-permute-start(bf16[256,1024]{1,0:T(8,128)(2,1)S(1)} %get-tuple-element.255), channel_id=1, source_target_pairs={{0,8},{4,12},{8,0},{12,4},{1,9},{5,13},{9,1},{13,5},{2,10},{6,14},... | collective-permute-start | bytes 1572872 | tf_op jit(solution)/shard_map/ppermute | solution.py:523
  95.9 28.0 %collective-permute-start.7 = (bf16[256,1024]{1,0:T(8,128)(2,1)S(1)}, bf16[256,1024]{1,0:T(8,128)(2,1)}, u32[]{:S(2)}, u32[]{:S(2)}) collective-permute-start(bf16[256,1024]{1,0:T(8,128)(2,1)S(1)} %get-tuple-element.254), channel_id=1, source_target_pairs={{0,8},{4,12},{8,0},{12,4},{1,9},{5,13},{9,1},{13,5},{2,10},{6,14},... | collective-permute-start | bytes 1572872 | tf_op jit(solution)/shard_map/ppermute | solution.py:523
  100.3 21.0 %collective-permute-start.2 = (s32[512]{0:T(512)S(1)}, s32[512]{0:T(512)S(1)}, u32[]{:S(2)}, u32[]{:S(2)}) collective-permute-start(s32[512]{0:T(512)S(1)} %collective-permute-done.1), channel_id=1, source_target_pairs={{0,8},{4,12},{8,0},{12,4},{1,9},{5,13},{9,1},{13,5},{2,10},{6,14},... | collective-permute-start | bytes 6152 | tf_op jit(solution)/shard_map/ppermute | solution.py:523
  134.2 38.6 %collective-permute-start.9 = (bf16[128,2112]{0,1:T(8,128)(2,1)}, bf16[128,2112]{0,1:T(8,128)(2,1)}, u32[]{:S(2)}, u32[]{:S(2)}) collective-permute-start(bf16[128,2112]{0,1:T(8,128)(2,1)} %pad_maximum_fusion.19), channel_id=1, source_target_pairs={{0,0},{1,4},{2,8},{3,12},{4,1},{5,5},{6,9},{7,13},{8,2},{9,6},{10,... | collective-permute-start | bytes 1622024 | tf_op jit(solution)/shard_map/ppermute | solution.py:528
  138.2 76.4 %all-to-all-start.1 = ((bf16[8,64,1024]{2,1,0:T(8,128)(2,1)}), bf16[8,64,1024]{2,1,0:T(8,128)(2,1)S(1)}, u32[]{:S(2)}, u32[]{:S(2)}) async-start(bf16[8,64,1024]{2,1,0:T(8,128)(2,1)} %bitcast.224), calls=%async_computation.1 | async-start | bytes 2097152 | tf_op jit(solution)/shard_map/all_to_all | solution.py:641
  143.7 157.0 %all-gather.5.cloned.1.call-start = ((), (), s32[]{:S(2)}) async-start(), calls=%async_computation.7 | async-start | bytes 4866048 | tf_op jit(solution)/shard_map/all_gather | solution.py:589
  211.3 30.2 %collective-permute-start.10 = (f32[512,1024]{1,0:T(8,128)}, f32[512,1024]{1,0:T(8,128)}, u32[]{:S(2)}, u32[]{:S(2)}) collective-permute-start(f32[512,1024]{1,0:T(8,128)} %slice.310), channel_id=1, source_target_pairs={{0,4},{4,0},{8,12},{12,8},{1,5},{5,1},{9,13},{13,9},{2,6},{6,2},{1... | collective-permute-start | bytes 6291464 | tf_op jit(solution)/shard_map/ppermute | solution.py:523
  211.4 272.0 %reduce-scatter.3.cloned.1.call-start = ((), (), s32[]{:S(2)}) async-start(), calls=%async_computation.8 | async-start | bytes 5013504 | tf_op jit(solution)/shard_map/reduce_scatter | solution.py:594
  214.9 25.6 %collective-permute-start.12 = (bf16[256,1024]{1,0:T(8,128)(2,1)S(1)}, bf16[256,1024]{1,0:T(8,128)(2,1)S(1)}, u32[]{:S(2)}, u32[]{:S(2)}) collective-permute-start(bf16[256,1024]{1,0:T(8,128)(2,1)S(1)} %bitcast.208), channel_id=1, source_target_pairs={{0,8},{4,12},{8,0},{12,4},{1,9},{5,13},{9,1},{13,5},{2,10},{6,14},... | collective-permute-start | bytes 1572872 | tf_op jit(solution)/shard_map/ppermute | solution.py:523
  244.6 32.2 %collective-permute-start.14 = (f32[256,1024]{1,0:T(8,128)}, f32[256,1024]{1,0:T(8,128)S(1)}, u32[]{:S(2)}, u32[]{:S(2)}) collective-permute-start(f32[256,1024]{1,0:T(8,128)} %get-tuple-element.96), channel_id=1, source_target_pairs={{0,8},{4,12},{8,0},{12,4},{1,9},{5,13},{9,1},{13,5},{2,10},{6,14},... | collective-permute-start | bytes 3145736 | tf_op jit(solution)/shard_map/ppermute | solution.py:523
  279.7 17.1 %collective-permute-start.17 = (bf16[512,1024]{1,0:T(8,128)(2,1)S(1)}, bf16[512,1024]{1,0:T(8,128)(2,1)S(1)}, u32[]{:S(2)}, u32[]{:S(2)}) collective-permute-start(bf16[512,1024]{1,0:T(8,128)(2,1)S(1)} %pad_maximum_fusion.12), channel_id=1, source_target_pairs={{0,4},{4,0},{8,12},{12,8},{1,5},{5,1},{9,13},{13,9},{2,6},{6,2},{1... | collective-permute-start | bytes 3145736 | tf_op jit(solution)/shard_map/ppermute | solution.py:523
  296.8 26.0 %collective-permute-start.16 = (f32[256,1024]{1,0:T(8,128)}, f32[256,1024]{1,0:T(8,128)}, u32[]{:S(2)}, u32[]{:S(2)}) collective-permute-start(f32[256,1024]{1,0:T(8,128)} %get-tuple-element.99), channel_id=1, source_target_pairs={{0,8},{4,12},{8,0},{12,4},{1,9},{5,13},{9,1},{13,5},{2,10},{6,14},... | collective-permute-start | bytes 3145736 | tf_op jit(solution)/shard_map/ppermute | solution.py:523
  313.7 24.6 %collective-permute-start.20 = (bf16[512,1024]{1,0:T(8,128)(2,1)S(1)}, bf16[512,1024]{1,0:T(8,128)(2,1)S(1)}, u32[]{:S(2)}, u32[]{:S(2)}) collective-permute-start(bf16[512,1024]{1,0:T(8,128)(2,1)S(1)} %slice.326), channel_id=1, source_target_pairs={{0,4},{4,0},{8,12},{12,8},{1,5},{5,1},{9,13},{13,9},{2,6},{6,2},{1... | collective-permute-start | bytes 3145736 | tf_op jit(solution)/shard_map/ppermute | solution.py:523
  340.3 16.1 %collective-permute-start.24 = (bf16[256,1024]{1,0:T(8,128)(2,1)S(1)}, bf16[256,1024]{1,0:T(8,128)(2,1)S(1)}, u32[]{:S(2)}, u32[]{:S(2)}) collective-permute-start(bf16[256,1024]{1,0:T(8,128)(2,1)S(1)} %slice.431), channel_id=1, source_target_pairs={{0,8},{4,12},{8,0},{12,4},{1,9},{5,13},{9,1},{13,5},{2,10},{6,14},... | collective-permute-start | bytes 1572872 | tf_op jit(solution)/shard_map/ppermute | solution.py:523
  392.1 16.0 %collective-permute-start.28 = (bf16[512,1024]{1,0:T(8,128)(2,1)}, bf16[512,1024]{1,0:T(8,128)(2,1)S(1)}, u32[]{:S(2)}, u32[]{:S(2)}) collective-permute-start(bf16[512,1024]{1,0:T(8,128)(2,1)} %pad_maximum_fusion.16), channel_id=1, source_target_pairs={{0,4},{4,0},{8,12},{12,8},{1,5},{5,1},{9,13},{13,9},{2,6},{6,2},{1... | collective-permute-start | bytes 3145736 | tf_op jit(solution)/shard_map/ppermute | solution.py:523
  393.7 16.2 %collective-permute-start.29 = (bf16[512,1024]{1,0:T(8,128)(2,1)S(1)}, bf16[512,1024]{1,0:T(8,128)(2,1)S(1)}, u32[]{:S(2)}, u32[]{:S(2)}) collective-permute-start(bf16[512,1024]{1,0:T(8,128)(2,1)S(1)} %slice.269), channel_id=1, source_target_pairs={{0,4},{4,0},{8,12},{12,8},{1,5},{5,1},{9,13},{13,9},{2,6},{6,2},{1... | collective-permute-start | bytes 3145736 | tf_op jit(solution)/shard_map/ppermute | solution.py:523
  395.2 16.5 %collective-permute-start.30 = (bf16[512,1024]{1,0:T(8,128)(2,1)S(1)}, bf16[512,1024]{1,0:T(8,128)(2,1)S(1)}, u32[]{:S(2)}, u32[]{:S(2)}) collective-permute-start(bf16[512,1024]{1,0:T(8,128)(2,1)S(1)} %slice.273), channel_id=1, source_target_pairs={{0,4},{4,0},{8,12},{12,8},{1,5},{5,1},{9,13},{13,9},{2,6},{6,2},{1... | collective-permute-start | bytes 3145736 | tf_op jit(solution)/shard_map/ppermute | solution.py:523
  413.0 57.7 %collective-permute-start.33 = (bf16[256,1024]{1,0:T(8,128)(2,1)S(1)}, bf16[256,1024]{1,0:T(8,128)(2,1)}, u32[]{:S(2)}, u32[]{:S(2)}) collective-permute-start(bf16[256,1024]{1,0:T(8,128)(2,1)S(1)} %slice.429), channel_id=1, source_target_pairs={{0,8},{4,12},{8,0},{12,4},{1,9},{5,13},{9,1},{13,5},{2,10},{6,14},... | collective-permute-start | bytes 1572872 | tf_op jit(solution)/shard_map/ppermute | solution.py:523
  414.0 58.8 %collective-permute-start.34 = (bf16[256,1024]{1,0:T(8,128)(2,1)}, bf16[256,1024]{1,0:T(8,128)(2,1)}, u32[]{:S(2)}, u32[]{:S(2)}) collective-permute-start(bf16[256,1024]{1,0:T(8,128)(2,1)} %slice.428), channel_id=1, source_target_pairs={{0,8},{4,12},{8,0},{12,4},{1,9},{5,13},{9,1},{13,5},{2,10},{6,14},... | collective-permute-start | bytes 1572872 | tf_op jit(solution)/shard_map/ppermute | solution.py:523
  458.8 16.1 %collective-permute-start.31 = (bf16[512,1024]{1,0:T(8,128)(2,1)S(1)}, bf16[512,1024]{1,0:T(8,128)(2,1)S(1)}, u32[]{:S(2)}, u32[]{:S(2)}) collective-permute-start(bf16[512,1024]{1,0:T(8,128)(2,1)S(1)} %pad_maximum_fusion.17), channel_id=1, source_target_pairs={{0,4},{4,0},{8,12},{12,8},{1,5},{5,1},{9,13},{13,9},{2,6},{6,2},{1... | collective-permute-start | bytes 3145736 | tf_op jit(solution)/shard_map/ppermute | solution.py:523
  470.2 19.5 %collective-permute-start.32 = (bf16[512,1024]{1,0:T(8,128)(2,1)}, bf16[512,1024]{1,0:T(8,128)(2,1)}, u32[]{:S(2)}, u32[]{:S(2)}) collective-permute-start(bf16[512,1024]{1,0:T(8,128)(2,1)} %bitcast.57), channel_id=1, source_target_pairs={{0,4},{4,0},{8,12},{12,8},{1,5},{5,1},{9,13},{13,9},{2,6},{6,2},{1... | collective-permute-start | bytes 3145736 | tf_op jit(solution)/shard_map/ppermute | solution.py:523
  485.4 29.9 %collective-permute-start.35 = (bf16[128,2112]{0,1:T(8,128)(2,1)}, bf16[128,2112]{0,1:T(8,128)(2,1)S(1)}, u32[]{:S(2)}, u32[]{:S(2)}) collective-permute-start(bf16[128,2112]{0,1:T(8,128)(2,1)} %copy.193), channel_id=1, source_target_pairs={{0,0},{1,4},{2,8},{3,12},{4,1},{5,5},{6,9},{7,13},{8,2},{9,6},{10,... | collective-permute-start | bytes 1622024 | tf_op jit(solution)/shard_map/ppermute | solution.py:528
  516.5 42.7 %all-to-all-start.2 = ((bf16[8,64,1024]{2,1,0:T(8,128)(2,1)}), bf16[8,64,1024]{2,1,0:T(8,128)(2,1)S(1)}, u32[]{:S(2)}, u32[]{:S(2)}) async-start(bf16[8,64,1024]{2,1,0:T(8,128)(2,1)} %bitcast.60), calls=%async_computation.3 | async-start | bytes 2097152 | tf_op jit(solution)/shard_map/all_to_all | solution.py:641
  520.1 156.9 %reduce-scatter.5.cloned.1.call-start = ((), (), s32[]{:S(2)}) async-start(), calls=%async_computation.9 | async-start | bytes 5013504 | tf_op jit(solution)/shard_map/reduce_scatter | solution.py:594
  586.8 22.4 %collective-permute-start.37 = (bf16[256,1024]{1,0:T(8,128)(2,1)S(1)}, bf16[256,1024]{1,0:T(8,128)(2,1)S(1)}, u32[]{:S(2)}, u32[]{:S(2)}) collective-permute-start(bf16[256,1024]{1,0:T(8,128)(2,1)S(1)} %slice.426), channel_id=1, source_target_pairs={{0,8},{4,12},{8,0},{12,4},{1,9},{5,13},{9,1},{13,5},{2,10},{6,14},... | collective-permute-start | bytes 1572872 | tf_op jit(solution)/shard_map/ppermute | solution.py:523
  613.1 69.7 %all-to-all-start.3 = ((bf16[8,64,1024]{2,1,0:T(8,128)(2,1)}), bf16[8,64,1024]{2,1,0:T(8,128)(2,1)}, u32[]{:S(2)}, u32[]{:S(2)}) async-start(bf16[8,64,1024]{2,1,0:T(8,128)(2,1)} %bitcast.73), calls=%async_computation.4 | async-start | bytes 2097152 | tf_op jit(solution)/shard_map/all_to_all | solution.py:641
  677.0 31.0 %collective-permute-start.39 = (bf16[128,2176]{1,0:T(8,128)(2,1)}, bf16[128,2176]{1,0:T(8,128)(2,1)S(1)}, u32[]{:S(2)}, u32[]{:S(2)}) collective-permute-start(bf16[128,2176]{1,0:T(8,128)(2,1)} %reduce-scatter.5.cloned.1.call-done), channel_id=1, source_target_pairs={{0,0},{1,4},{2,8},{3,12},{4,1},{5,5},{6,9},{7,13},{8,2},{9,6},{10,... | collective-permute-start | bytes 1671176 | tf_op jit(solution)/shard_map/ppermute | solution.py:528
  (87 other events, 781.0 us)
Sparse Core Ops, SparseCore 0:
  42.5 92.9 all-gather.2
  211.5 75.5 all-gather.4
  392.3 90.6 reduce-scatter.2
  573.7 103.2 reduce-scatter.4

commit v3 on v2

--- a/solution.py
+++ b/solution.py
@@ -32,7 +32,7 @@
 def dot3(a, b, ca=1, cb=0):
     ah, al = halves(a)
     bh, bl = halves(b)
-    return dot(ah, bh, ca, cb) + (dot(ah, bl, ca, cb) + dot(al, bh, ca, cb))
+    return dot(jnp.concatenate([ah, al, ah], axis=ca), jnp.concatenate([bh, bh, bl], axis=cb), ca, cb)
 
 
 def dot_exact(a, b, ca=1, cb=0):
@@ -429,7 +429,7 @@
             dimension_semantics=("arbitrary",), vmem_limit_bytes=56 * 1024 * 1024
         ),
         cost_estimate=pl.CostEstimate(
-            flops=total * heads * 6_000_000, bytes_accessed=total * heads * 9_000, transcendentals=total * heads * 2_000
+            flops=total * heads * 1_000_000, bytes_accessed=total * heads * 9_000, transcendentals=total * heads * 2_000
         ),
         name="mixer_forward",
     )(ends, proj, before, taps, rate, shift, gain, enter)
@@ -504,7 +504,8 @@
     )(ends, proj, proj, before, taps, rate, shift, gain, dgated, *saved, leave, later)
 
 
-BLOCK_ROWS = 256
+FORWARD_ROWS = 512
+BACKWARD_ROWS = 256
 RUNS = 2
 
 
@@ -590,9 +591,7 @@
 
 
 def narrow(columns):
-    return exchange_roles(
-        lax.psum_scatter(columns.astype(bf16), ("hi", "tensor"), scatter_dimension=0, tiled=True)
-    ).astype(f32)
+    return lax.psum_scatter(columns.astype(bf16), ("hi", "tensor"), scatter_dimension=0, tiled=True)
 
 
 def product(a, b, ca=1, cb=0, dtype=f32):
@@ -641,56 +640,60 @@
         return lax.all_to_all(rows, spread, split_axis=0, concat_axis=0, tiled=True)
 
     def pack(rows):
-        return across(product(send_hot, rows, dtype=bf16).reshape(groups, per_peer, model_width))
+        return product(send_hot, rows, dtype=bf16).reshape(groups, per_peer, -1)
 
     def by_part(rows):
-        rows = jnp.transpose(rows.reshape(width, splits, per_peer, model_width), (1, 0, 2, 3))
-        return rows.reshape(local_rows, model_width)
-
-    def send_back(rows):
+        rows = jnp.transpose(rows.reshape(width, splits, per_peer, -1), (1, 0, 2, 3))
+        return rows.reshape(local_rows, -1)
+
+    def from_part(rows):
         rows = jnp.transpose(rows.reshape(splits, width, per_peer, model_width), (1, 0, 2, 3))
-        return across(rows.reshape(groups, per_peer, model_width))
-
-    def unpack(got):
-        return product(send_hot, got.reshape(local_rows, model_width), 0, 0, bf16)
-
-    pieces = jnp.array(reversed_bits(splits), jnp.int32)
-    orders = gather_rows(exchange_roles(token_order)).reshape(splits, local_rows)
-    parts = jnp.arange(splits, dtype=jnp.int32)
-    stand = jnp.sum(jnp.where(pieces[None, :] == (parts ^ me)[:, None], parts[None, :], 0), axis=1)
-    orders = jnp.sum(jnp.where((stand[:, None] == parts[None, :])[:, :, None], orders[None], 0), axis=1)
-    given = orders // group_rows
-    place_of = rank_of(given * local_rows + span[None, :]) % per_peer
-    piece_of = jnp.sum(jnp.where((given % splits)[..., None] == parts, stand, 0), axis=-1)
-    held_at = (piece_of * width + given // splits) * per_peer + place_of
-    order_hot = (held_at[:, :, None] == span[None, None, :]).astype(bf16)
+        return rows.reshape(groups, per_peer, model_width)
+
+    def unpack(rows):
+        return product(send_hot, rows.reshape(local_rows, model_width), 0, 0, bf16)
+
+    place = token_return % local_rows
+    lane = jnp.arange(128, dtype=jnp.int32)[None, :]
+    digits = jnp.where(lane == 0, (place // 16)[:, None], jnp.where(lane == 1, (place % 16)[:, None], 0))
+    tagged = jnp.concatenate([tokens, digits.astype(bf16)], axis=1)
+    arrived = across(pack(tagged))
+    packed_grad = across(pack(after(cotangent, arrived)))
     run_parts = splits // RUNS
     run_rows = run_parts * local_rows
 
-    def order_of(run):
-        return order_hot[run * run_parts : (run + 1) * run_parts]
-
-    def to_sequence(run, rows):
+    def in_parts(rows):
         rows = rows.reshape(splits, run_parts, part_rows, -1)
-        rows = jnp.transpose(rows, (1, 0, 2, 3)).reshape(run_parts, local_rows, -1)
+        return jnp.transpose(rows, (1, 0, 2, 3)).reshape(run_parts, local_rows, -1)
+
+    def order_of(tags):
+        tags = in_parts(tags)[:, :, :2].astype(jnp.int32)
+        at = tags[:, :, 0] * 16 + tags[:, :, 1]
+        return (at[:, None, :] == span[None, :, None]).astype(bf16)
+
+    def to_sequence(order, rows):
         return lax.dot_general(
-            order_of(run), rows, (((2,), (1,)), ((0,), (0,))), preferred_element_type=f32
+            order, in_parts(rows), (((2,), (1,)), ((0,), (0,))), preferred_element_type=f32
         ).astype(bf16).reshape(run_rows, -1)
 
-    def from_sequence(run, rows):
+    def from_sequence(order, rows):
         rows = lax.dot_general(
-            order_of(run), rows.reshape(run_parts, local_rows, -1), (((1,), (1,)), ((0,), (0,))),
+            order, rows.reshape(run_parts, local_rows, -1), (((1,), (1,)), ((0,), (0,))),
             preferred_element_type=f32,
         ).astype(bf16).reshape(run_parts, splits, part_rows, -1)
         return jnp.transpose(rows, (1, 0, 2, 3)).reshape(run_rows, -1)
 
+    head_start = me * heads
+    lanes = jnp.zeros((1, 128), f32)
+    rate_row = lanes.at[0, 1 : 2 * heads : 2].set(lax.dynamic_slice_in_dim(decay_log, head_start, heads))
+    shift_row = lanes.at[0, 1 : 2 * heads : 2].set(lax.dynamic_slice_in_dim(decay_bias, head_start, heads))
     own_lengths = exchange_roles(lengths)
     ends = jnp.sum(jnp.where(jnp.tri(SEQS, dtype=bool), own_lengths, 0), axis=1).astype(jnp.int32)
     small_at = proj_width
     conv_at = small_at + heads * w_ba.shape[2]
     spare = 128 - heads * w_ba.shape[2] - taps
-    mix_all = widen(
-        exchange_roles(jnp.concatenate(
+    mix_own = exchange_roles(
+        jnp.concatenate(
             [
                 w_mix.reshape(weight_rows, proj_width).astype(bf16),
                 w_ba.reshape(weight_rows, -1).astype(bf16),
@@ -699,9 +702,11 @@
                 w_out.reshape(weight_rows, heads * DV).astype(bf16),
             ],
             axis=1,
-        ))
+        )
     )
-    packed_in = by_part(pack(tokens))
+    mix_all = widen(mix_own)
+    arrived = by_part(after(arrived, ends, rate_row, shift_row))
+    packed_in, tags = arrived[:, :model_width], arrived[:, model_width:]
     runs = range(RUNS)
     own_rows = local_rows // RUNS
 
@@ -711,23 +716,16 @@
     input_f32 = packed_in.astype(f32)
     input_scale = rms_scale(input_f32)
     input_runs = split(input_f32)
-    gathered = [gather_rows(x) for x in split((input_f32 * input_scale * gain_attn).astype(bf16))]
-    cotangent, w_down, w_gate_up = after((cotangent, w_down, w_gate_up), *gathered)
-    packed_grad = pack(cotangent)
-    ffn_own = exchange_roles(
-        jnp.concatenate([w_gate_up.reshape(weight_rows, 2 * units).astype(bf16), w_down.astype(bf16)], axis=1)
+    normed_runs = split(jnp.concatenate([(input_f32 * input_scale * gain_attn).astype(bf16), tags], axis=1))
+    gathered_0 = gather_rows(normed_runs[0])
+    ffn_sent = jnp.concatenate(
+        [w_gate_up.reshape(weight_rows, 2 * units).astype(bf16), w_down.astype(bf16)], axis=1
     )
-    ffn_all = widen(ffn_own)
-    w_pair, w_last = ffn_all[:, : 2 * units], ffn_all[:, 2 * units :]
     out_all = mix_all[:, small_at + 128 :]
     mix_all = mix_all[:, : small_at + 128]
 
     conv_all = mix_all[:, conv_at : conv_at + taps].reshape(-1, heads, taps).astype(f32)
     tap_rows = jnp.transpose(conv_all, (2, 1, 0)).reshape(taps, heads * conv_width)
-    head_start = me * heads
-    lanes = jnp.zeros((1, 128), f32)
-    rate_row = lanes.at[0, 1 : 2 * heads : 2].set(lax.dynamic_slice_in_dim(decay_log, head_start, heads))
-    shift_row = lanes.at[0, 1 : 2 * heads : 2].set(lax.dynamic_slice_in_dim(decay_bias, head_start, heads))
     gain_row = gain_out[None]
     constants = (tap_rows, rate_row, shift_row, gain_row)
 
@@ -738,13 +736,13 @@
 
     def mix_forward(r, state):
         return mixer_forward(
-            ends, projected[r], *ahead(r), *constants, state, heads=heads, rows=BLOCK_ROWS, start=r * run_rows
+            ends, projected[r], *ahead(r), *constants, state, heads=heads, rows=FORWARD_ROWS, start=r * run_rows
         )
 
     def feed_forward(r, normed_mid):
         place = (r * run_parts + jnp.arange(run_parts, dtype=jnp.int32))[:, None, None] * local_rows
         alive = (place + span[None, :, None] < ends[SEQS - 1]).astype(bf16)
-        live = from_sequence(r, jnp.broadcast_to(alive, (run_parts, local_rows, 128)))[:, :1].astype(f32)
+        live = from_sequence(orders[r], jnp.broadcast_to(alive, (run_parts, local_rows, 128)))[:, :1].astype(f32)
         grad_hidden = product(grad_all[r], w_last) * live
         gate_up = product(normed_mid, w_pair)
         gate, up = gate_up[:, :units], gate_up[:, units:]
@@ -760,24 +758,37 @@
         return scale, (middle * scale * gain_ffn).astype(bf16)
 
     constants = (tap_rows, rate_row, shift_row, gain_row)
-    seq_0 = to_sequence(0, gathered[0])
-    projected = [after(product(seq_0, mix_all), ffn_own)]
+    orders = [order_of(gathered_0[:, model_width:])]
+    seq_0 = to_sequence(orders[0], gathered_0[:, :model_width])
+    projected = [product(seq_0, mix_all)]
+    packed_grad = by_part(packed_grad)
+    projected[0], normed_runs, ffn_sent, packed_grad = lax.optimization_barrier(
+        (projected[0], normed_runs, ffn_sent, packed_grad)
+    )
     *saved_0, state = mix_forward(0, state)
-    terms_0 = product(from_sequence(0, saved_0[0]), out_all, 1, 1)
-    seq_1 = to_sequence(1, after(gathered[1], terms_0))
+    crossed = swap(packed_grad, "lo", bits(splits)[-1])
+    saved_0, first_1, ffn_own = lax.optimization_barrier(
+        (saved_0, gather_first(normed_runs[1]), exchange_roles(ffn_sent))
+    )
+    ffn_all = widen(ffn_own)
+    grad_runs = split(packed_grad)
+    gathered_1 = gather_last(first_1)
+    terms_0 = product(from_sequence(orders[0], saved_0[0]), out_all, 1, 1)
+    gathered_1 = after(gathered_1, terms_0)
+    orders.append(order_of(gathered_1[:, model_width:]))
+    seq_1 = to_sequence(orders[1], gathered_1[:, :model_width])
     projected.append(product(seq_1, mix_all))
-    grad_runs = split(by_part(after(packed_grad, terms_0)))
     kept_0, sent_0 = scatter_first(terms_0)
-    grad_first = [gather_first(x) for x in grad_runs]
-    projected[1], kept_0, sent_0, grad_first = lax.optimization_barrier((projected[1], kept_0, sent_0, grad_first))
-    grad_all = [gather_last(x) for x in grad_first]
+    projected[1], kept_0, sent_0, crossed = lax.optimization_barrier((projected[1], kept_0, sent_0, crossed))
+    grad_all = [gather_last(jnp.concatenate(x, axis=0)) for x in zip(grad_runs, split(crossed))]
     *saved_1, state = mix_forward(1, state)
     middle_0 = input_runs[0] + after(scatter_last(kept_0, sent_0), saved_1[0])
     scale_0, normed_mid_0 = normed_of(middle_0)
-    terms_1 = product(from_sequence(1, saved_1[0]), out_all, 1, 1)
+    terms_1 = product(from_sequence(orders[1], saved_1[0]), out_all, 1, 1)
     first_0 = gather_first(normed_mid_0)
     kept_1, sent_1 = scatter_first(terms_1)
-    kept_1, sent_1, first_0 = lax.optimization_barrier((kept_1, sent_1, first_0))
+    kept_1, sent_1, first_0, ffn_all = lax.optimization_barrier((kept_1, sent_1, first_0, ffn_all))
+    w_pair, w_last = ffn_all[:, : 2 * units], ffn_all[:, 2 * units :]
     normed_mid_0 = gather_last(first_0)
 
     hidden_0, pair_0, grad_terms_0 = feed_forward(0, normed_mid_0)
@@ -807,49 +818,48 @@
     first_1, grad_last, layer_terms, grad_low_0 = lax.optimization_barrier(
         (first_1, grad_last, layer_terms, grad_middle_0.astype(bf16))
     )
-    grad_mid_seq_1 = to_sequence(1, gather_last(first_1))
+    grad_mid_seq_1 = to_sequence(orders[1], gather_last(first_1))
     grad_ffn = narrow(jnp.concatenate([grad_pairs.astype(bf16), grad_last.astype(bf16)], axis=1))
 
     def mix_backward(r, grad_gated, saved, leave, later):
         return mixer_backward(
             ends, projected[r], *ahead(r), *constants, grad_gated, saved[1:], leave, later,
-            heads=heads, rows=BLOCK_ROWS, start=r * run_rows,
+            heads=heads, rows=BACKWARD_ROWS, start=r * run_rows,
         )
 
     leave = jnp.zeros((heads, DK, DV), f32)
     later = jnp.zeros((8, heads * conv_width), f32)
-    first_0 = gather_first(grad_low_0)
     layer_parts = [scatter_first(x) for x in layer_terms]
     grad_gated_1 = product(grad_mid_seq_1, out_all)
-    grad_proj_1, *sums_1, leave, later = mix_backward(
-        1, after(grad_gated_1, grad_low_0, layer_parts), saved_1, leave, later
-    )
-    grad_mid_seq_0 = to_sequence(0, gather_last(after(first_0, grad_proj_1)))
+    grad_gated_1, grad_low_0, layer_parts = lax.optimization_barrier((grad_gated_1, grad_low_0, layer_parts))
+    grad_proj_1, *sums_1, leave, later = mix_backward(1, grad_gated_1, saved_1, leave, later)
+    grad_proj_1, first_0 = lax.optimization_barrier((grad_proj_1, gather_first(grad_low_0)))
+    grad_mid_seq_0 = to_sequence(orders[0], gather_last(first_0))
     grad_gated_0 = product(grad_mid_seq_0, out_all)
-    grad_out_w = product(grad_mid_seq_0, saved_0[0], 0, 0) + product(grad_mid_seq_1, saved_1[0], 0, 0)
-    normed_kept_1, normed_sent_1 = scatter_first(from_sequence(1, product(grad_proj_1, mix_all, 1, 1, bf16)))
+    grad_gated_0, layer_parts = lax.optimization_barrier((grad_gated_0, layer_parts))
+    grad_proj_0, *sums_0, leave, later = mix_backward(0, grad_gated_0, saved_0, leave, later)
     layer_sums = [scatter_last(*x) for x in layer_parts]
-    layer_rows = [(m + x).astype(bf16) for m, x in zip((middle_0, middle_1), layer_sums)]
-    grad_out_w = grad_out_w.astype(bf16)
-    grad_gated_0, normed_kept_1, normed_sent_1, layer_rows, grad_out_w, grad_ffn = lax.optimization_barrier(
-        (grad_gated_0, normed_kept_1, normed_sent_1, layer_rows, grad_out_w, grad_ffn)
-    )
-    layer_back = send_back(jnp.concatenate(layer_rows, axis=0))
-    grad_proj_0, *sums_0, leave, later = mix_backward(0, grad_gated_0, saved_0, leave, later)
-    grad_proj_0, layer_back = lax.optimization_barrier((grad_proj_0, layer_back))
+    grad_proj_0, grad_ffn, layer_sums = lax.optimization_barrier((grad_proj_0, grad_ffn, layer_sums))
     grad_taps, grad_gain_out, grad_decay = [a + b for a, b in zip(sums_0, sums_1)]
     grad_conv = jnp.sum(grad_taps.reshape(taps, 8, heads, conv_width), axis=1)
     grad_conv = jnp.transpose(grad_conv, (2, 1, 0)).reshape(-1, taps)
     grad_mix = product(seq_0, grad_proj_0, 0, 0) + product(seq_1, grad_proj_1, 0, 0)
     grad_mix = (grad_mix + jnp.pad(grad_conv, ((0, 0), (conv_at, spare)))).astype(bf16)
-    grad_mix = jnp.concatenate([grad_mix, grad_out_w], axis=1)
-    normed_terms_0 = from_sequence(0, product(after(grad_proj_0, grad_mix), mix_all, 1, 1, bf16))
-    grad_mix = narrow(grad_mix)
-    normed_sum_1 = scatter_last(normed_kept_1, normed_sent_1)
-    grad_normed = jnp.concatenate([scatter_last(*scatter_first(normed_terms_0)), normed_sum_1], axis=0)
+    grad_out_w = product(grad_mid_seq_0, saved_0[0], 0, 0) + product(grad_mid_seq_1, saved_1[0], 0, 0)
+    grad_mix = jnp.concatenate([grad_mix, grad_out_w.astype(bf16)], axis=1)
+    layer_rows = jnp.concatenate([m + x for m, x in zip((middle_0, middle_1), layer_sums)], axis=0)
+    layer_back = across(from_part(layer_rows.astype(bf16)))
+    grad_mix, layer_back, grad_ffn = lax.optimization_barrier((grad_mix, layer_back, exchange_roles(grad_ffn)))
+    proj_parts = after((grad_proj_0, grad_proj_1), grad_mix)
+    normed_terms = [from_sequence(orders[r], product(proj_parts[r], mix_all, 1, 1, bf16)) for r in runs]
+    grad_mix = exchange_roles(narrow(grad_mix)).astype(f32)
+    grad_ffn = grad_ffn.astype(f32)
+    normed_terms = [x.reshape(splits, own_rows, model_width) for x in normed_terms]
+    normed_terms = jnp.concatenate(normed_terms, axis=1).reshape(group_rows, model_width)
+    grad_normed = scatter_last(*scatter_first(normed_terms))
     grad_input_norm, grad_gain_attn = norm_back(input_f32, input_scale, gain_attn, grad_normed)
     grad_middle = jnp.concatenate([grad_middle_0, grad_middle_1], axis=0)
-    input_grad = unpack(send_back((grad_middle + grad_input_norm).astype(bf16)))
+    input_grad = unpack(across(from_part((grad_middle + grad_input_norm).astype(bf16))))
     layer_out = unpack(layer_back)
 
     head_total = decay_log.shape[0]

time: 728 us -> 693 us (0.952)
  Pallas kernels: 126 us -> 114 us
  starting transfers between devices: 69.7 us -> 58.3 us
  other arithmetic: 51.2 us -> 41.6 us
  local copies, waits for them, and re-layouts: 48.5 us -> 39 us
    reduce_scatter x2, waiting for transfers between devices: 28.7 us -> 0.34 us  [narrow(): lax.psum_scatter(columns.astype(bf16), ('hi', 'tensor'), scatter_dimensio...]
    ppermute x6 -> x5, waiting for transfers between devices: 82.4 us -> 110 us  [exchange_roles(): lax.ppermute(x, ('lo', 'tensor'), [(a * n + b, b * n + a) for a in range(...]
    dot_general x28, matrix products: 116 us -> 127 us  [product(): lax.dot_general(a, b, (((ca,), (cb,)), ((), ())), preferred_element_type=...]
    ppermute x39 -> x34, waiting for transfers between devices: 124 us -> 132 us  [swap(): return lax.ppermute(x, axis, [(i, i ^ bit) for i in range(size)])]
    ppermute x6 -> x5, starting transfers between devices: 22.7 us -> 17.7 us  [exchange_roles(): lax.ppermute(x, ('lo', 'tensor'), [(a * n + b, b * n + a) for a in range(...]
    ppermute x39 -> x34, starting transfers between devices: 28.1 us -> 25.8 us  [swap(): return lax.ppermute(x, axis, [(i, i ^ bit) for i in range(size)])]
  transfers between devices with their start and end apart: 53 -> 47, of which waited for: 23 -> 23; matrix products, arithmetic and copies ran while one was open for 28% -> 27% of each run, Pallas kernels for 18% -> 17%
where the time goes in v3:
time: 693 us; the launch traced here: 684 us
  waiting for transfers between devices  274 us (40%)
  matrix products  142 us (20%)
  Pallas kernels  114 us (16%)
  starting transfers between devices  58.3 us (8%)
  other arithmetic  41.6 us (6%)
  local copies, waits for them, and re-layouts  39 us (6%)
  between operations  15.7 us (2%)
    ppermute x34, waiting for transfers between devices, swap(): return lax.ppermute(x, axis, [(i, i ^ bit) for i in range(size)])  132 us
    dot_general x28, matrix products, product(): lax.dot_general(a, b, (((ca,), (cb,)), ((), ())), preferred_element_type=...  127 us
    ppermute x5, waiting for transfers between devices, exchange_roles(): lax.ppermute(x, ('lo', 'tensor'), [(a * n + b, b * n + a) for a in range(...  110 us
    pallas_call x2, Pallas kernels, mixer_backward(): pl.pallas_call(kernel, grid_spec=pltpu.PrefetchScalarGridSpec(num_scalar_...  68.6 us
    pallas_call x2, Pallas kernels, mixer_forward(): pl.pallas_call(kernel, grid_spec=pltpu.PrefetchScalarGridSpec(num_scalar_...  45 us
    all_to_all x4, waiting for transfers between devices, across(): return lax.all_to_all(rows, spread, split_axis=0, concat_axis=0, tiled=True)  30.8 us
    ppermute x34, starting transfers between devices, swap(): return lax.ppermute(x, axis, [(i, i ^ bit) for i in range(size)])  25.8 us
    ppermute x5, starting transfers between devices, exchange_roles(): lax.ppermute(x, ('lo', 'tensor'), [(a * n + b, b * n + a) for a in range(...  17.7 us
  transfers between devices with their start and end apart: 47, of which 23 were waited for; matrix products, arithmetic and copies ran while one was open for 27% of the time, Pallas kernels for 17%

profile of v3, /device:TPU:2, one launch (start us, length us, event | category | flops | bytes accessed | tf_op | source)
XLA Modules:
  0.0 683.5 jit_solution(15060371152800677688)
XLA Ops:
  15.4 26.2 %collective-permute-done.3 = bf16[128,2176]{1,0:T(8,128)(2,1)S(1)} collective-permute-done((bf16[128,2176]{1,0:T(8,128)(2,1)S(1)}, bf16[128,2176]{1,0:T(8,128)(2,1)S(1)}, u32[]{:S(2)}, u32[]{:S(2)}) %collective-permute-start.3) | collective-permute-done | bytes 557088 | tf_op jit(solution)/shard_map/ppermute | solution.py:529
  54.1 39.0 %collective-permute-done = s32[1,3]{1,0:T(1,128)S(1)} collective-permute-done((s32[1,3]{1,0:T(1,128)S(1)}, s32[1,3]{1,0:T(1,128)S(1)}, u32[]{:S(2)}, u32[]{:S(2)}) %collective-permute-start) | collective-permute-done | bytes 44 | tf_op jit(solution)/shard_map/ppermute | solution.py:529
  97.4 14.9 %collective-permute-done.1 = bf16[256,1152]{1,0:T(8,128)(2,1)S(1)} collective-permute-done((bf16[256,1152]{1,0:T(8,128)(2,1)S(1)}, bf16[256,1152]{1,0:T(8,128)(2,1)S(1)}, u32[]{:S(2)}, u32[]{:S(2)}) %collective-permute-start.1) | collective-permute-done | bytes 589856 | tf_op jit(solution)/shard_map/ppermute | solution.py:524
  127.6 30.8 %all-to-all-done.1 = bf16[8,64,1024]{2,1,0:T(8,128)(2,1)S(1)} async-done(((bf16[8,64,1024]{2,1,0:T(8,128)(2,1)}), bf16[8,64,1024]{2,1,0:T(8,128)(2,1)S(1)}, u32[]{:S(2)}, u32[]{:S(2)}) %all-to-all-start.1) | async-done | bytes 1048608 | tf_op jit(solution)/shard_map/all_to_all | solution.py:640
  158.5 9.3 %fusion.8.proj_ref.before_ref.halo_ref = f32[1024,1664]{1,0:T(8,128)} fusion(bf16[1024,1024]{1,0:T(8,128)(2,1)} %bitcast.225, bf16[1024,2176]{1,0:T(8,128)(2,1)} %all-gather.3.cloned.1.call-done), kind=kOutput, calls=%fused_computation.29 | convolution fusion | flops 3489660928 | bytes 12320768 | tf_op jit(solution)/shard_map/dot_general | solution.py:598
  175.4 22.6 %mixer_forward.2 = (bf16[1024,512]{1,0:T(8,128)(2,1)}, f32[1024,512]{1,0:T(8,128)}, f32[1024,512]{1,0:T(8,128)}, f32[8,2,128,256]{3,2,1,0:T(8,128)}, f32[8,2,128...) custom-call(s32[3]{0:T(128)} %select_reduce_fusion.ends_ref, ...), custom_call_target="tpu_custom_call" | custom-call | flops 2048000000 | bytes 18432000 | tf_op jit(solution)/shard_map/mixer_forward/pallas_call | solution.py:392
  205.8 4.9 collective-permute-start.8
  215.9 6.2 fusion.6.proj_ref.halo_ref
  223.6 10.4 %collective-permute-done.8 = bf16[512,1024]{1,0:T(8,128)(2,1)S(1)} collective-permute-done((bf16[512,1024]{1,0:T(8,128)(2,1)S(1)}, bf16[512,1024]{1,0:T(8,128)(2,1)S(1)}, u32[]{:S(2)}, u32[]{:S(2)}) %collective-permute-start.8) | collective-permute-done | bytes 1048608 | tf_op jit(solution)/shard_map/ppermute | solution.py:524
  235.8 22.4 %mixer_forward.3 = (bf16[1024,512]{1,0:T(8,128)(2,1)}, f32[1024,512]{1,0:T(8,128)}, f32[1024,512]{1,0:T(8,128)}, f32[8,2,128,256]{3,2,1,0:T(8,128)}, f32[8,2,128...) custom-call(s32[3]{0:T(128)} %select_reduce_fusion.ends_ref, ...), custom_call_target="tpu_custom_call" | custom-call | flops 2048000000 | bytes 18432000 | tf_op jit(solution)/shard_map/mixer_forward/pallas_call | solution.py:392
  266.5 12.7 %collective-permute-done.11 = bf16[256,1024]{1,0:T(8,128)(2,1)S(1)} collective-permute-done((bf16[256,1024]{1,0:T(8,128)(2,1)S(1)}, bf16[256,1024]{1,0:T(8,128)(2,1)S(1)}, u32[]{:S(2)}, u32[]{:S(2)}) %collective-permute-start.11) | collective-permute-done | bytes 524320 | tf_op jit(solution)/shard_map/ppermute | solution.py:524
  285.9 4.9 fusion.38
  290.9 6.3 multiply_convert_fusion.5
  301.4 7.9 %collective-permute-done.12 = f32[256,1024]{1,0:T(8,128)S(1)} collective-permute-done((f32[256,1024]{1,0:T(8,128)S(1)}, f32[256,1024]{1,0:T(8,128)S(1)}, u32[]{:S(2)}, u32[]{:S(2)}) %collective-permute-start.12) | collective-permute-done | bytes 1048608 | tf_op jit(solution)/shard_map/ppermute | solution.py:524
  310.2 12.7 %collective-permute-done.17 = bf16[256,1024]{1,0:T(8,128)(2,1)S(1)} collective-permute-done((bf16[256,1024]{1,0:T(8,128)(2,1)S(1)}, bf16[256,1024]{1,0:T(8,128)(2,1)S(1)}, u32[]{:S(2)}, u32[]{:S(2)}) %collective-permute-start.17) | collective-permute-done | bytes 524320 | tf_op jit(solution)/shard_map/ppermute | solution.py:524
  326.3 5.0 fusion.35
  331.3 6.3 multiply_convert_fusion.3
  345.7 5.3 fusion.104
  351.0 5.8 convolution_add_fusion
  391.7 34.2 %mixer_backward.2 = (bf16[1024,1664]{1,0:T(8,128)(2,1)}, f32[32,1024]{1,0:T(8,128)}, f32[8,256]{1,0:T(8,128)}, f32[16,128]{1,0:T(8,128)}, f32[2,128,256]{2,1,0:T(8,128)}, /*index=5*/f32[8,1024]{1,0:T(8,128)}) custom-call(s32[3]{0:T(128)} %select_reduce_fusion.ends_ref, f32[1024,1664]{1,0:T(8,128)} %fusion.6.proj_ref.halo_ref, ...), custom_call_target="tpu_custom_call" | custom-call | flops 2048000000 | bytes 18432000 | tf_op jit(solution)/shard_map/mixer_backward/pallas_call | solution.py:453
  437.1 34.4 %mixer_backward.3 = (bf16[1024,1664]{1,0:T(8,128)(2,1)}, f32[32,1024]{1,0:T(8,128)}, f32[8,256]{1,0:T(8,128)}, f32[16,128]{1,0:T(8,128)}, f32[2,128,256]{2,1,0:T(8,128)}, /*index=5*/f32[8,1024]{1,0:T(8,128)}) custom-call(s32[3]{0:T(128)} %select_reduce_fusion.ends_ref, f32[1024,1664]{1,0:T(8,128)} %fusion.8.proj_ref.before_ref.halo_ref, ...), custom_call_target="tpu_custom_call" | custom-call | flops 2048000000 | bytes 18432000 | tf_op jit(solution)/shard_map/mixer_backward/pallas_call | solution.py:453
  480.7 6.4 collective-permute-done.29
  494.7 9.4 %fusion.105 = f32[1024,1664]{1,0:T(8,128)} fusion(bf16[1024,1024]{1,0:T(8,128)(2,1)} %bitcast.226, bf16[1024,1664]{1,0:T(8,128)(2,1)} %get-tuple-element.190), kind=kOutput, calls=%fused_computation.245 | convolution fusion | flops 3489660928 | bytes 12320768 | tf_op jit(solution)/shard_map/dot_general | solution.py:598
  504.4 5.3 collective-permute-start.30
  509.8 8.7 %add_convert_fusion = bf16[1024,1664]{1,0:T(8,128)(2,1)S(1)} fusion(f32[1024,4]{1,0:T(8,128)S(1)} %bitcast.196, f32[1024,1664]{1,0:T(8,128)} %fusion.105, bf16[1024,1024]{1,0:T(8,128)(2,1)} %bitcast.228, bf16[1024,1664]{1,0:T(8,128)(2,1)} %get-tuple-element.191), kind=kOutput, calls=%fused_computation.2 | convolution fusion | flops 3494772736 | bytes 15745024 | tf_op jit(solution)/shard_map/dot_general | solution.py:598
  520.9 22.1 %collective-permute-done.30 = bf16[128,2112]{0,1:T(8,128)(2,1)S(1)} collective-permute-done((bf16[128,2112]{0,1:T(8,128)(2,1)S(1)}, bf16[128,2112]{0,1:T(8,128)(2,1)S(1)}, u32[]{:S(2)}, u32[]{:S(2)}) %collective-permute-start.30) | collective-permute-done | bytes 540704 | tf_op jit(solution)/shard_map/ppermute | solution.py:529
  543.1 7.0 %fusion.28 = bf16[1024,1024]{1,0:T(8,128)(2,1)S(1)} fusion(bf16[1024,1664]{1,0:T(8,128)(2,1)} %get-tuple-element.190, bf16[1024,2176]{1,0:T(8,128)(2,1)} %all-gather.3.cloned.1.call-done), kind=kOutput, calls=%fused_computation.73 | convolution fusion | flops 3490709504 | bytes 8912896 | tf_op jit(solution)/shard_map/dot_general | solution.py:598
  553.3 6.4 fusion.31
  567.2 25.2 %collective-permute-done.32 = bf16[512,1024]{1,0:T(8,128)(2,1)S(1)} collective-permute-done((bf16[512,1024]{1,0:T(8,128)(2,1)S(1)}, bf16[512,1024]{1,0:T(8,128)(2,1)S(1)}, u32[]{:S(2)}, u32[]{:S(2)}) %collective-permute-start.32) | collective-permute-done | bytes 1048608 | tf_op jit(solution)/shard_map/ppermute | solution.py:524
  606.1 9.9 %collective-permute-done.36 = f32[8,384]{1,0:T(8,128)S(1)} collective-permute-done((f32[8,384]{1,0:T(8,128)S(1)}, f32[8,384]{1,0:T(8,128)S(1)}, u32[]{:S(2)}, u32[]{:S(2)}) %collective-permute-start.36) | collective-permute-done | bytes 12320 | tf_op jit(solution)/shard_map/ppermute | solution.py:524
  620.4 18.1 %collective-permute-done.37 = f32[8,384]{1,0:T(8,128)S(1)} collective-permute-done((f32[8,384]{1,0:T(8,128)S(1)}, f32[8,384]{1,0:T(8,128)S(1)}, u32[]{:S(2)}, u32[]{:S(2)}) %collective-permute-start.37) | collective-permute-done | bytes 12320 | tf_op jit(solution)/shard_map/ppermute | solution.py:524
  649.8 23.0 %collective-permute-done.33 = bf16[128,2176]{1,0:T(8,128)(2,1)S(1)} collective-permute-done((bf16[128,2176]{1,0:T(8,128)(2,1)}, bf16[128,2176]{1,0:T(8,128)(2,1)S(1)}, u32[]{:S(2)}, u32[]{:S(2)}) %collective-permute-start.33) | collective-permute-done | bytes 557088 | tf_op jit(solution)/shard_map/ppermute | solution.py:529
  (381 shorter events, 204.2 us)
Async XLA Ops:
  7.2 151.3 %all-gather.3.cloned.1.call-start = ((), (), s32[]{:S(2)}) async-start(), calls=%async_computation.6 | async-start | bytes 5013504 | tf_op jit(solution)/shard_map/all_gather | solution.py:590
  10.9 30.7 %collective-permute-start.3 = (bf16[128,2176]{1,0:T(8,128)(2,1)S(1)}, bf16[128,2176]{1,0:T(8,128)(2,1)S(1)}, u32[]{:S(2)}, u32[]{:S(2)}) collective-permute-start(bf16[128,2176]{1,0:T(8,128)(2,1)S(1)} %concatenate.99), channel_id=1, source_target_pairs={{0,0},{1,4},{2,8},{3,12},{4,1},{5,5},{6,9},{7,13},{8,2},{9,6},{10,... | collective-permute-start | bytes 1671176 | tf_op jit(solution)/shard_map/ppermute | solution.py:529
  44.9 48.8 %all-to-all-start = ((bf16[8,64,1152]{2,1,0:T(8,128)(2,1)}), bf16[8,64,1152]{2,1,0:T(8,128)(2,1)S(1)}, u32[]{:S(2)}, u32[]{:S(2)}) async-start(bf16[8,64,1152]{2,1,0:T(8,128)(2,1)} %bitcast), calls=%async_computation | async-start | bytes 2359296 | tf_op jit(solution)/shard_map/all_to_all | solution.py:640
  48.6 44.5 %collective-permute-start = (s32[1,3]{1,0:T(1,128)S(1)}, s32[1,3]{1,0:T(1,128)S(1)}, u32[]{:S(2)}, u32[]{:S(2)}) collective-permute-start(s32[1,3]{1,0:T(1,128)S(1)} %copy-done.47), channel_id=1, source_target_pairs={{0,0},{1,4},{2,8},{3,12},{4,1},{5,5},{6,9},{7,13},{8,2},{9,6},{10,... | collective-permute-start | bytes 44 | tf_op jit(solution)/shard_map/ppermute | solution.py:529
  96.6 15.7 %collective-permute-start.1 = (bf16[256,1152]{1,0:T(8,128)(2,1)S(1)}, bf16[256,1152]{1,0:T(8,128)(2,1)S(1)}, u32[]{:S(2)}, u32[]{:S(2)}) collective-permute-start(bf16[256,1152]{1,0:T(8,128)(2,1)S(1)} %get-tuple-element.289), channel_id=1, source_target_pairs={{0,8},{4,12},{8,0},{12,4},{1,9},{5,13},{9,1},{13,5},{2,10},{6,14},... | collective-permute-start | bytes 1769480 | tf_op jit(solution)/shard_map/ppermute | solution.py:524
  115.1 43.3 %all-to-all-start.1 = ((bf16[8,64,1024]{2,1,0:T(8,128)(2,1)}), bf16[8,64,1024]{2,1,0:T(8,128)(2,1)S(1)}, u32[]{:S(2)}, u32[]{:S(2)}) async-start(bf16[8,64,1024]{2,1,0:T(8,128)(2,1)} %bitcast.185), calls=%async_computation.1 | async-start | bytes 2097152 | tf_op jit(solution)/shard_map/all_to_all | solution.py:640
  118.7 163.1 %all-gather.5.cloned.1.call-start = ((), (), s32[]{:S(2)}) async-start(), calls=%async_computation.7 | async-start | bytes 4866048 | tf_op jit(solution)/shard_map/all_gather | solution.py:590
  167.9 30.1 %collective-permute-start.4 = (bf16[256,1152]{1,0:T(8,128)(2,1)S(1)}, bf16[256,1152]{1,0:T(8,128)(2,1)}, u32[]{:S(2)}, u32[]{:S(2)}) collective-permute-start(bf16[256,1152]{1,0:T(8,128)(2,1)S(1)} %copy-done.14), channel_id=1, source_target_pairs={{0,8},{4,12},{8,0},{12,4},{1,9},{5,13},{9,1},{13,5},{2,10},{6,14},... | collective-permute-start | bytes 1769480 | tf_op jit(solution)/shard_map/ppermute | solution.py:524
  168.6 31.6 %collective-permute-start.5 = (bf16[128,2112]{0,1:T(8,128)(2,1)}, bf16[128,2112]{0,1:T(8,128)(2,1)}, u32[]{:S(2)}, u32[]{:S(2)}) collective-permute-start(bf16[128,2112]{0,1:T(8,128)(2,1)} %pad_maximum_fusion.26), channel_id=1, source_target_pairs={{0,0},{1,4},{2,8},{3,12},{4,1},{5,5},{6,9},{7,13},{8,2},{9,6},{10,... | collective-permute-start | bytes 1622024 | tf_op jit(solution)/shard_map/ppermute | solution.py:529
  200.2 288.0 %reduce-scatter.3.cloned.1.call-start = ((), (), s32[]{:S(2)}) async-start(), calls=%async_computation.8 | async-start | bytes 5013504 | tf_op jit(solution)/shard_map/reduce_scatter | solution.py:594
  205.2 16.9 %collective-permute-start.7 = (f32[512,1024]{1,0:T(8,128)S(1)}, f32[512,1024]{1,0:T(8,128)S(1)}, u32[]{:S(2)}, u32[]{:S(2)}) collective-permute-start(f32[512,1024]{1,0:T(8,128)S(1)} %slice.318), channel_id=1, source_target_pairs={{0,4},{4,0},{8,12},{12,8},{1,5},{5,1},{9,13},{13,9},{2,6},{6,2},{1... | collective-permute-start | bytes 6291464 | tf_op jit(solution)/shard_map/ppermute | solution.py:524
  205.8 28.3 %collective-permute-start.8 = (bf16[512,1024]{1,0:T(8,128)(2,1)S(1)}, bf16[512,1024]{1,0:T(8,128)(2,1)S(1)}, u32[]{:S(2)}, u32[]{:S(2)}) collective-permute-start(bf16[512,1024]{1,0:T(8,128)(2,1)S(1)} %bitcast.154), channel_id=1, source_target_pairs={{0,8},{4,12},{8,0},{12,4},{1,9},{5,13},{9,1},{13,5},{2,10},{6,14},... | collective-permute-start | bytes 3145736 | tf_op jit(solution)/shard_map/ppermute | solution.py:524
  234.0 29.2 %collective-permute-start.10 = (f32[256,1024]{1,0:T(8,128)}, f32[256,1024]{1,0:T(8,128)S(1)}, u32[]{:S(2)}, u32[]{:S(2)}) collective-permute-start(f32[256,1024]{1,0:T(8,128)} %get-tuple-element.125), channel_id=1, source_target_pairs={{0,8},{4,12},{8,0},{12,4},{1,9},{5,13},{9,1},{13,5},{2,10},{6,14},... | collective-permute-start | bytes 3145736 | tf_op jit(solution)/shard_map/ppermute | solution.py:524
  262.9 17.3 %collective-permute-start.9 = (f32[512,1024]{1,0:T(8,128)S(1)}, f32[512,1024]{1,0:T(8,128)S(1)}, u32[]{:S(2)}, u32[]{:S(2)}) collective-permute-start(f32[512,1024]{1,0:T(8,128)S(1)} %slice.323), channel_id=1, source_target_pairs={{0,4},{4,0},{8,12},{12,8},{1,5},{5,1},{9,13},{13,9},{2,6},{6,2},{1... | collective-permute-start | bytes 6291464 | tf_op jit(solution)/shard_map/ppermute | solution.py:524
  264.8 14.4 %collective-permute-start.11 = (bf16[256,1024]{1,0:T(8,128)(2,1)S(1)}, bf16[256,1024]{1,0:T(8,128)(2,1)S(1)}, u32[]{:S(2)}, u32[]{:S(2)}) collective-permute-start(bf16[256,1024]{1,0:T(8,128)(2,1)S(1)} %multiply_convert_fusion.8), channel_id=1, source_target_pairs={{0,8},{4,12},{8,0},{12,4},{1,9},{5,13},{9,1},{13,5},{2,10},{6,14},... | collective-permute-start | bytes 1572872 | tf_op jit(solution)/shard_map/ppermute | solution.py:524
  284.2 25.1 %collective-permute-start.12 = (f32[256,1024]{1,0:T(8,128)S(1)}, f32[256,1024]{1,0:T(8,128)S(1)}, u32[]{:S(2)}, u32[]{:S(2)}) collective-permute-start(f32[256,1024]{1,0:T(8,128)S(1)} %copy-done.21), channel_id=1, source_target_pairs={{0,8},{4,12},{8,0},{12,4},{1,9},{5,13},{9,1},{13,5},{2,10},{6,14},... | collective-permute-start | bytes 3145736 | tf_op jit(solution)/shard_map/ppermute | solution.py:524
  301.1 21.9 %collective-permute-start.16 = (bf16[512,1024]{1,0:T(8,128)(2,1)S(1)}, bf16[512,1024]{1,0:T(8,128)(2,1)S(1)}, u32[]{:S(2)}, u32[]{:S(2)}) collective-permute-start(bf16[512,1024]{1,0:T(8,128)(2,1)S(1)} %slice.332), channel_id=1, source_target_pairs={{0,4},{4,0},{8,12},{12,8},{1,5},{5,1},{9,13},{13,9},{2,6},{6,2},{1... | collective-permute-start | bytes 3145736 | tf_op jit(solution)/shard_map/ppermute | solution.py:524
  309.9 13.1 %collective-permute-start.17 = (bf16[256,1024]{1,0:T(8,128)(2,1)S(1)}, bf16[256,1024]{1,0:T(8,128)(2,1)S(1)}, u32[]{:S(2)}, u32[]{:S(2)}) collective-permute-start(bf16[256,1024]{1,0:T(8,128)(2,1)S(1)} %multiply_convert_fusion.7), channel_id=1, source_target_pairs={{0,8},{4,12},{8,0},{12,4},{1,9},{5,13},{9,1},{13,5},{2,10},{6,14},... | collective-permute-start | bytes 1572872 | tf_op jit(solution)/shard_map/ppermute | solution.py:524
  325.1 16.7 %collective-permute-start.20 = (bf16[256,1024]{1,0:T(8,128)(2,1)S(1)}, bf16[256,1024]{1,0:T(8,128)(2,1)S(1)}, u32[]{:S(2)}, u32[]{:S(2)}) collective-permute-start(bf16[256,1024]{1,0:T(8,128)(2,1)S(1)} %slice.473), channel_id=1, source_target_pairs={{0,8},{4,12},{8,0},{12,4},{1,9},{5,13},{9,1},{13,5},{2,10},{6,14},... | collective-permute-start | bytes 1572872 | tf_op jit(solution)/shard_map/ppermute | solution.py:524
  344.6 14.0 %collective-permute-start.21 = (bf16[256,1024]{1,0:T(8,128)(2,1)S(1)}, bf16[256,1024]{1,0:T(8,128)(2,1)S(1)}, u32[]{:S(2)}, u32[]{:S(2)}) collective-permute-start(bf16[256,1024]{1,0:T(8,128)(2,1)S(1)} %slice.472), channel_id=1, source_target_pairs={{0,8},{4,12},{8,0},{12,4},{1,9},{5,13},{9,1},{13,5},{2,10},{6,14},... | collective-permute-start | bytes 1572872 | tf_op jit(solution)/shard_map/ppermute | solution.py:524
  360.5 13.2 %collective-permute-start.22 = (bf16[256,1024]{1,0:T(8,128)(2,1)S(1)}, bf16[256,1024]{1,0:T(8,128)(2,1)S(1)}, u32[]{:S(2)}, u32[]{:S(2)}) collective-permute-start(bf16[256,1024]{1,0:T(8,128)(2,1)S(1)} %get-tuple-element.270), channel_id=1, source_target_pairs={{0,8},{4,12},{8,0},{12,4},{1,9},{5,13},{9,1},{13,5},{2,10},{6,14},... | collective-permute-start | bytes 1572872 | tf_op jit(solution)/shard_map/ppermute | solution.py:524
  389.9 36.0 %collective-permute-start.26 = (bf16[256,1024]{1,0:T(8,128)(2,1)S(1)}, bf16[256,1024]{1,0:T(8,128)(2,1)S(1)}, u32[]{:S(2)}, u32[]{:S(2)}) collective-permute-start(bf16[256,1024]{1,0:T(8,128)(2,1)S(1)} %copy-done.15), channel_id=1, source_target_pairs={{0,8},{4,12},{8,0},{12,4},{1,9},{5,13},{9,1},{13,5},{2,10},{6,14},... | collective-permute-start | bytes 1572872 | tf_op jit(solution)/shard_map/ppermute | solution.py:524
  436.2 43.3 %collective-permute-start.28 = (bf16[256,1024]{1,0:T(8,128)(2,1)}, bf16[256,1024]{1,0:T(8,128)(2,1)}, u32[]{:S(2)}, u32[]{:S(2)}) collective-permute-start(bf16[256,1024]{1,0:T(8,128)(2,1)} %slice.471), channel_id=1, source_target_pairs={{0,8},{4,12},{8,0},{12,4},{1,9},{5,13},{9,1},{13,5},{2,10},{6,14},... | collective-permute-start | bytes 1572872 | tf_op jit(solution)/shard_map/ppermute | solution.py:524
  473.5 13.6 %collective-permute-start.29 = (bf16[256,1024]{1,0:T(8,128)(2,1)}, bf16[256,1024]{1,0:T(8,128)(2,1)S(1)}, u32[]{:S(2)}, u32[]{:S(2)}) collective-permute-start(bf16[256,1024]{1,0:T(8,128)(2,1)} %slice.470), channel_id=1, source_target_pairs={{0,8},{4,12},{8,0},{12,4},{1,9},{5,13},{9,1},{13,5},{2,10},{6,14},... | collective-permute-start | bytes 1572872 | tf_op jit(solution)/shard_map/ppermute | solution.py:524
  490.9 52.1 %all-to-all-start.2 = ((bf16[8,64,1024]{2,1,0:T(8,128)(2,1)}), bf16[8,64,1024]{2,1,0:T(8,128)(2,1)S(1)}, u32[]{:S(2)}, u32[]{:S(2)}) async-start(bf16[8,64,1024]{2,1,0:T(8,128)(2,1)} %bitcast.61), calls=%async_computation.3 | async-start | bytes 2097152 | tf_op jit(solution)/shard_map/all_to_all | solution.py:640
  494.5 149.3 %reduce-scatter.5.cloned.1.call-start = ((), (), s32[]{:S(2)}) async-start(), calls=%async_computation.9 | async-start | bytes 5013504 | tf_op jit(solution)/shard_map/reduce_scatter | solution.py:594
  504.4 38.6 %collective-permute-start.30 = (bf16[128,2112]{0,1:T(8,128)(2,1)S(1)}, bf16[128,2112]{0,1:T(8,128)(2,1)S(1)}, u32[]{:S(2)}, u32[]{:S(2)}) collective-permute-start(bf16[128,2112]{0,1:T(8,128)(2,1)S(1)} %copy.187), channel_id=1, source_target_pairs={{0,0},{1,4},{2,8},{3,12},{4,1},{5,5},{6,9},{7,13},{8,2},{9,6},{10,... | collective-permute-start | bytes 1622024 | tf_op jit(solution)/shard_map/ppermute | solution.py:529
  567.1 25.3 %collective-permute-start.32 = (bf16[512,1024]{1,0:T(8,128)(2,1)S(1)}, bf16[512,1024]{1,0:T(8,128)(2,1)S(1)}, u32[]{:S(2)}, u32[]{:S(2)}) collective-permute-start(bf16[512,1024]{1,0:T(8,128)(2,1)S(1)} %slice.469), channel_id=1, source_target_pairs={{0,8},{4,12},{8,0},{12,4},{1,9},{5,13},{9,1},{13,5},{2,10},{6,14},... | collective-permute-start | bytes 3145736 | tf_op jit(solution)/shard_map/ppermute | solution.py:524
  595.2 52.8 %all-to-all-start.3 = ((bf16[8,64,1024]{2,1,0:T(8,128)(2,1)}), bf16[8,64,1024]{2,1,0:T(8,128)(2,1)S(1)}, u32[]{:S(2)}, u32[]{:S(2)}) async-start(bf16[8,64,1024]{2,1,0:T(8,128)(2,1)} %bitcast.75), calls=%async_computation.4 | async-start | bytes 2097152 | tf_op jit(solution)/shard_map/all_to_all | solution.py:640
  604.2 11.8 %collective-permute-start.36 = (f32[8,384]{1,0:T(8,128)S(1)}, f32[8,384]{1,0:T(8,128)S(1)}, u32[]{:S(2)}, u32[]{:S(2)}) collective-permute-start(f32[8,384]{1,0:T(8,128)S(1)} %add.314), channel_id=1, source_target_pairs={{0,1},{1,0},{2,3},{3,2},{4,5},{5,4},{6,7},{7,6},{8,9},{9,8},{10,11... | collective-permute-start | bytes 36872 | tf_op jit(solution)/shard_map/ppermute | solution.py:524
  616.0 22.5 %collective-permute-start.37 = (f32[8,384]{1,0:T(8,128)S(1)}, f32[8,384]{1,0:T(8,128)S(1)}, u32[]{:S(2)}, u32[]{:S(2)}) collective-permute-start(f32[8,384]{1,0:T(8,128)S(1)} %add.315), channel_id=1, source_target_pairs={{0,2},{1,3},{2,0},{3,1},{4,6},{5,7},{6,4},{7,5},{8,10},{9,11},{10,... | collective-permute-start | bytes 36872 | tf_op jit(solution)/shard_map/ppermute | solution.py:524
  643.8 29.0 %collective-permute-start.33 = (bf16[128,2176]{1,0:T(8,128)(2,1)}, bf16[128,2176]{1,0:T(8,128)(2,1)S(1)}, u32[]{:S(2)}, u32[]{:S(2)}) collective-permute-start(bf16[128,2176]{1,0:T(8,128)(2,1)} %reduce-scatter.5.cloned.1.call-done), channel_id=1, source_target_pairs={{0,0},{1,4},{2,8},{3,12},{4,1},{5,5},{6,9},{7,13},{8,2},{9,6},{10,... | collective-permute-start | bytes 1671176 | tf_op jit(solution)/shard_map/ppermute | solution.py:529
  (71 other events, 988.4 us)
Sparse Core Ops, SparseCore 0:
  42.6 112.7 all-gather.2
  200.4 77.3 all-gather.4
  376.3 88.8 reduce-scatter.2
  543.2 100.5 reduce-scatter.4

commit v4 on v3

--- a/solution.py
+++ b/solution.py
@@ -833,13 +833,15 @@
     grad_gated_1 = product(grad_mid_seq_1, out_all)
     grad_gated_1, grad_low_0, layer_parts = lax.optimization_barrier((grad_gated_1, grad_low_0, layer_parts))
     grad_proj_1, *sums_1, leave, later = mix_backward(1, grad_gated_1, saved_1, leave, later)
-    grad_proj_1, first_0 = lax.optimization_barrier((grad_proj_1, gather_first(grad_low_0)))
+    layer_sums = [scatter_last(*x) for x in layer_parts]
+    grad_proj_1, first_0, layer_sums = lax.optimization_barrier((grad_proj_1, gather_first(grad_low_0), layer_sums))
     grad_mid_seq_0 = to_sequence(orders[0], gather_last(first_0))
     grad_gated_0 = product(grad_mid_seq_0, out_all)
-    grad_gated_0, layer_parts = lax.optimization_barrier((grad_gated_0, layer_parts))
+    layer_rows = jnp.concatenate([m + x for m, x in zip((middle_0, middle_1), layer_sums)], axis=0)
+    layer_rows = from_part(layer_rows.astype(bf16))
+    grad_gated_0, layer_rows = lax.optimization_barrier((grad_gated_0, layer_rows))
     grad_proj_0, *sums_0, leave, later = mix_backward(0, grad_gated_0, saved_0, leave, later)
-    layer_sums = [scatter_last(*x) for x in layer_parts]
-    grad_proj_0, grad_ffn, layer_sums = lax.optimization_barrier((grad_proj_0, grad_ffn, layer_sums))
+    grad_proj_0, grad_ffn, layer_back = lax.optimization_barrier((grad_proj_0, grad_ffn, across(layer_rows)))
     grad_taps, grad_gain_out, grad_decay = [a + b for a, b in zip(sums_0, sums_1)]
     grad_conv = jnp.sum(grad_taps.reshape(taps, 8, heads, conv_width), axis=1)
     grad_conv = jnp.transpose(grad_conv, (2, 1, 0)).reshape(-1, taps)
@@ -847,16 +849,14 @@
     grad_mix = (grad_mix + jnp.pad(grad_conv, ((0, 0), (conv_at, spare)))).astype(bf16)
     grad_out_w = product(grad_mid_seq_0, saved_0[0], 0, 0) + product(grad_mid_seq_1, saved_1[0], 0, 0)
     grad_mix = jnp.concatenate([grad_mix, grad_out_w.astype(bf16)], axis=1)
-    layer_rows = jnp.concatenate([m + x for m, x in zip((middle_0, middle_1), layer_sums)], axis=0)
-    layer_back = across(from_part(layer_rows.astype(bf16)))
-    grad_mix, layer_back, grad_ffn = lax.optimization_barrier((grad_mix, layer_back, exchange_roles(grad_ffn)))
-    proj_parts = after((grad_proj_0, grad_proj_1), grad_mix)
+    grad_mix, *proj_parts = lax.optimization_barrier((grad_mix, grad_proj_0, grad_proj_1))
     normed_terms = [from_sequence(orders[r], product(proj_parts[r], mix_all, 1, 1, bf16)) for r in runs]
     grad_mix = exchange_roles(narrow(grad_mix)).astype(f32)
-    grad_ffn = grad_ffn.astype(f32)
     normed_terms = [x.reshape(splits, own_rows, model_width) for x in normed_terms]
     normed_terms = jnp.concatenate(normed_terms, axis=1).reshape(group_rows, model_width)
     grad_normed = scatter_last(*scatter_first(normed_terms))
+    grad_normed, grad_ffn = lax.optimization_barrier((grad_normed, exchange_roles(grad_ffn)))
+    grad_ffn = grad_ffn.astype(f32)
     grad_input_norm, grad_gain_attn = norm_back(input_f32, input_scale, gain_attn, grad_normed)
     grad_middle = jnp.concatenate([grad_middle_0, grad_middle_1], axis=0)
     input_grad = unpack(across(from_part((grad_middle + grad_input_norm).astype(bf16))))

time: 693 us -> 677 us (0.977)
  waiting for transfers between devices: 274 us -> 260 us
  matrix products: 142 us -> 135 us
    ppermute x34, waiting for transfers between devices: 132 us -> 115 us  [swap(): return lax.ppermute(x, axis, [(i, i ^ bit) for i in range(size)])]
    reduce_scatter x2, waiting for transfers between devices: 0.34 us -> 16 us  [narrow(): lax.psum_scatter(columns.astype(bf16), ('hi', 'tensor'), scatter_dimensio...]
    ppermute x5, waiting for transfers between devices: 110 us -> 96.8 us  [exchange_roles(): lax.ppermute(x, ('lo', 'tensor'), [(a * n + b, b * n + a) for a in range(...]
    unnamed x110 -> x118, local copies, waits for them, and re-layouts: 13.1 us -> 15.7 us
  transfers between devices with their start and end apart: 47 -> 47, of which waited for: 23 -> 26; matrix products, arithmetic and copies ran while one was open for 27% -> 25% of each run, Pallas kernels for 17% -> 17%
where the time goes in v4:
time: 677 us; the launch traced here: 668 us
  waiting for transfers between devices  260 us (38%)
  matrix products  135 us (20%)
  Pallas kernels  113 us (17%)
  starting transfers between devices  60.9 us (9%)
  local copies, waits for them, and re-layouts  42.5 us (6%)
  other arithmetic  40.1 us (6%)
  between operations  15.8 us (2%)
    dot_general x28, matrix products, product(): lax.dot_general(a, b, (((ca,), (cb,)), ((), ())), preferred_element_type=...  121 us
    ppermute x34, waiting for transfers between devices, swap(): return lax.ppermute(x, axis, [(i, i ^ bit) for i in range(size)])  115 us
    ppermute x5, waiting for transfers between devices, exchange_roles(): lax.ppermute(x, ('lo', 'tensor'), [(a * n + b, b * n + a) for a in range(...  96.8 us
    pallas_call x2, Pallas kernels, mixer_backward(): pl.pallas_call(kernel, grid_spec=pltpu.PrefetchScalarGridSpec(num_scalar_...  68.5 us
    pallas_call x2, Pallas kernels, mixer_forward(): pl.pallas_call(kernel, grid_spec=pltpu.PrefetchScalarGridSpec(num_scalar_...  44.9 us
    all_to_all x4, waiting for transfers between devices, across(): return lax.all_to_all(rows, spread, split_axis=0, concat_axis=0, tiled=True)  31.2 us
    ppermute x34, starting transfers between devices, swap(): return lax.ppermute(x, axis, [(i, i ^ bit) for i in range(size)])  25.9 us
    ppermute x5, starting transfers between devices, exchange_roles(): lax.ppermute(x, ('lo', 'tensor'), [(a * n + b, b * n + a) for a in range(...  18.7 us
  transfers between devices with their start and end apart: 47, of which 26 were waited for; matrix products, arithmetic and copies ran while one was open for 25% of the time, Pallas kernels for 17%

profile of v4, /device:TPU:2, one launch (start us, length us, event | category | flops | bytes accessed | tf_op | source)
XLA Modules:
  0.0 667.6 jit_solution(4319182185634249902)
XLA Ops:
  15.4 26.2 %collective-permute-done.3 = bf16[128,2176]{1,0:T(8,128)(2,1)S(1)} collective-permute-done((bf16[128,2176]{1,0:T(8,128)(2,1)S(1)}, bf16[128,2176]{1,0:T(8,128)(2,1)S(1)}, u32[]{:S(2)}, u32[]{:S(2)}) %collective-permute-start.3) | collective-permute-done | bytes 557088 | tf_op jit(solution)/shard_map/ppermute | solution.py:529
  54.1 39.0 %collective-permute-done = s32[1,3]{1,0:T(1,128)S(1)} collective-permute-done((s32[1,3]{1,0:T(1,128)S(1)}, s32[1,3]{1,0:T(1,128)S(1)}, u32[]{:S(2)}, u32[]{:S(2)}) %collective-permute-start) | collective-permute-done | bytes 44 | tf_op jit(solution)/shard_map/ppermute | solution.py:529
  97.4 14.9 %collective-permute-done.1 = bf16[256,1152]{1,0:T(8,128)(2,1)S(1)} collective-permute-done((bf16[256,1152]{1,0:T(8,128)(2,1)S(1)}, bf16[256,1152]{1,0:T(8,128)(2,1)S(1)}, u32[]{:S(2)}, u32[]{:S(2)}) %collective-permute-start.1) | collective-permute-done | bytes 589856 | tf_op jit(solution)/shard_map/ppermute | solution.py:524
  128.3 30.6 %all-to-all-done.1 = bf16[8,64,1024]{2,1,0:T(8,128)(2,1)} async-done(((bf16[8,64,1024]{2,1,0:T(8,128)(2,1)}), bf16[8,64,1024]{2,1,0:T(8,128)(2,1)}, u32[]{:S(2)}, u32[]{:S(2)}) %all-to-all-start.1) | async-done | bytes 1048608 | tf_op jit(solution)/shard_map/all_to_all | solution.py:640
  160.2 9.5 %fusion.8.proj_ref.before_ref.halo_ref = f32[1024,1664]{1,0:T(8,128)} fusion(bf16[1024,1024]{1,0:T(8,128)(2,1)} %bitcast.225, bf16[1024,2176]{1,0:T(8,128)(2,1)} %all-gather.3.cloned.1.call-done), kind=kOutput, calls=%fused_computation.29 | convolution fusion | flops 3489660928 | bytes 12320768 | tf_op jit(solution)/shard_map/dot_general | solution.py:598
  177.3 22.5 %mixer_forward.2 = (bf16[1024,512]{1,0:T(8,128)(2,1)}, f32[1024,512]{1,0:T(8,128)}, f32[1024,512]{1,0:T(8,128)}, f32[8,2,128,256]{3,2,1,0:T(8,128)}, f32[8,2,128...) custom-call(s32[3]{0:T(128)} %select_reduce_fusion.ends_ref, ...), custom_call_target="tpu_custom_call" | custom-call | flops 2048000000 | bytes 18432000 | tf_op jit(solution)/shard_map/mixer_forward/pallas_call | solution.py:392
  207.5 4.9 collective-permute-start.8
  217.6 6.1 fusion.6.proj_ref.halo_ref
  224.3 11.5 %collective-permute-done.8 = bf16[512,1024]{1,0:T(8,128)(2,1)S(1)} collective-permute-done((bf16[512,1024]{1,0:T(8,128)(2,1)S(1)}, bf16[512,1024]{1,0:T(8,128)(2,1)S(1)}, u32[]{:S(2)}, u32[]{:S(2)}) %collective-permute-start.8) | collective-permute-done | bytes 1048608 | tf_op jit(solution)/shard_map/ppermute | solution.py:524
  238.4 22.5 %mixer_forward.3 = (bf16[1024,512]{1,0:T(8,128)(2,1)}, f32[1024,512]{1,0:T(8,128)}, f32[1024,512]{1,0:T(8,128)}, f32[8,2,128,256]{3,2,1,0:T(8,128)}, f32[8,2,128...) custom-call(s32[3]{0:T(128)} %select_reduce_fusion.ends_ref, ...), custom_call_target="tpu_custom_call" | custom-call | flops 2048000000 | bytes 18432000 | tf_op jit(solution)/shard_map/mixer_forward/pallas_call | solution.py:392
  269.1 12.7 %collective-permute-done.11 = bf16[256,1024]{1,0:T(8,128)(2,1)S(1)} collective-permute-done((bf16[256,1024]{1,0:T(8,128)(2,1)S(1)}, bf16[256,1024]{1,0:T(8,128)(2,1)S(1)}, u32[]{:S(2)}, u32[]{:S(2)}) %collective-permute-start.11) | collective-permute-done | bytes 524320 | tf_op jit(solution)/shard_map/ppermute | solution.py:524
  288.7 5.0 fusion.38
  293.7 6.3 multiply_convert_fusion.5
  304.1 8.1 %collective-permute-done.12 = f32[256,1024]{1,0:T(8,128)S(1)} collective-permute-done((f32[256,1024]{1,0:T(8,128)S(1)}, f32[256,1024]{1,0:T(8,128)S(1)}, u32[]{:S(2)}, u32[]{:S(2)}) %collective-permute-start.12) | collective-permute-done | bytes 1048608 | tf_op jit(solution)/shard_map/ppermute | solution.py:524
  313.0 12.7 %collective-permute-done.17 = bf16[256,1024]{1,0:T(8,128)(2,1)S(1)} collective-permute-done((bf16[256,1024]{1,0:T(8,128)(2,1)S(1)}, bf16[256,1024]{1,0:T(8,128)(2,1)S(1)}, u32[]{:S(2)}, u32[]{:S(2)}) %collective-permute-start.17) | collective-permute-done | bytes 524320 | tf_op jit(solution)/shard_map/ppermute | solution.py:524
  329.1 5.1 fusion.35
  334.3 6.3 multiply_convert_fusion.3
  348.7 5.3 fusion.104
  353.9 5.8 convolution_add_fusion
  397.5 34.1 %mixer_backward.2 = (bf16[1024,1664]{1,0:T(8,128)(2,1)}, f32[32,1024]{1,0:T(8,128)}, f32[8,256]{1,0:T(8,128)}, f32[16,128]{1,0:T(8,128)}, f32[2,128,256]{2,1,0:T(8,128)}, /*index=5*/f32[8,1024]{1,0:T(8,128)}) custom-call(s32[3]{0:T(128)} %select_reduce_fusion.ends_ref, f32[1024,1664]{1,0:T(8,128)} %fusion.6.proj_ref.halo_ref, ...), custom_call_target="tpu_custom_call" | custom-call | flops 2048000000 | bytes 18432000 | tf_op jit(solution)/shard_map/mixer_backward/pallas_call | solution.py:453
  437.8 4.6 fusion.64.dgated_ref
  450.9 34.4 %mixer_backward.3 = (bf16[1024,1664]{1,0:T(8,128)(2,1)}, f32[32,1024]{1,0:T(8,128)}, f32[8,256]{1,0:T(8,128)}, f32[16,128]{1,0:T(8,128)}, f32[2,128,256]{2,1,0:T(8,128)}, /*index=5*/f32[8,1024]{1,0:T(8,128)}) custom-call(s32[3]{0:T(128)} %select_reduce_fusion.ends_ref, f32[1024,1664]{1,0:T(8,128)} %fusion.8.proj_ref.before_ref.halo_ref, ...), custom_call_target="tpu_custom_call" | custom-call | flops 2048000000 | bytes 18432000 | tf_op jit(solution)/shard_map/mixer_backward/pallas_call | solution.py:453
  491.1 6.9 %fusion.105 = f32[1024,1664]{1,0:T(8,128)S(1)} fusion(bf16[1024,1024]{1,0:T(8,128)(2,1)} %bitcast.226, bf16[1024,1664]{1,0:T(8,128)(2,1)} %get-tuple-element.183), kind=kOutput, calls=%fused_computation.245 | convolution fusion | flops 3489660928 | bytes 12320768 | tf_op jit(solution)/shard_map/dot_general | solution.py:598
  498.1 4.6 add_convert_fusion
  505.1 7.1 %fusion.28 = bf16[1024,1024]{1,0:T(8,128)(2,1)S(1)} fusion(bf16[1024,1664]{1,0:T(8,128)(2,1)} %get-tuple-element.183, bf16[1024,2176]{1,0:T(8,128)(2,1)} %all-gather.3.cloned.1.call-done), kind=kOutput, calls=%fused_computation.73 | convolution fusion | flops 3490709504 | bytes 8912896 | tf_op jit(solution)/shard_map/dot_general | solution.py:598
  531.9 5.0 collective-permute-start.32
  536.9 26.2 %collective-permute-done.31 = bf16[512,1024]{1,0:T(8,128)(2,1)S(1)} collective-permute-done((bf16[512,1024]{1,0:T(8,128)(2,1)}, bf16[512,1024]{1,0:T(8,128)(2,1)S(1)}, u32[]{:S(2)}, u32[]{:S(2)}) %collective-permute-start.31) | collective-permute-done | bytes 1048608 | tf_op jit(solution)/shard_map/ppermute | solution.py:524
  565.2 9.6 %collective-permute-done.32 = bf16[128,2112]{0,1:T(8,128)(2,1)S(1)} collective-permute-done((bf16[128,2112]{0,1:T(8,128)(2,1)}, bf16[128,2112]{0,1:T(8,128)(2,1)S(1)}, u32[]{:S(2)}, u32[]{:S(2)}) %collective-permute-start.32) | collective-permute-done | bytes 540704 | tf_op jit(solution)/shard_map/ppermute | solution.py:529
  588.8 7.2 %collective-permute-done.36 = f32[8,384]{1,0:T(8,128)S(1)} collective-permute-done((f32[8,384]{1,0:T(8,128)S(1)}, f32[8,384]{1,0:T(8,128)S(1)}, u32[]{:S(2)}, u32[]{:S(2)}) %collective-permute-start.36) | collective-permute-done | bytes 12320 | tf_op jit(solution)/shard_map/ppermute | solution.py:524
  596.0 4.8 collective-permute-start.37
  609.9 16.0 %reduce-scatter.5.cloned.1.call-done = bf16[128,2176]{1,0:T(8,128)(2,1)} async-done(((bf16[1024,2176]{1,0:T(8,128)(2,1)}), bf16[128,2176]{1,0:T(8,128)(2,1)}) %reduce-scatter.5.cloned.1.call-update) | async-done | bytes 557072 | tf_op jit(solution)/shard_map/reduce_scatter | solution.py:594
  634.8 22.1 %collective-permute-done.33 = bf16[128,2176]{1,0:T(8,128)(2,1)S(1)} collective-permute-done((bf16[128,2176]{1,0:T(8,128)(2,1)}, bf16[128,2176]{1,0:T(8,128)(2,1)S(1)}, u32[]{:S(2)}, u32[]{:S(2)}) %collective-permute-start.33) | collective-permute-done | bytes 557088 | tf_op jit(solution)/shard_map/ppermute | solution.py:529
  (391 shorter events, 214.6 us)
Async XLA Ops:
  7.2 153.0 %all-gather.3.cloned.1.call-start = ((), (), s32[]{:S(2)}) async-start(), calls=%async_computation.6 | async-start | bytes 5013504 | tf_op jit(solution)/shard_map/all_gather | solution.py:590
  10.9 30.7 %collective-permute-start.3 = (bf16[128,2176]{1,0:T(8,128)(2,1)S(1)}, bf16[128,2176]{1,0:T(8,128)(2,1)S(1)}, u32[]{:S(2)}, u32[]{:S(2)}) collective-permute-start(bf16[128,2176]{1,0:T(8,128)(2,1)S(1)} %concatenate.99), channel_id=1, source_target_pairs={{0,0},{1,4},{2,8},{3,12},{4,1},{5,5},{6,9},{7,13},{8,2},{9,6},{10,... | collective-permute-start | bytes 1671176 | tf_op jit(solution)/shard_map/ppermute | solution.py:529
  44.9 48.8 %all-to-all-start = ((bf16[8,64,1152]{2,1,0:T(8,128)(2,1)}), bf16[8,64,1152]{2,1,0:T(8,128)(2,1)S(1)}, u32[]{:S(2)}, u32[]{:S(2)}) async-start(bf16[8,64,1152]{2,1,0:T(8,128)(2,1)} %bitcast.1), calls=%async_computation | async-start | bytes 2359296 | tf_op jit(solution)/shard_map/all_to_all | solution.py:640
  48.6 44.5 %collective-permute-start = (s32[1,3]{1,0:T(1,128)S(1)}, s32[1,3]{1,0:T(1,128)S(1)}, u32[]{:S(2)}, u32[]{:S(2)}) collective-permute-start(s32[1,3]{1,0:T(1,128)S(1)} %copy-done.47), channel_id=1, source_target_pairs={{0,0},{1,4},{2,8},{3,12},{4,1},{5,5},{6,9},{7,13},{8,2},{9,6},{10,... | collective-permute-start | bytes 44 | tf_op jit(solution)/shard_map/ppermute | solution.py:529
  96.6 15.7 %collective-permute-start.1 = (bf16[256,1152]{1,0:T(8,128)(2,1)S(1)}, bf16[256,1152]{1,0:T(8,128)(2,1)S(1)}, u32[]{:S(2)}, u32[]{:S(2)}) collective-permute-start(bf16[256,1152]{1,0:T(8,128)(2,1)S(1)} %get-tuple-element.285), channel_id=1, source_target_pairs={{0,8},{4,12},{8,0},{12,4},{1,9},{5,13},{9,1},{13,5},{2,10},{6,14},... | collective-permute-start | bytes 1769480 | tf_op jit(solution)/shard_map/ppermute | solution.py:524
  115.1 43.8 %all-to-all-start.1 = ((bf16[8,64,1024]{2,1,0:T(8,128)(2,1)}), bf16[8,64,1024]{2,1,0:T(8,128)(2,1)}, u32[]{:S(2)}, u32[]{:S(2)}) async-start(bf16[8,64,1024]{2,1,0:T(8,128)(2,1)} %bitcast.183), calls=%async_computation.1 | async-start | bytes 2097152 | tf_op jit(solution)/shard_map/all_to_all | solution.py:640
  119.4 165.2 %all-gather.5.cloned.1.call-start = ((), (), s32[]{:S(2)}) async-start(), calls=%async_computation.7 | async-start | bytes 4866048 | tf_op jit(solution)/shard_map/all_gather | solution.py:590
  169.7 30.0 %collective-permute-start.4 = (bf16[256,1152]{1,0:T(8,128)(2,1)S(1)}, bf16[256,1152]{1,0:T(8,128)(2,1)}, u32[]{:S(2)}, u32[]{:S(2)}) collective-permute-start(bf16[256,1152]{1,0:T(8,128)(2,1)S(1)} %copy-done.15), channel_id=1, source_target_pairs={{0,8},{4,12},{8,0},{12,4},{1,9},{5,13},{9,1},{13,5},{2,10},{6,14},... | collective-permute-start | bytes 1769480 | tf_op jit(solution)/shard_map/ppermute | solution.py:524
  170.8 31.2 %collective-permute-start.5 = (bf16[128,2112]{0,1:T(8,128)(2,1)}, bf16[128,2112]{0,1:T(8,128)(2,1)}, u32[]{:S(2)}, u32[]{:S(2)}) collective-permute-start(bf16[128,2112]{0,1:T(8,128)(2,1)} %pad_maximum_fusion.26), channel_id=1, source_target_pairs={{0,0},{1,4},{2,8},{3,12},{4,1},{5,5},{6,9},{7,13},{8,2},{9,6},{10,... | collective-permute-start | bytes 1622024 | tf_op jit(solution)/shard_map/ppermute | solution.py:529
  202.0 289.2 %reduce-scatter.3.cloned.1.call-start = ((), (), s32[]{:S(2)}) async-start(), calls=%async_computation.8 | async-start | bytes 5013504 | tf_op jit(solution)/shard_map/reduce_scatter | solution.py:594
  202.0 10.3 %collective-permute-start.6 = (bf16[512,1152]{1,0:T(8,128)(2,1)}, bf16[512,1152]{1,0:T(8,128)(2,1)S(1)}, u32[]{:S(2)}, u32[]{:S(2)}) collective-permute-start(bf16[512,1152]{1,0:T(8,128)(2,1)} %pad_maximum_fusion.13), channel_id=1, source_target_pairs={{0,4},{4,0},{8,12},{12,8},{1,5},{5,1},{9,13},{13,9},{2,6},{6,2},{1... | collective-permute-start | bytes 3538952 | tf_op jit(solution)/shard_map/ppermute | solution.py:524
  206.9 16.8 %collective-permute-start.7 = (f32[512,1024]{1,0:T(8,128)S(1)}, f32[512,1024]{1,0:T(8,128)S(1)}, u32[]{:S(2)}, u32[]{:S(2)}) collective-permute-start(f32[512,1024]{1,0:T(8,128)S(1)} %slice.318), channel_id=1, source_target_pairs={{0,4},{4,0},{8,12},{12,8},{1,5},{5,1},{9,13},{13,9},{2,6},{6,2},{1... | collective-permute-start | bytes 6291464 | tf_op jit(solution)/shard_map/ppermute | solution.py:524
  207.5 28.3 %collective-permute-start.8 = (bf16[512,1024]{1,0:T(8,128)(2,1)S(1)}, bf16[512,1024]{1,0:T(8,128)(2,1)S(1)}, u32[]{:S(2)}, u32[]{:S(2)}) collective-permute-start(bf16[512,1024]{1,0:T(8,128)(2,1)S(1)} %bitcast.154), channel_id=1, source_target_pairs={{0,8},{4,12},{8,0},{12,4},{1,9},{5,13},{9,1},{13,5},{2,10},{6,14},... | collective-permute-start | bytes 3145736 | tf_op jit(solution)/shard_map/ppermute | solution.py:524
  236.7 29.3 %collective-permute-start.10 = (f32[256,1024]{1,0:T(8,128)S(1)}, f32[256,1024]{1,0:T(8,128)S(1)}, u32[]{:S(2)}, u32[]{:S(2)}) collective-permute-start(f32[256,1024]{1,0:T(8,128)S(1)} %get-tuple-element.123), channel_id=1, source_target_pairs={{0,8},{4,12},{8,0},{12,4},{1,9},{5,13},{9,1},{13,5},{2,10},{6,14},... | collective-permute-start | bytes 3145736 | tf_op jit(solution)/shard_map/ppermute | solution.py:524
  265.6 17.2 %collective-permute-start.9 = (f32[512,1024]{1,0:T(8,128)S(1)}, f32[512,1024]{1,0:T(8,128)S(1)}, u32[]{:S(2)}, u32[]{:S(2)}) collective-permute-start(f32[512,1024]{1,0:T(8,128)S(1)} %slice.323), channel_id=1, source_target_pairs={{0,4},{4,0},{8,12},{12,8},{1,5},{5,1},{9,13},{13,9},{2,6},{6,2},{1... | collective-permute-start | bytes 6291464 | tf_op jit(solution)/shard_map/ppermute | solution.py:524
  267.5 14.4 %collective-permute-start.11 = (bf16[256,1024]{1,0:T(8,128)(2,1)S(1)}, bf16[256,1024]{1,0:T(8,128)(2,1)S(1)}, u32[]{:S(2)}, u32[]{:S(2)}) collective-permute-start(bf16[256,1024]{1,0:T(8,128)(2,1)S(1)} %multiply_convert_fusion.8), channel_id=1, source_target_pairs={{0,8},{4,12},{8,0},{12,4},{1,9},{5,13},{9,1},{13,5},{2,10},{6,14},... | collective-permute-start | bytes 1572872 | tf_op jit(solution)/shard_map/ppermute | solution.py:524
  287.0 25.1 %collective-permute-start.12 = (f32[256,1024]{1,0:T(8,128)S(1)}, f32[256,1024]{1,0:T(8,128)S(1)}, u32[]{:S(2)}, u32[]{:S(2)}) collective-permute-start(f32[256,1024]{1,0:T(8,128)S(1)} %copy-done.21), channel_id=1, source_target_pairs={{0,8},{4,12},{8,0},{12,4},{1,9},{5,13},{9,1},{13,5},{2,10},{6,14},... | collective-permute-start | bytes 3145736 | tf_op jit(solution)/shard_map/ppermute | solution.py:524
  303.8 22.0 %collective-permute-start.16 = (bf16[512,1024]{1,0:T(8,128)(2,1)S(1)}, bf16[512,1024]{1,0:T(8,128)(2,1)S(1)}, u32[]{:S(2)}, u32[]{:S(2)}) collective-permute-start(bf16[512,1024]{1,0:T(8,128)(2,1)S(1)} %slice.332), channel_id=1, source_target_pairs={{0,4},{4,0},{8,12},{12,8},{1,5},{5,1},{9,13},{13,9},{2,6},{6,2},{1... | collective-permute-start | bytes 3145736 | tf_op jit(solution)/shard_map/ppermute | solution.py:524
  312.7 13.1 %collective-permute-start.17 = (bf16[256,1024]{1,0:T(8,128)(2,1)S(1)}, bf16[256,1024]{1,0:T(8,128)(2,1)S(1)}, u32[]{:S(2)}, u32[]{:S(2)}) collective-permute-start(bf16[256,1024]{1,0:T(8,128)(2,1)S(1)} %multiply_convert_fusion.7), channel_id=1, source_target_pairs={{0,8},{4,12},{8,0},{12,4},{1,9},{5,13},{9,1},{13,5},{2,10},{6,14},... | collective-permute-start | bytes 1572872 | tf_op jit(solution)/shard_map/ppermute | solution.py:524
  327.9 16.9 %collective-permute-start.20 = (bf16[256,1024]{1,0:T(8,128)(2,1)S(1)}, bf16[256,1024]{1,0:T(8,128)(2,1)S(1)}, u32[]{:S(2)}, u32[]{:S(2)}) collective-permute-start(bf16[256,1024]{1,0:T(8,128)(2,1)S(1)} %slice.467), channel_id=1, source_target_pairs={{0,8},{4,12},{8,0},{12,4},{1,9},{5,13},{9,1},{13,5},{2,10},{6,14},... | collective-permute-start | bytes 1572872 | tf_op jit(solution)/shard_map/ppermute | solution.py:524
  347.6 14.0 %collective-permute-start.21 = (bf16[256,1024]{1,0:T(8,128)(2,1)S(1)}, bf16[256,1024]{1,0:T(8,128)(2,1)S(1)}, u32[]{:S(2)}, u32[]{:S(2)}) collective-permute-start(bf16[256,1024]{1,0:T(8,128)(2,1)S(1)} %slice.466), channel_id=1, source_target_pairs={{0,8},{4,12},{8,0},{12,4},{1,9},{5,13},{9,1},{13,5},{2,10},{6,14},... | collective-permute-start | bytes 1572872 | tf_op jit(solution)/shard_map/ppermute | solution.py:524
  363.5 13.1 %collective-permute-start.22 = (bf16[256,1024]{1,0:T(8,128)(2,1)S(1)}, bf16[256,1024]{1,0:T(8,128)(2,1)S(1)}, u32[]{:S(2)}, u32[]{:S(2)}) collective-permute-start(bf16[256,1024]{1,0:T(8,128)(2,1)S(1)} %get-tuple-element.266), channel_id=1, source_target_pairs={{0,8},{4,12},{8,0},{12,4},{1,9},{5,13},{9,1},{13,5},{2,10},{6,14},... | collective-permute-start | bytes 1572872 | tf_op jit(solution)/shard_map/ppermute | solution.py:524
  393.7 37.9 %collective-permute-start.26 = (bf16[256,1024]{1,0:T(8,128)(2,1)S(1)}, bf16[256,1024]{1,0:T(8,128)(2,1)S(1)}, u32[]{:S(2)}, u32[]{:S(2)}) collective-permute-start(bf16[256,1024]{1,0:T(8,128)(2,1)S(1)} %copy-done.16), channel_id=1, source_target_pairs={{0,8},{4,12},{8,0},{12,4},{1,9},{5,13},{9,1},{13,5},{2,10},{6,14},... | collective-permute-start | bytes 1572872 | tf_op jit(solution)/shard_map/ppermute | solution.py:524
  394.8 36.9 %collective-permute-start.27 = (bf16[256,1024]{1,0:T(8,128)(2,1)S(1)}, bf16[256,1024]{1,0:T(8,128)(2,1)S(1)}, u32[]{:S(2)}, u32[]{:S(2)}) collective-permute-start(bf16[256,1024]{1,0:T(8,128)(2,1)S(1)} %slice.465), channel_id=1, source_target_pairs={{0,8},{4,12},{8,0},{12,4},{1,9},{5,13},{9,1},{13,5},{2,10},{6,14},... | collective-permute-start | bytes 1572872 | tf_op jit(solution)/shard_map/ppermute | solution.py:524
  395.7 37.3 %collective-permute-start.28 = (bf16[256,1024]{1,0:T(8,128)(2,1)S(1)}, bf16[256,1024]{1,0:T(8,128)(2,1)S(1)}, u32[]{:S(2)}, u32[]{:S(2)}) collective-permute-start(bf16[256,1024]{1,0:T(8,128)(2,1)S(1)} %slice.464), channel_id=1, source_target_pairs={{0,8},{4,12},{8,0},{12,4},{1,9},{5,13},{9,1},{13,5},{2,10},{6,14},... | collective-permute-start | bytes 1572872 | tf_op jit(solution)/shard_map/ppermute | solution.py:524
  442.4 48.7 %all-to-all-start.2 = ((bf16[8,64,1024]{2,1,0:T(8,128)(2,1)}), bf16[8,64,1024]{2,1,0:T(8,128)(2,1)S(1)}, u32[]{:S(2)}, u32[]{:S(2)}) async-start(bf16[8,64,1024]{2,1,0:T(8,128)(2,1)} %bitcast.58), calls=%async_computation.3 | async-start | bytes 2097152 | tf_op jit(solution)/shard_map/all_to_all | solution.py:640
  446.1 179.7 %reduce-scatter.5.cloned.1.call-start = ((), (), s32[]{:S(2)}) async-start(), calls=%async_computation.9 | async-start | bytes 5013504 | tf_op jit(solution)/shard_map/reduce_scatter | solution.py:594
  530.3 32.7 %collective-permute-start.31 = (bf16[512,1024]{1,0:T(8,128)(2,1)}, bf16[512,1024]{1,0:T(8,128)(2,1)S(1)}, u32[]{:S(2)}, u32[]{:S(2)}) collective-permute-start(bf16[512,1024]{1,0:T(8,128)(2,1)} %slice.463), channel_id=1, source_target_pairs={{0,8},{4,12},{8,0},{12,4},{1,9},{5,13},{9,1},{13,5},{2,10},{6,14},... | collective-permute-start | bytes 3145736 | tf_op jit(solution)/shard_map/ppermute | solution.py:524
  531.9 42.9 %collective-permute-start.32 = (bf16[128,2112]{0,1:T(8,128)(2,1)}, bf16[128,2112]{0,1:T(8,128)(2,1)S(1)}, u32[]{:S(2)}, u32[]{:S(2)}) collective-permute-start(bf16[128,2112]{0,1:T(8,128)(2,1)} %copy.189), channel_id=1, source_target_pairs={{0,0},{1,4},{2,8},{3,12},{4,1},{5,5},{6,9},{7,13},{8,2},{9,6},{10,... | collective-permute-start | bytes 1622024 | tf_op jit(solution)/shard_map/ppermute | solution.py:529
  577.2 54.5 %all-to-all-start.3 = ((bf16[8,64,1024]{2,1,0:T(8,128)(2,1)}), bf16[8,64,1024]{2,1,0:T(8,128)(2,1)}, u32[]{:S(2)}, u32[]{:S(2)}) async-start(bf16[8,64,1024]{2,1,0:T(8,128)(2,1)} %bitcast.75), calls=%async_computation.4 | async-start | bytes 2097152 | tf_op jit(solution)/shard_map/all_to_all | solution.py:640
  586.9 9.1 %collective-permute-start.36 = (f32[8,384]{1,0:T(8,128)S(1)}, f32[8,384]{1,0:T(8,128)S(1)}, u32[]{:S(2)}, u32[]{:S(2)}) collective-permute-start(f32[8,384]{1,0:T(8,128)S(1)} %add.314), channel_id=1, source_target_pairs={{0,1},{1,0},{2,3},{3,2},{4,5},{5,4},{6,7},{7,6},{8,9},{9,8},{10,11... | collective-permute-start | bytes 36872 | tf_op jit(solution)/shard_map/ppermute | solution.py:524
  625.9 31.0 %collective-permute-start.33 = (bf16[128,2176]{1,0:T(8,128)(2,1)}, bf16[128,2176]{1,0:T(8,128)(2,1)S(1)}, u32[]{:S(2)}, u32[]{:S(2)}) collective-permute-start(bf16[128,2176]{1,0:T(8,128)(2,1)} %reduce-scatter.5.cloned.1.call-done), channel_id=1, source_target_pairs={{0,0},{1,4},{2,8},{3,12},{4,1},{5,5},{6,9},{7,13},{8,2},{9,6},{10,... | collective-permute-start | bytes 1671176 | tf_op jit(solution)/shard_map/ppermute | solution.py:529
  (75 other events, 954.6 us)
Sparse Core Ops, SparseCore 0:
  42.6 112.7 all-gather.2
  202.1 77.6 all-gather.4
  379.2 110.0 reduce-scatter.2
  505.2 120.5 reduce-scatter.4

commit v5 on v4

--- a/solution.py
+++ b/solution.py
@@ -761,25 +761,22 @@
     orders = [order_of(gathered_0[:, model_width:])]
     seq_0 = to_sequence(orders[0], gathered_0[:, :model_width])
     projected = [product(seq_0, mix_all)]
-    packed_grad = by_part(packed_grad)
-    projected[0], normed_runs, ffn_sent, packed_grad = lax.optimization_barrier(
-        (projected[0], normed_runs, ffn_sent, packed_grad)
+    gathered_1 = gather_rows(normed_runs[1])
+    orders.append(order_of(gathered_1[:, model_width:]))
+    seq_1 = to_sequence(orders[1], gathered_1[:, :model_width])
+    ffn_own = exchange_roles(after(ffn_sent, gathered_1))
+    projected[0], seq_1, ffn_own, packed_grad = lax.optimization_barrier(
+        (projected[0], seq_1, ffn_own, by_part(packed_grad))
     )
+    ffn_all = widen(ffn_own)
     *saved_0, state = mix_forward(0, state)
     crossed = swap(packed_grad, "lo", bits(splits)[-1])
-    saved_0, first_1, ffn_own = lax.optimization_barrier(
-        (saved_0, gather_first(normed_runs[1]), exchange_roles(ffn_sent))
-    )
-    ffn_all = widen(ffn_own)
+    saved_0, crossed = lax.optimization_barrier((saved_0, crossed))
     grad_runs = split(packed_grad)
-    gathered_1 = gather_last(first_1)
     terms_0 = product(from_sequence(orders[0], saved_0[0]), out_all, 1, 1)
-    gathered_1 = after(gathered_1, terms_0)
-    orders.append(order_of(gathered_1[:, model_width:]))
-    seq_1 = to_sequence(orders[1], gathered_1[:, :model_width])
-    projected.append(product(seq_1, mix_all))
+    projected.append(product(after(seq_1, terms_0), mix_all))
     kept_0, sent_0 = scatter_first(terms_0)
-    projected[1], kept_0, sent_0, crossed = lax.optimization_barrier((projected[1], kept_0, sent_0, crossed))
+    projected[1], kept_0, sent_0 = lax.optimization_barrier((projected[1], kept_0, sent_0))
     grad_all = [gather_last(jnp.concatenate(x, axis=0)) for x in zip(grad_runs, split(crossed))]
     *saved_1, state = mix_forward(1, state)
     middle_0 = input_runs[0] + after(scatter_last(kept_0, sent_0), saved_1[0])

time: 677 us -> 660 us (0.975)
  waiting for transfers between devices: 260 us -> 247 us
    all_to_all x4, waiting for transfers between devices: 31.2 us -> 8.92 us  [across(): return lax.all_to_all(rows, spread, split_axis=0, concat_axis=0, tiled=True)]
    ppermute x5, waiting for transfers between devices: 96.8 us -> 109 us  [exchange_roles(): lax.ppermute(x, ('lo', 'tensor'), [(a * n + b, b * n + a) for a in range(...]
    unnamed x118 -> x120, local copies, waits for them, and re-layouts: 15.7 us -> 13.9 us
  transfers between devices with their start and end apart: 47 -> 47, of which waited for: 26 -> 27; matrix products, arithmetic and copies ran while one was open for 25% -> 26% of each run, Pallas kernels for 17% -> 17%
where the time goes in v5:
time: 660 us; the launch traced here: 653 us
  waiting for transfers between devices  247 us (37%)
  matrix products  137 us (21%)
  Pallas kernels  114 us (17%)
  starting transfers between devices  62.1 us (9%)
  local copies, waits for them, and re-layouts  41.4 us (6%)
  other arithmetic  37 us (6%)
  between operations  15.7 us (2%)
    dot_general x28, matrix products, product(): lax.dot_general(a, b, (((ca,), (cb,)), ((), ())), preferred_element_type=...  121 us
    ppermute x34, waiting for transfers between devices, swap(): return lax.ppermute(x, axis, [(i, i ^ bit) for i in range(size)])  112 us
    ppermute x5, waiting for transfers between devices, exchange_roles(): lax.ppermute(x, ('lo', 'tensor'), [(a * n + b, b * n + a) for a in range(...  109 us
    pallas_call x2, Pallas kernels, mixer_backward(): pl.pallas_call(kernel, grid_spec=pltpu.PrefetchScalarGridSpec(num_scalar_...  68.5 us
    pallas_call x2, Pallas kernels, mixer_forward(): pl.pallas_call(kernel, grid_spec=pltpu.PrefetchScalarGridSpec(num_scalar_...  45.2 us
    ppermute x34, starting transfers between devices, swap(): return lax.ppermute(x, axis, [(i, i ^ bit) for i in range(size)])  23.7 us
    ppermute x5, starting transfers between devices, exchange_roles(): lax.ppermute(x, ('lo', 'tensor'), [(a * n + b, b * n + a) for a in range(...  22.2 us
    reduce_scatter x2, waiting for transfers between devices, narrow(): lax.psum_scatter(columns.astype(bf16), ('hi', 'tensor'), scatter_dimensio...  16 us
  transfers between devices with their start and end apart: 47, of which 27 were waited for; matrix products, arithmetic and copies ran while one was open for 26% of the time, Pallas kernels for 17%

profile of v5, /device:TPU:2, one launch (start us, length us, event | category | flops | bytes accessed | tf_op | source)
XLA Modules:
  0.0 653.5 jit_solution(10843401263846914016)
XLA Ops:
  15.5 26.2 %collective-permute-done.3 = bf16[128,2176]{1,0:T(8,128)(2,1)S(1)} collective-permute-done((bf16[128,2176]{1,0:T(8,128)(2,1)S(1)}, bf16[128,2176]{1,0:T(8,128)(2,1)S(1)}, u32[]{:S(2)}, u32[]{:S(2)}) %collective-permute-start.3) | collective-permute-done | bytes 557088 | tf_op jit(solution)/shard_map/ppermute | solution.py:529
  54.0 39.0 %collective-permute-done = s32[1,3]{1,0:T(1,128)S(1)} collective-permute-done((s32[1,3]{1,0:T(1,128)S(1)}, s32[1,3]{1,0:T(1,128)S(1)}, u32[]{:S(2)}, u32[]{:S(2)}) %collective-permute-start) | collective-permute-done | bytes 44 | tf_op jit(solution)/shard_map/ppermute | solution.py:529
  97.9 14.1 %collective-permute-done.4 = bf16[256,1152]{1,0:T(8,128)(2,1)S(1)} collective-permute-done((bf16[256,1152]{1,0:T(8,128)(2,1)S(1)}, bf16[256,1152]{1,0:T(8,128)(2,1)S(1)}, u32[]{:S(2)}, u32[]{:S(2)}) %collective-permute-start.4) | collective-permute-done | bytes 589856 | tf_op jit(solution)/shard_map/ppermute | solution.py:524
  113.2 11.0 %collective-permute-done.1 = bf16[256,1152]{1,0:T(8,128)(2,1)S(1)} collective-permute-done((bf16[256,1152]{1,0:T(8,128)(2,1)S(1)}, bf16[256,1152]{1,0:T(8,128)(2,1)S(1)}, u32[]{:S(2)}, u32[]{:S(2)}) %collective-permute-start.1) | collective-permute-done | bytes 589856 | tf_op jit(solution)/shard_map/ppermute | solution.py:524
  139.7 5.8 collective-permute-start.6
  151.8 8.1 %all-to-all-done.1 = bf16[8,64,1024]{2,1,0:T(8,128)(2,1)} async-done(((bf16[8,64,1024]{2,1,0:T(8,128)(2,1)}), bf16[8,64,1024]{2,1,0:T(8,128)(2,1)}, u32[]{:S(2)}, u32[]{:S(2)}) %all-to-all-start.1) | async-done | bytes 1048608 | tf_op jit(solution)/shard_map/all_to_all | solution.py:640
  161.3 9.4 %fusion.8.proj_ref.before_ref.halo_ref = f32[1024,1664]{1,0:T(8,128)} fusion(bf16[1024,1024]{1,0:T(8,128)(2,1)} %bitcast.225, bf16[1024,2176]{1,0:T(8,128)(2,1)} %all-gather.3.cloned.1.call-done), kind=kOutput, calls=%fused_computation.29 | convolution fusion | flops 3489660928 | bytes 12320768 | tf_op jit(solution)/shard_map/dot_general | solution.py:598
  170.7 12.4 %collective-permute-done.6 = bf16[128,2112]{0,1:T(8,128)(2,1)} collective-permute-done((bf16[128,2112]{0,1:T(8,128)(2,1)}, bf16[128,2112]{0,1:T(8,128)(2,1)}, u32[]{:S(2)}, u32[]{:S(2)}) %collective-permute-start.6) | collective-permute-done | bytes 540704 | tf_op jit(solution)/shard_map/ppermute | solution.py:529
  186.5 22.9 %mixer_forward.2 = (bf16[1024,512]{1,0:T(8,128)(2,1)}, f32[1024,512]{1,0:T(8,128)}, f32[1024,512]{1,0:T(8,128)}, f32[8,2,128,256]{3,2,1,0:T(8,128)}, f32[8,2,128...) custom-call(s32[3]{0:T(128)} %select_reduce_fusion.ends_ref, ...), custom_call_target="tpu_custom_call" | custom-call | flops 2048000000 | bytes 18432000 | tf_op jit(solution)/shard_map/mixer_forward/pallas_call | solution.py:392
  215.8 6.1 fusion.6.proj_ref.halo_ref
  223.8 22.3 %mixer_forward.3 = (bf16[1024,512]{1,0:T(8,128)(2,1)}, f32[1024,512]{1,0:T(8,128)}, f32[1024,512]{1,0:T(8,128)}, f32[8,2,128,256]{3,2,1,0:T(8,128)}, f32[8,2,128...) custom-call(s32[3]{0:T(128)} %select_reduce_fusion.ends_ref, ...), custom_call_target="tpu_custom_call" | custom-call | flops 2048000000 | bytes 18432000 | tf_op jit(solution)/shard_map/mixer_forward/pallas_call | solution.py:392
  254.8 12.3 %collective-permute-done.11 = bf16[256,1024]{1,0:T(8,128)(2,1)S(1)} collective-permute-done((bf16[256,1024]{1,0:T(8,128)(2,1)S(1)}, bf16[256,1024]{1,0:T(8,128)(2,1)S(1)}, u32[]{:S(2)}, u32[]{:S(2)}) %collective-permute-start.11) | collective-permute-done | bytes 524320 | tf_op jit(solution)/shard_map/ppermute | solution.py:524
  274.9 5.0 fusion.38
  279.8 6.3 multiply_convert_fusion.5
  290.1 7.9 %collective-permute-done.12 = f32[256,1024]{1,0:T(8,128)S(1)} collective-permute-done((f32[256,1024]{1,0:T(8,128)S(1)}, f32[256,1024]{1,0:T(8,128)S(1)}, u32[]{:S(2)}, u32[]{:S(2)}) %collective-permute-start.12) | collective-permute-done | bytes 1048608 | tf_op jit(solution)/shard_map/ppermute | solution.py:524
  299.3 12.3 %collective-permute-done.17 = bf16[256,1024]{1,0:T(8,128)(2,1)S(1)} collective-permute-done((bf16[256,1024]{1,0:T(8,128)(2,1)S(1)}, bf16[256,1024]{1,0:T(8,128)(2,1)S(1)}, u32[]{:S(2)}, u32[]{:S(2)}) %collective-permute-start.17) | collective-permute-done | bytes 524320 | tf_op jit(solution)/shard_map/ppermute | solution.py:524
  314.9 5.1 fusion.35
  320.0 6.3 multiply_convert_fusion.3
  334.4 5.3 fusion.104
  339.7 5.8 convolution_add_fusion
  383.3 34.1 %mixer_backward.2 = (bf16[1024,1664]{1,0:T(8,128)(2,1)}, f32[32,1024]{1,0:T(8,128)}, f32[8,256]{1,0:T(8,128)}, f32[16,128]{1,0:T(8,128)}, f32[2,128,256]{2,1,0:T(8,128)}, /*index=5*/f32[8,1024]{1,0:T(8,128)}) custom-call(s32[3]{0:T(128)} %select_reduce_fusion.ends_ref, f32[1024,1664]{1,0:T(8,128)} %fusion.6.proj_ref.halo_ref, ...), custom_call_target="tpu_custom_call" | custom-call | flops 2048000000 | bytes 18432000 | tf_op jit(solution)/shard_map/mixer_backward/pallas_call | solution.py:453
  436.6 34.4 %mixer_backward.3 = (bf16[1024,1664]{1,0:T(8,128)(2,1)}, f32[32,1024]{1,0:T(8,128)}, f32[8,256]{1,0:T(8,128)}, f32[16,128]{1,0:T(8,128)}, f32[2,128,256]{2,1,0:T(8,128)}, /*index=5*/f32[8,1024]{1,0:T(8,128)}) custom-call(s32[3]{0:T(128)} %select_reduce_fusion.ends_ref, f32[1024,1664]{1,0:T(8,128)} %fusion.8.proj_ref.before_ref.halo_ref, ...), custom_call_target="tpu_custom_call" | custom-call | flops 2048000000 | bytes 18432000 | tf_op jit(solution)/shard_map/mixer_backward/pallas_call | solution.py:453
  477.0 6.9 %fusion.105 = f32[1024,1664]{1,0:T(8,128)S(1)} fusion(bf16[1024,1024]{1,0:T(8,128)(2,1)} %bitcast.226, bf16[1024,1664]{1,0:T(8,128)(2,1)} %get-tuple-element.181), kind=kOutput, calls=%fused_computation.245 | convolution fusion | flops 3489660928 | bytes 12320768 | tf_op jit(solution)/shard_map/dot_general | solution.py:598
  483.9 4.6 add_convert_fusion
  491.0 7.1 %fusion.28 = bf16[1024,1024]{1,0:T(8,128)(2,1)S(1)} fusion(bf16[1024,1664]{1,0:T(8,128)(2,1)} %get-tuple-element.181, bf16[1024,2176]{1,0:T(8,128)(2,1)} %all-gather.3.cloned.1.call-done), kind=kOutput, calls=%fused_computation.73 | convolution fusion | flops 3490709504 | bytes 8912896 | tf_op jit(solution)/shard_map/dot_general | solution.py:598
  518.1 4.7 collective-permute-start.32
  522.9 26.1 %collective-permute-done.31 = bf16[512,1024]{1,0:T(8,128)(2,1)S(1)} collective-permute-done((bf16[512,1024]{1,0:T(8,128)(2,1)}, bf16[512,1024]{1,0:T(8,128)(2,1)S(1)}, u32[]{:S(2)}, u32[]{:S(2)}) %collective-permute-start.31) | collective-permute-done | bytes 1048608 | tf_op jit(solution)/shard_map/ppermute | solution.py:524
  551.1 9.7 %collective-permute-done.32 = bf16[128,2112]{0,1:T(8,128)(2,1)S(1)} collective-permute-done((bf16[128,2112]{0,1:T(8,128)(2,1)}, bf16[128,2112]{0,1:T(8,128)(2,1)S(1)}, u32[]{:S(2)}, u32[]{:S(2)}) %collective-permute-start.32) | collective-permute-done | bytes 540704 | tf_op jit(solution)/shard_map/ppermute | solution.py:529
  574.7 7.2 %collective-permute-done.36 = f32[8,384]{1,0:T(8,128)S(1)} collective-permute-done((f32[8,384]{1,0:T(8,128)S(1)}, f32[8,384]{1,0:T(8,128)S(1)}, u32[]{:S(2)}, u32[]{:S(2)}) %collective-permute-start.36) | collective-permute-done | bytes 12320 | tf_op jit(solution)/shard_map/ppermute | solution.py:524
  582.0 4.8 collective-permute-start.37
  595.9 16.0 %reduce-scatter.5.cloned.1.call-done = bf16[128,2176]{1,0:T(8,128)(2,1)} async-done(((bf16[1024,2176]{1,0:T(8,128)(2,1)}), bf16[128,2176]{1,0:T(8,128)(2,1)}) %reduce-scatter.5.cloned.1.call-update) | async-done | bytes 557072 | tf_op jit(solution)/shard_map/reduce_scatter | solution.py:594
  620.8 22.1 %collective-permute-done.33 = bf16[128,2176]{1,0:T(8,128)(2,1)S(1)} collective-permute-done((bf16[128,2176]{1,0:T(8,128)(2,1)}, bf16[128,2176]{1,0:T(8,128)(2,1)S(1)}, u32[]{:S(2)}, u32[]{:S(2)}) %collective-permute-start.33) | collective-permute-done | bytes 557088 | tf_op jit(solution)/shard_map/ppermute | solution.py:529
  (394 shorter events, 216.7 us)
Async XLA Ops:
  7.2 154.1 %all-gather.3.cloned.1.call-start = ((), (), s32[]{:S(2)}) async-start(), calls=%async_computation.6 | async-start | bytes 5013504 | tf_op jit(solution)/shard_map/all_gather | solution.py:590
  10.9 30.7 %collective-permute-start.3 = (bf16[128,2176]{1,0:T(8,128)(2,1)S(1)}, bf16[128,2176]{1,0:T(8,128)(2,1)S(1)}, u32[]{:S(2)}, u32[]{:S(2)}) collective-permute-start(bf16[128,2176]{1,0:T(8,128)(2,1)S(1)} %concatenate.100), channel_id=1, source_target_pairs={{0,0},{1,4},{2,8},{3,12},{4,1},{5,5},{6,9},{7,13},{8,2},{9,6},{10,... | collective-permute-start | bytes 1671176 | tf_op jit(solution)/shard_map/ppermute | solution.py:529
  44.9 48.8 %all-to-all-start = ((bf16[8,64,1152]{2,1,0:T(8,128)(2,1)}), bf16[8,64,1152]{2,1,0:T(8,128)(2,1)S(1)}, u32[]{:S(2)}, u32[]{:S(2)}) async-start(bf16[8,64,1152]{2,1,0:T(8,128)(2,1)} %bitcast.1), calls=%async_computation | async-start | bytes 2359296 | tf_op jit(solution)/shard_map/all_to_all | solution.py:640
  48.6 44.5 %collective-permute-start = (s32[1,3]{1,0:T(1,128)S(1)}, s32[1,3]{1,0:T(1,128)S(1)}, u32[]{:S(2)}, u32[]{:S(2)}) collective-permute-start(s32[1,3]{1,0:T(1,128)S(1)} %copy-done.48), channel_id=1, source_target_pairs={{0,0},{1,4},{2,8},{3,12},{4,1},{5,5},{6,9},{7,13},{8,2},{9,6},{10,... | collective-permute-start | bytes 44 | tf_op jit(solution)/shard_map/ppermute | solution.py:529
  95.8 16.2 %collective-permute-start.4 = (bf16[256,1152]{1,0:T(8,128)(2,1)S(1)}, bf16[256,1152]{1,0:T(8,128)(2,1)S(1)}, u32[]{:S(2)}, u32[]{:S(2)}) collective-permute-start(bf16[256,1152]{1,0:T(8,128)(2,1)S(1)} %get-tuple-element.282), channel_id=1, source_target_pairs={{0,8},{4,12},{8,0},{12,4},{1,9},{5,13},{9,1},{13,5},{2,10},{6,14},... | collective-permute-start | bytes 1769480 | tf_op jit(solution)/shard_map/ppermute | solution.py:524
  96.7 27.5 %collective-permute-start.1 = (bf16[256,1152]{1,0:T(8,128)(2,1)S(1)}, bf16[256,1152]{1,0:T(8,128)(2,1)S(1)}, u32[]{:S(2)}, u32[]{:S(2)}) collective-permute-start(bf16[256,1152]{1,0:T(8,128)(2,1)S(1)} %get-tuple-element.283), channel_id=1, source_target_pairs={{0,8},{4,12},{8,0},{12,4},{1,9},{5,13},{9,1},{13,5},{2,10},{6,14},... | collective-permute-start | bytes 1769480 | tf_op jit(solution)/shard_map/ppermute | solution.py:524
  113.2 19.2 %collective-permute-start.5 = (bf16[512,1152]{1,0:T(8,128)(2,1)}, bf16[512,1152]{1,0:T(8,128)(2,1)}, u32[]{:S(2)}, u32[]{:S(2)}) collective-permute-start(bf16[512,1152]{1,0:T(8,128)(2,1)} %pad_maximum_fusion.13), channel_id=1, source_target_pairs={{0,4},{4,0},{8,12},{12,8},{1,5},{5,1},{9,13},{13,9},{2,6},{6,2},{1... | collective-permute-start | bytes 3538952 | tf_op jit(solution)/shard_map/ppermute | solution.py:524
  125.3 10.2 %collective-permute-start.2 = (bf16[512,1152]{1,0:T(8,128)(2,1)}, bf16[512,1152]{1,0:T(8,128)(2,1)}, u32[]{:S(2)}, u32[]{:S(2)}) collective-permute-start(bf16[512,1152]{1,0:T(8,128)(2,1)} %pad_maximum_fusion.12), channel_id=1, source_target_pairs={{0,4},{4,0},{8,12},{12,8},{1,5},{5,1},{9,13},{13,9},{2,6},{6,2},{1... | collective-permute-start | bytes 3538952 | tf_op jit(solution)/shard_map/ppermute | solution.py:524
  128.0 32.0 %all-to-all-start.1 = ((bf16[8,64,1024]{2,1,0:T(8,128)(2,1)}), bf16[8,64,1024]{2,1,0:T(8,128)(2,1)}, u32[]{:S(2)}, u32[]{:S(2)}) async-start(bf16[8,64,1024]{2,1,0:T(8,128)(2,1)} %bitcast.183), calls=%async_computation.1 | async-start | bytes 2097152 | tf_op jit(solution)/shard_map/all_to_all | solution.py:640
  132.3 137.5 %all-gather.5.cloned.1.call-start = ((), (), s32[]{:S(2)}) async-start(), calls=%async_computation.7 | async-start | bytes 4866048 | tf_op jit(solution)/shard_map/all_gather | solution.py:590
  139.7 43.4 %collective-permute-start.6 = (bf16[128,2112]{0,1:T(8,128)(2,1)}, bf16[128,2112]{0,1:T(8,128)(2,1)}, u32[]{:S(2)}, u32[]{:S(2)}) collective-permute-start(bf16[128,2112]{0,1:T(8,128)(2,1)} %pad_maximum_fusion.26), channel_id=1, source_target_pairs={{0,0},{1,4},{2,8},{3,12},{4,1},{5,5},{6,9},{7,13},{8,2},{9,6},{10,... | collective-permute-start | bytes 1622024 | tf_op jit(solution)/shard_map/ppermute | solution.py:529
  183.1 26.3 %collective-permute-start.7 = (bf16[512,1024]{1,0:T(8,128)(2,1)S(1)}, bf16[512,1024]{1,0:T(8,128)(2,1)}, u32[]{:S(2)}, u32[]{:S(2)}) collective-permute-start(bf16[512,1024]{1,0:T(8,128)(2,1)S(1)} %bitcast.154), channel_id=1, source_target_pairs={{0,8},{4,12},{8,0},{12,4},{1,9},{5,13},{9,1},{13,5},{2,10},{6,14},... | collective-permute-start | bytes 3145736 | tf_op jit(solution)/shard_map/ppermute | solution.py:524
  183.9 293.1 %reduce-scatter.3.cloned.1.call-start = ((), (), s32[]{:S(2)}) async-start(), calls=%async_computation.8 | async-start | bytes 5013504 | tf_op jit(solution)/shard_map/reduce_scatter | solution.py:594
  222.4 28.8 %collective-permute-start.10 = (f32[256,1024]{1,0:T(8,128)S(1)}, f32[256,1024]{1,0:T(8,128)S(1)}, u32[]{:S(2)}, u32[]{:S(2)}) collective-permute-start(f32[256,1024]{1,0:T(8,128)S(1)} %get-tuple-element.121), channel_id=1, source_target_pairs={{0,8},{4,12},{8,0},{12,4},{1,9},{5,13},{9,1},{13,5},{2,10},{6,14},... | collective-permute-start | bytes 3145736 | tf_op jit(solution)/shard_map/ppermute | solution.py:524
  250.8 17.3 %collective-permute-start.9 = (f32[512,1024]{1,0:T(8,128)S(1)}, f32[512,1024]{1,0:T(8,128)S(1)}, u32[]{:S(2)}, u32[]{:S(2)}) collective-permute-start(f32[512,1024]{1,0:T(8,128)S(1)} %slice.325), channel_id=1, source_target_pairs={{0,4},{4,0},{8,12},{12,8},{1,5},{5,1},{9,13},{13,9},{2,6},{6,2},{1... | collective-permute-start | bytes 6291464 | tf_op jit(solution)/shard_map/ppermute | solution.py:524
  252.7 14.4 %collective-permute-start.11 = (bf16[256,1024]{1,0:T(8,128)(2,1)S(1)}, bf16[256,1024]{1,0:T(8,128)(2,1)S(1)}, u32[]{:S(2)}, u32[]{:S(2)}) collective-permute-start(bf16[256,1024]{1,0:T(8,128)(2,1)S(1)} %multiply_convert_fusion.8), channel_id=1, source_target_pairs={{0,8},{4,12},{8,0},{12,4},{1,9},{5,13},{9,1},{13,5},{2,10},{6,14},... | collective-permute-start | bytes 1572872 | tf_op jit(solution)/shard_map/ppermute | solution.py:524
  272.8 25.2 %collective-permute-start.12 = (f32[256,1024]{1,0:T(8,128)S(1)}, f32[256,1024]{1,0:T(8,128)S(1)}, u32[]{:S(2)}, u32[]{:S(2)}) collective-permute-start(f32[256,1024]{1,0:T(8,128)S(1)} %copy-done.20), channel_id=1, source_target_pairs={{0,8},{4,12},{8,0},{12,4},{1,9},{5,13},{9,1},{13,5},{2,10},{6,14},... | collective-permute-start | bytes 3145736 | tf_op jit(solution)/shard_map/ppermute | solution.py:524
  289.9 21.7 %collective-permute-start.16 = (bf16[512,1024]{1,0:T(8,128)(2,1)S(1)}, bf16[512,1024]{1,0:T(8,128)(2,1)S(1)}, u32[]{:S(2)}, u32[]{:S(2)}) collective-permute-start(bf16[512,1024]{1,0:T(8,128)(2,1)S(1)} %slice.334), channel_id=1, source_target_pairs={{0,4},{4,0},{8,12},{12,8},{1,5},{5,1},{9,13},{13,9},{2,6},{6,2},{1... | collective-permute-start | bytes 3145736 | tf_op jit(solution)/shard_map/ppermute | solution.py:524
  298.5 13.1 %collective-permute-start.17 = (bf16[256,1024]{1,0:T(8,128)(2,1)S(1)}, bf16[256,1024]{1,0:T(8,128)(2,1)S(1)}, u32[]{:S(2)}, u32[]{:S(2)}) collective-permute-start(bf16[256,1024]{1,0:T(8,128)(2,1)S(1)} %multiply_convert_fusion.7), channel_id=1, source_target_pairs={{0,8},{4,12},{8,0},{12,4},{1,9},{5,13},{9,1},{13,5},{2,10},{6,14},... | collective-permute-start | bytes 1572872 | tf_op jit(solution)/shard_map/ppermute | solution.py:524
  313.7 16.9 %collective-permute-start.20 = (bf16[256,1024]{1,0:T(8,128)(2,1)S(1)}, bf16[256,1024]{1,0:T(8,128)(2,1)S(1)}, u32[]{:S(2)}, u32[]{:S(2)}) collective-permute-start(bf16[256,1024]{1,0:T(8,128)(2,1)S(1)} %slice.469), channel_id=1, source_target_pairs={{0,8},{4,12},{8,0},{12,4},{1,9},{5,13},{9,1},{13,5},{2,10},{6,14},... | collective-permute-start | bytes 1572872 | tf_op jit(solution)/shard_map/ppermute | solution.py:524
  333.4 14.0 %collective-permute-start.21 = (bf16[256,1024]{1,0:T(8,128)(2,1)S(1)}, bf16[256,1024]{1,0:T(8,128)(2,1)S(1)}, u32[]{:S(2)}, u32[]{:S(2)}) collective-permute-start(bf16[256,1024]{1,0:T(8,128)(2,1)S(1)} %slice.468), channel_id=1, source_target_pairs={{0,8},{4,12},{8,0},{12,4},{1,9},{5,13},{9,1},{13,5},{2,10},{6,14},... | collective-permute-start | bytes 1572872 | tf_op jit(solution)/shard_map/ppermute | solution.py:524
  349.3 13.1 %collective-permute-start.22 = (bf16[256,1024]{1,0:T(8,128)(2,1)S(1)}, bf16[256,1024]{1,0:T(8,128)(2,1)S(1)}, u32[]{:S(2)}, u32[]{:S(2)}) collective-permute-start(bf16[256,1024]{1,0:T(8,128)(2,1)S(1)} %get-tuple-element.264), channel_id=1, source_target_pairs={{0,8},{4,12},{8,0},{12,4},{1,9},{5,13},{9,1},{13,5},{2,10},{6,14},... | collective-permute-start | bytes 1572872 | tf_op jit(solution)/shard_map/ppermute | solution.py:524
  379.5 37.9 %collective-permute-start.26 = (bf16[256,1024]{1,0:T(8,128)(2,1)S(1)}, bf16[256,1024]{1,0:T(8,128)(2,1)S(1)}, u32[]{:S(2)}, u32[]{:S(2)}) collective-permute-start(bf16[256,1024]{1,0:T(8,128)(2,1)S(1)} %copy-done.17), channel_id=1, source_target_pairs={{0,8},{4,12},{8,0},{12,4},{1,9},{5,13},{9,1},{13,5},{2,10},{6,14},... | collective-permute-start | bytes 1572872 | tf_op jit(solution)/shard_map/ppermute | solution.py:524
  380.6 36.9 %collective-permute-start.27 = (bf16[256,1024]{1,0:T(8,128)(2,1)S(1)}, bf16[256,1024]{1,0:T(8,128)(2,1)S(1)}, u32[]{:S(2)}, u32[]{:S(2)}) collective-permute-start(bf16[256,1024]{1,0:T(8,128)(2,1)S(1)} %slice.467), channel_id=1, source_target_pairs={{0,8},{4,12},{8,0},{12,4},{1,9},{5,13},{9,1},{13,5},{2,10},{6,14},... | collective-permute-start | bytes 1572872 | tf_op jit(solution)/shard_map/ppermute | solution.py:524
  381.5 37.3 %collective-permute-start.28 = (bf16[256,1024]{1,0:T(8,128)(2,1)S(1)}, bf16[256,1024]{1,0:T(8,128)(2,1)S(1)}, u32[]{:S(2)}, u32[]{:S(2)}) collective-permute-start(bf16[256,1024]{1,0:T(8,128)(2,1)S(1)} %slice.466), channel_id=1, source_target_pairs={{0,8},{4,12},{8,0},{12,4},{1,9},{5,13},{9,1},{13,5},{2,10},{6,14},... | collective-permute-start | bytes 1572872 | tf_op jit(solution)/shard_map/ppermute | solution.py:524
  428.2 48.8 %all-to-all-start.2 = ((bf16[8,64,1024]{2,1,0:T(8,128)(2,1)}), bf16[8,64,1024]{2,1,0:T(8,128)(2,1)S(1)}, u32[]{:S(2)}, u32[]{:S(2)}) async-start(bf16[8,64,1024]{2,1,0:T(8,128)(2,1)} %bitcast.58), calls=%async_computation.3 | async-start | bytes 2097152 | tf_op jit(solution)/shard_map/all_to_all | solution.py:640
  431.9 180.0 %reduce-scatter.5.cloned.1.call-start = ((), (), s32[]{:S(2)}) async-start(), calls=%async_computation.9 | async-start | bytes 5013504 | tf_op jit(solution)/shard_map/reduce_scatter | solution.py:594
  516.2 32.7 %collective-permute-start.31 = (bf16[512,1024]{1,0:T(8,128)(2,1)}, bf16[512,1024]{1,0:T(8,128)(2,1)S(1)}, u32[]{:S(2)}, u32[]{:S(2)}) collective-permute-start(bf16[512,1024]{1,0:T(8,128)(2,1)} %slice.465), channel_id=1, source_target_pairs={{0,8},{4,12},{8,0},{12,4},{1,9},{5,13},{9,1},{13,5},{2,10},{6,14},... | collective-permute-start | bytes 3145736 | tf_op jit(solution)/shard_map/ppermute | solution.py:524
  518.1 42.6 %collective-permute-start.32 = (bf16[128,2112]{0,1:T(8,128)(2,1)}, bf16[128,2112]{0,1:T(8,128)(2,1)S(1)}, u32[]{:S(2)}, u32[]{:S(2)}) collective-permute-start(bf16[128,2112]{0,1:T(8,128)(2,1)} %copy.189), channel_id=1, source_target_pairs={{0,0},{1,4},{2,8},{3,12},{4,1},{5,5},{6,9},{7,13},{8,2},{9,6},{10,... | collective-permute-start | bytes 1622024 | tf_op jit(solution)/shard_map/ppermute | solution.py:529
  563.2 54.5 %all-to-all-start.3 = ((bf16[8,64,1024]{2,1,0:T(8,128)(2,1)}), bf16[8,64,1024]{2,1,0:T(8,128)(2,1)}, u32[]{:S(2)}, u32[]{:S(2)}) async-start(bf16[8,64,1024]{2,1,0:T(8,128)(2,1)} %bitcast.75), calls=%async_computation.4 | async-start | bytes 2097152 | tf_op jit(solution)/shard_map/all_to_all | solution.py:640
  572.9 9.1 %collective-permute-start.36 = (f32[8,384]{1,0:T(8,128)S(1)}, f32[8,384]{1,0:T(8,128)S(1)}, u32[]{:S(2)}, u32[]{:S(2)}) collective-permute-start(f32[8,384]{1,0:T(8,128)S(1)} %add.314), channel_id=1, source_target_pairs={{0,1},{1,0},{2,3},{3,2},{4,5},{5,4},{6,7},{7,6},{8,9},{9,8},{10,11... | collective-permute-start | bytes 36872 | tf_op jit(solution)/shard_map/ppermute | solution.py:524
  611.9 31.0 %collective-permute-start.33 = (bf16[128,2176]{1,0:T(8,128)(2,1)}, bf16[128,2176]{1,0:T(8,128)(2,1)S(1)}, u32[]{:S(2)}, u32[]{:S(2)}) collective-permute-start(bf16[128,2176]{1,0:T(8,128)(2,1)} %reduce-scatter.5.cloned.1.call-done), channel_id=1, source_target_pairs={{0,0},{1,4},{2,8},{3,12},{4,1},{5,5},{6,9},{7,13},{8,2},{9,6},{10,... | collective-permute-start | bytes 1671176 | tf_op jit(solution)/shard_map/ppermute | solution.py:529
  (77 other events, 1021.0 us)
Sparse Core Ops, SparseCore 0:
  42.6 96.0 all-gather.2
  184.0 74.5 all-gather.4
  365.0 110.2 reduce-scatter.2
  491.1 120.7 reduce-scatter.4

commit v6 on v5

--- a/solution.py
+++ b/solution.py
@@ -658,7 +658,6 @@
     digits = jnp.where(lane == 0, (place // 16)[:, None], jnp.where(lane == 1, (place % 16)[:, None], 0))
     tagged = jnp.concatenate([tokens, digits.astype(bf16)], axis=1)
     arrived = across(pack(tagged))
-    packed_grad = across(pack(after(cotangent, arrived)))
     run_parts = splits // RUNS
     run_rows = run_parts * local_rows
 
@@ -760,6 +759,8 @@
     constants = (tap_rows, rate_row, shift_row, gain_row)
     orders = [order_of(gathered_0[:, model_width:])]
     seq_0 = to_sequence(orders[0], gathered_0[:, :model_width])
+    cotangent, mix_all = lax.optimization_barrier((cotangent, mix_all))
+    packed_grad = across(pack(cotangent))
     projected = [product(seq_0, mix_all)]
     gathered_1 = gather_rows(normed_runs[1])
     orders.append(order_of(gathered_1[:, model_width:]))

time: 660 us -> 669 us (1.014)
  local copies, waits for them, and re-layouts: 41.4 us -> 50.8 us
  starting transfers between devices: 62.1 us -> 68.9 us
    ppermute x5, waiting for transfers between devices: 109 us -> 96.8 us  [exchange_roles(): lax.ppermute(x, ('lo', 'tensor'), [(a * n + b, b * n + a) for a in range(...]
    all_to_all x4, starting transfers between devices: 16 us -> 27.7 us  [across(): return lax.all_to_all(rows, spread, split_axis=0, concat_axis=0, tiled=True)]
    unnamed x120 -> x118, local copies, waits for them, and re-layouts: 13.9 us -> 16.2 us
  transfers between devices with their start and end apart: 47 -> 47, of which waited for: 27 -> 28; matrix products, arithmetic and copies ran while one was open for 26% -> 26% of each run, Pallas kernels for 17% -> 17%
where the time goes in v6:
time: 669 us; the launch traced here: 660 us
  waiting for transfers between devices  245 us (37%)
  matrix products  134 us (20%)
  Pallas kernels  114 us (17%)
  starting transfers between devices  68.9 us (10%)
  local copies, waits for them, and re-layouts  50.8 us (8%)
  other arithmetic  31.6 us (5%)
  between operations  15.9 us (2%)
    dot_general x28, matrix products, product(): lax.dot_general(a, b, (((ca,), (cb,)), ((), ())), preferred_element_type=...  117 us
    ppermute x34, waiting for transfers between devices, swap(): return lax.ppermute(x, axis, [(i, i ^ bit) for i in range(size)])  115 us
    ppermute x5, waiting for transfers between devices, exchange_roles(): lax.ppermute(x, ('lo', 'tensor'), [(a * n + b, b * n + a) for a in range(...  96.8 us
    pallas_call x2, Pallas kernels, mixer_backward(): pl.pallas_call(kernel, grid_spec=pltpu.PrefetchScalarGridSpec(num_scalar_...  68.5 us
    pallas_call x2, Pallas kernels, mixer_forward(): pl.pallas_call(kernel, grid_spec=pltpu.PrefetchScalarGridSpec(num_scalar_...  45 us
    all_to_all x4, starting transfers between devices, across(): return lax.all_to_all(rows, spread, split_axis=0, concat_axis=0, tiled=True)  27.7 us
    ppermute x34, starting transfers between devices, swap(): return lax.ppermute(x, axis, [(i, i ^ bit) for i in range(size)])  21.4 us
    ppermute x5, starting transfers between devices, exchange_roles(): lax.ppermute(x, ('lo', 'tensor'), [(a * n + b, b * n + a) for a in range(...  19.5 us
  transfers between devices with their start and end apart: 47, of which 28 were waited for; matrix products, arithmetic and copies ran while one was open for 26% of the time, Pallas kernels for 17%

profile of v6, /device:TPU:2, one launch (start us, length us, event | category | flops | bytes accessed | tf_op | source)
XLA Modules:
  0.0 659.6 jit_solution(17762101499831114736)
XLA Ops:
  15.4 26.2 %collective-permute-done.3 = bf16[128,2176]{1,0:T(8,128)(2,1)S(1)} collective-permute-done((bf16[128,2176]{1,0:T(8,128)(2,1)S(1)}, bf16[128,2176]{1,0:T(8,128)(2,1)S(1)}, u32[]{:S(2)}, u32[]{:S(2)}) %collective-permute-start.3) | collective-permute-done | bytes 557088 | tf_op jit(solution)/shard_map/ppermute | solution.py:529
  54.1 39.0 %collective-permute-done = s32[1,3]{1,0:T(1,128)S(1)} collective-permute-done((s32[1,3]{1,0:T(1,128)S(1)}, s32[1,3]{1,0:T(1,128)S(1)}, u32[]{:S(2)}, u32[]{:S(2)}) %collective-permute-start) | collective-permute-done | bytes 44 | tf_op jit(solution)/shard_map/ppermute | solution.py:529
  97.4 14.1 %collective-permute-done.4 = bf16[256,1152]{1,0:T(8,128)(2,1)S(1)} collective-permute-done((bf16[256,1152]{1,0:T(8,128)(2,1)S(1)}, bf16[256,1152]{1,0:T(8,128)(2,1)S(1)}, u32[]{:S(2)}, u32[]{:S(2)}) %collective-permute-start.4) | collective-permute-done | bytes 589856 | tf_op jit(solution)/shard_map/ppermute | solution.py:524
  111.7 12.1 %collective-permute-done.1 = bf16[256,1152]{1,0:T(8,128)(2,1)S(1)} collective-permute-done((bf16[256,1152]{1,0:T(8,128)(2,1)S(1)}, bf16[256,1152]{1,0:T(8,128)(2,1)S(1)}, u32[]{:S(2)}, u32[]{:S(2)}) %collective-permute-start.1) | collective-permute-done | bytes 589856 | tf_op jit(solution)/shard_map/ppermute | solution.py:524
  143.2 16.1 %all-to-all-start.1 = ((bf16[8,64,1024]{2,1,0:T(8,128)(2,1)}), bf16[8,64,1024]{2,1,0:T(8,128)(2,1)S(1)}, u32[]{:S(2)}, u32[]{:S(2)}) async-start(bf16[8,64,1024]{2,1,0:T(8,128)(2,1)} %bitcast.188), calls=%async_computation.1 | async-start | bytes 2097152 | tf_op jit(solution)/shard_map/all_to_all | solution.py:640
  166.5 5.9 fusion.90.proj_ref.before_ref.halo_ref
  172.3 13.9 %all-to-all-done.1 = bf16[8,64,1024]{2,1,0:T(8,128)(2,1)S(1)} async-done(((bf16[8,64,1024]{2,1,0:T(8,128)(2,1)}), bf16[8,64,1024]{2,1,0:T(8,128)(2,1)S(1)}, u32[]{:S(2)}, u32[]{:S(2)}) %all-to-all-start.1) | async-done | bytes 1048608 | tf_op jit(solution)/shard_map/all_to_all | solution.py:640
  191.3 22.7 %mixer_forward.2 = (bf16[1024,512]{1,0:T(8,128)(2,1)}, f32[1024,512]{1,0:T(8,128)}, f32[1024,512]{1,0:T(8,128)}, f32[8,2,128,256]{3,2,1,0:T(8,128)}, f32[8,2,128...) custom-call(s32[3]{0:T(128)} %select_reduce_fusion.ends_ref, ...), custom_call_target="tpu_custom_call" | custom-call | flops 2048000000 | bytes 18432000 | tf_op jit(solution)/shard_map/mixer_forward/pallas_call | solution.py:392
  220.7 6.2 fusion.91.proj_ref.halo_ref
  229.7 22.2 %mixer_forward.3 = (bf16[1024,512]{1,0:T(8,128)(2,1)}, f32[1024,512]{1,0:T(8,128)}, f32[1024,512]{1,0:T(8,128)}, f32[8,2,128,256]{3,2,1,0:T(8,128)}, f32[8,2,128...) custom-call(s32[3]{0:T(128)} %select_reduce_fusion.ends_ref, ...), custom_call_target="tpu_custom_call" | custom-call | flops 2048000000 | bytes 18432000 | tf_op jit(solution)/shard_map/mixer_forward/pallas_call | solution.py:392
  259.9 13.0 %collective-permute-done.11 = bf16[256,1024]{1,0:T(8,128)(2,1)S(1)} collective-permute-done((bf16[256,1024]{1,0:T(8,128)(2,1)S(1)}, bf16[256,1024]{1,0:T(8,128)(2,1)S(1)}, u32[]{:S(2)}, u32[]{:S(2)}) %collective-permute-start.11) | collective-permute-done | bytes 524320 | tf_op jit(solution)/shard_map/ppermute | solution.py:524
  280.7 5.0 fusion.24
  285.7 6.3 multiply_convert_fusion.5
  295.9 7.9 %collective-permute-done.12 = f32[256,1024]{1,0:T(8,128)S(1)} collective-permute-done((f32[256,1024]{1,0:T(8,128)S(1)}, f32[256,1024]{1,0:T(8,128)S(1)}, u32[]{:S(2)}, u32[]{:S(2)}) %collective-permute-start.12) | collective-permute-done | bytes 1048608 | tf_op jit(solution)/shard_map/ppermute | solution.py:524
  304.7 12.7 %collective-permute-done.17 = bf16[256,1024]{1,0:T(8,128)(2,1)S(1)} collective-permute-done((bf16[256,1024]{1,0:T(8,128)(2,1)S(1)}, bf16[256,1024]{1,0:T(8,128)(2,1)S(1)}, u32[]{:S(2)}, u32[]{:S(2)}) %collective-permute-start.17) | collective-permute-done | bytes 524320 | tf_op jit(solution)/shard_map/ppermute | solution.py:524
  320.8 5.1 fusion.21
  325.9 6.3 multiply_convert_fusion.3
  340.3 5.3 fusion.92
  345.6 5.8 convolution_add_fusion
  389.4 34.1 %mixer_backward.2 = (bf16[1024,1664]{1,0:T(8,128)(2,1)}, f32[32,1024]{1,0:T(8,128)}, f32[8,256]{1,0:T(8,128)}, f32[16,128]{1,0:T(8,128)}, f32[2,128,256]{2,1,0:T(8,128)}, /*index=5*/f32[8,1024]{1,0:T(8,128)}) custom-call(s32[3]{0:T(128)} %select_reduce_fusion.ends_ref, f32[1024,1664]{1,0:T(8,128)} %fusion.91.proj_ref.halo_ref, ...), custom_call_target="tpu_custom_call" | custom-call | flops 2048000000 | bytes 18432000 | tf_op jit(solution)/shard_map/mixer_backward/pallas_call | solution.py:453
  429.7 4.6 fusion.50.dgated_ref
  442.8 34.5 %mixer_backward.3 = (bf16[1024,1664]{1,0:T(8,128)(2,1)}, f32[32,1024]{1,0:T(8,128)}, f32[8,256]{1,0:T(8,128)}, f32[16,128]{1,0:T(8,128)}, f32[2,128,256]{2,1,0:T(8,128)}, /*index=5*/f32[8,1024]{1,0:T(8,128)}) custom-call(s32[3]{0:T(128)} %select_reduce_fusion.ends_ref, f32[1024,1664]{1,0:T(8,128)} %fusion.90.proj_ref.before_ref.halo_ref, ...), custom_call_target="tpu_custom_call" | custom-call | flops 2048000000 | bytes 18432000 | tf_op jit(solution)/shard_map/mixer_backward/pallas_call | solution.py:453
  483.0 6.9 %fusion.93 = f32[1024,1664]{1,0:T(8,128)S(1)} fusion(bf16[1024,1024]{1,0:T(8,128)(2,1)} %bitcast.227, bf16[1024,1664]{1,0:T(8,128)(2,1)} %get-tuple-element.183), kind=kOutput, calls=%fused_computation.239 | convolution fusion | flops 3489660928 | bytes 12320768 | tf_op jit(solution)/shard_map/dot_general | solution.py:598
  490.0 4.6 add_convert_fusion
  497.0 7.0 %convolution_convert_fusion.2 = bf16[1024,1024]{1,0:T(8,128)(2,1)S(1)} fusion(bf16[1024,1664]{1,0:T(8,128)(2,1)} %get-tuple-element.183, bf16[1024,1664]{1,0:T(8,128)(2,1)} %slice.311), kind=kOutput, calls=%fused_computation.66 | convolution fusion | flops 3490709504 | bytes 8912896 | tf_op jit(solution)/shard_map/dot_general | solution.py:598
  524.0 5.0 collective-permute-start.32
  529.0 26.2 %collective-permute-done.31 = bf16[512,1024]{1,0:T(8,128)(2,1)S(1)} collective-permute-done((bf16[512,1024]{1,0:T(8,128)(2,1)}, bf16[512,1024]{1,0:T(8,128)(2,1)S(1)}, u32[]{:S(2)}, u32[]{:S(2)}) %collective-permute-start.31) | collective-permute-done | bytes 1048608 | tf_op jit(solution)/shard_map/ppermute | solution.py:524
  557.3 9.5 %collective-permute-done.32 = bf16[128,2112]{0,1:T(8,128)(2,1)S(1)} collective-permute-done((bf16[128,2112]{0,1:T(8,128)(2,1)}, bf16[128,2112]{0,1:T(8,128)(2,1)S(1)}, u32[]{:S(2)}, u32[]{:S(2)}) %collective-permute-start.32) | collective-permute-done | bytes 540704 | tf_op jit(solution)/shard_map/ppermute | solution.py:529
  580.8 7.2 %collective-permute-done.36 = f32[8,384]{1,0:T(8,128)S(1)} collective-permute-done((f32[8,384]{1,0:T(8,128)S(1)}, f32[8,384]{1,0:T(8,128)S(1)}, u32[]{:S(2)}, u32[]{:S(2)}) %collective-permute-start.36) | collective-permute-done | bytes 12320 | tf_op jit(solution)/shard_map/ppermute | solution.py:524
  588.0 4.8 collective-permute-start.37
  601.9 16.0 %reduce-scatter.5.cloned.1.call-done = bf16[128,2176]{1,0:T(8,128)(2,1)} async-done(((bf16[1024,2176]{1,0:T(8,128)(2,1)}), bf16[128,2176]{1,0:T(8,128)(2,1)}) %reduce-scatter.5.cloned.1.call-update) | async-done | bytes 557072 | tf_op jit(solution)/shard_map/reduce_scatter | solution.py:594
  626.8 22.1 %collective-permute-done.33 = bf16[128,2176]{1,0:T(8,128)(2,1)S(1)} collective-permute-done((bf16[128,2176]{1,0:T(8,128)(2,1)}, bf16[128,2176]{1,0:T(8,128)(2,1)S(1)}, u32[]{:S(2)}, u32[]{:S(2)}) %collective-permute-start.33) | collective-permute-done | bytes 557088 | tf_op jit(solution)/shard_map/ppermute | solution.py:529
  (391 shorter events, 215.7 us)
Async XLA Ops:
  7.2 130.3 %all-gather.3.cloned.1.call-start = ((), (), s32[]{:S(2)}) async-start(), calls=%async_computation.6 | async-start | bytes 5013504 | tf_op jit(solution)/shard_map/all_gather | solution.py:590
  10.9 30.7 %collective-permute-start.3 = (bf16[128,2176]{1,0:T(8,128)(2,1)S(1)}, bf16[128,2176]{1,0:T(8,128)(2,1)S(1)}, u32[]{:S(2)}, u32[]{:S(2)}) collective-permute-start(bf16[128,2176]{1,0:T(8,128)(2,1)S(1)} %concatenate.100), channel_id=1, source_target_pairs={{0,0},{1,4},{2,8},{3,12},{4,1},{5,5},{6,9},{7,13},{8,2},{9,6},{10,... | collective-permute-start | bytes 1671176 | tf_op jit(solution)/shard_map/ppermute | solution.py:529
  44.9 48.8 %all-to-all-start = ((bf16[8,64,1152]{2,1,0:T(8,128)(2,1)}), bf16[8,64,1152]{2,1,0:T(8,128)(2,1)S(1)}, u32[]{:S(2)}, u32[]{:S(2)}) async-start(bf16[8,64,1152]{2,1,0:T(8,128)(2,1)} %bitcast.1), calls=%async_computation | async-start | bytes 2359296 | tf_op jit(solution)/shard_map/all_to_all | solution.py:640
  48.6 44.5 %collective-permute-start = (s32[1,3]{1,0:T(1,128)S(1)}, s32[1,3]{1,0:T(1,128)S(1)}, u32[]{:S(2)}, u32[]{:S(2)}) collective-permute-start(s32[1,3]{1,0:T(1,128)S(1)} %copy-done.50), channel_id=1, source_target_pairs={{0,0},{1,4},{2,8},{3,12},{4,1},{5,5},{6,9},{7,13},{8,2},{9,6},{10,... | collective-permute-start | bytes 44 | tf_op jit(solution)/shard_map/ppermute | solution.py:529
  95.4 16.1 %collective-permute-start.4 = (bf16[256,1152]{1,0:T(8,128)(2,1)S(1)}, bf16[256,1152]{1,0:T(8,128)(2,1)S(1)}, u32[]{:S(2)}, u32[]{:S(2)}) collective-permute-start(bf16[256,1152]{1,0:T(8,128)(2,1)S(1)} %get-tuple-element.284), channel_id=1, source_target_pairs={{0,8},{4,12},{8,0},{12,4},{1,9},{5,13},{9,1},{13,5},{2,10},{6,14},... | collective-permute-start | bytes 1769480 | tf_op jit(solution)/shard_map/ppermute | solution.py:524
  96.2 27.5 %collective-permute-start.1 = (bf16[256,1152]{1,0:T(8,128)(2,1)S(1)}, bf16[256,1152]{1,0:T(8,128)(2,1)S(1)}, u32[]{:S(2)}, u32[]{:S(2)}) collective-permute-start(bf16[256,1152]{1,0:T(8,128)(2,1)S(1)} %get-tuple-element.285), channel_id=1, source_target_pairs={{0,8},{4,12},{8,0},{12,4},{1,9},{5,13},{9,1},{13,5},{2,10},{6,14},... | collective-permute-start | bytes 1769480 | tf_op jit(solution)/shard_map/ppermute | solution.py:524
  111.6 13.3 %collective-permute-start.5 = (bf16[512,1152]{1,0:T(8,128)(2,1)S(1)}, bf16[512,1152]{1,0:T(8,128)(2,1)S(1)}, u32[]{:S(2)}, u32[]{:S(2)}) collective-permute-start(bf16[512,1152]{1,0:T(8,128)(2,1)S(1)} %pad_maximum_fusion.13), channel_id=1, source_target_pairs={{0,4},{4,0},{8,12},{12,8},{1,5},{5,1},{9,13},{13,9},{2,6},{6,2},{1... | collective-permute-start | bytes 3538952 | tf_op jit(solution)/shard_map/ppermute | solution.py:524
  131.7 56.8 %collective-permute-start.6 = (bf16[128,2112]{0,1:T(8,128)(2,1)}, bf16[128,2112]{0,1:T(8,128)(2,1)}, u32[]{:S(2)}, u32[]{:S(2)}) collective-permute-start(bf16[128,2112]{0,1:T(8,128)(2,1)} %pad_maximum_fusion.26), channel_id=1, source_target_pairs={{0,0},{1,4},{2,8},{3,12},{4,1},{5,5},{6,9},{7,13},{8,2},{9,6},{10,... | collective-permute-start | bytes 1622024 | tf_op jit(solution)/shard_map/ppermute | solution.py:529
  143.2 42.9 %all-to-all-start.1 = ((bf16[8,64,1024]{2,1,0:T(8,128)(2,1)}), bf16[8,64,1024]{2,1,0:T(8,128)(2,1)S(1)}, u32[]{:S(2)}, u32[]{:S(2)}) async-start(bf16[8,64,1024]{2,1,0:T(8,128)(2,1)} %bitcast.188), calls=%async_computation.1 | async-start | bytes 2097152 | tf_op jit(solution)/shard_map/all_to_all | solution.py:640
  159.4 116.3 %all-gather.5.cloned.1.call-start = ((), (), s32[]{:S(2)}) async-start(), calls=%async_computation.7 | async-start | bytes 4866048 | tf_op jit(solution)/shard_map/all_gather | solution.py:590
  188.5 25.5 %collective-permute-start.7 = (bf16[512,1024]{1,0:T(8,128)(2,1)S(1)}, bf16[512,1024]{1,0:T(8,128)(2,1)}, u32[]{:S(2)}, u32[]{:S(2)}) collective-permute-start(bf16[512,1024]{1,0:T(8,128)(2,1)S(1)} %bitcast.158), channel_id=1, source_target_pairs={{0,8},{4,12},{8,0},{12,4},{1,9},{5,13},{9,1},{13,5},{2,10},{6,14},... | collective-permute-start | bytes 3145736 | tf_op jit(solution)/shard_map/ppermute | solution.py:524
  188.6 294.4 %reduce-scatter.3.cloned.1.call-start = ((), (), s32[]{:S(2)}) async-start(), calls=%async_computation.8 | async-start | bytes 5013504 | tf_op jit(solution)/shard_map/reduce_scatter | solution.py:594
  227.6 29.4 %collective-permute-start.10 = (f32[256,1024]{1,0:T(8,128)S(1)}, f32[256,1024]{1,0:T(8,128)S(1)}, u32[]{:S(2)}, u32[]{:S(2)}) collective-permute-start(f32[256,1024]{1,0:T(8,128)S(1)} %get-tuple-element.123), channel_id=1, source_target_pairs={{0,8},{4,12},{8,0},{12,4},{1,9},{5,13},{9,1},{13,5},{2,10},{6,14},... | collective-permute-start | bytes 3145736 | tf_op jit(solution)/shard_map/ppermute | solution.py:524
  256.7 17.3 %collective-permute-start.9 = (f32[512,1024]{1,0:T(8,128)S(1)}, f32[512,1024]{1,0:T(8,128)S(1)}, u32[]{:S(2)}, u32[]{:S(2)}) collective-permute-start(f32[512,1024]{1,0:T(8,128)S(1)} %slice.325), channel_id=1, source_target_pairs={{0,4},{4,0},{8,12},{12,8},{1,5},{5,1},{9,13},{13,9},{2,6},{6,2},{1... | collective-permute-start | bytes 6291464 | tf_op jit(solution)/shard_map/ppermute | solution.py:524
  258.5 14.4 %collective-permute-start.11 = (bf16[256,1024]{1,0:T(8,128)(2,1)S(1)}, bf16[256,1024]{1,0:T(8,128)(2,1)S(1)}, u32[]{:S(2)}, u32[]{:S(2)}) collective-permute-start(bf16[256,1024]{1,0:T(8,128)(2,1)S(1)} %multiply_convert_fusion.8), channel_id=1, source_target_pairs={{0,8},{4,12},{8,0},{12,4},{1,9},{5,13},{9,1},{13,5},{2,10},{6,14},... | collective-permute-start | bytes 1572872 | tf_op jit(solution)/shard_map/ppermute | solution.py:524
  278.7 25.2 %collective-permute-start.12 = (f32[256,1024]{1,0:T(8,128)S(1)}, f32[256,1024]{1,0:T(8,128)S(1)}, u32[]{:S(2)}, u32[]{:S(2)}) collective-permute-start(f32[256,1024]{1,0:T(8,128)S(1)} %copy-done.22), channel_id=1, source_target_pairs={{0,8},{4,12},{8,0},{12,4},{1,9},{5,13},{9,1},{13,5},{2,10},{6,14},... | collective-permute-start | bytes 3145736 | tf_op jit(solution)/shard_map/ppermute | solution.py:524
  295.8 21.7 %collective-permute-start.16 = (bf16[512,1024]{1,0:T(8,128)(2,1)S(1)}, bf16[512,1024]{1,0:T(8,128)(2,1)S(1)}, u32[]{:S(2)}, u32[]{:S(2)}) collective-permute-start(bf16[512,1024]{1,0:T(8,128)(2,1)S(1)} %slice.334), channel_id=1, source_target_pairs={{0,4},{4,0},{8,12},{12,8},{1,5},{5,1},{9,13},{13,9},{2,6},{6,2},{1... | collective-permute-start | bytes 3145736 | tf_op jit(solution)/shard_map/ppermute | solution.py:524
  304.3 13.1 %collective-permute-start.17 = (bf16[256,1024]{1,0:T(8,128)(2,1)S(1)}, bf16[256,1024]{1,0:T(8,128)(2,1)S(1)}, u32[]{:S(2)}, u32[]{:S(2)}) collective-permute-start(bf16[256,1024]{1,0:T(8,128)(2,1)S(1)} %multiply_convert_fusion.7), channel_id=1, source_target_pairs={{0,8},{4,12},{8,0},{12,4},{1,9},{5,13},{9,1},{13,5},{2,10},{6,14},... | collective-permute-start | bytes 1572872 | tf_op jit(solution)/shard_map/ppermute | solution.py:524
  319.5 16.9 %collective-permute-start.20 = (bf16[256,1024]{1,0:T(8,128)(2,1)S(1)}, bf16[256,1024]{1,0:T(8,128)(2,1)S(1)}, u32[]{:S(2)}, u32[]{:S(2)}) collective-permute-start(bf16[256,1024]{1,0:T(8,128)(2,1)S(1)} %slice.457), channel_id=1, source_target_pairs={{0,8},{4,12},{8,0},{12,4},{1,9},{5,13},{9,1},{13,5},{2,10},{6,14},... | collective-permute-start | bytes 1572872 | tf_op jit(solution)/shard_map/ppermute | solution.py:524
  339.3 14.0 %collective-permute-start.21 = (bf16[256,1024]{1,0:T(8,128)(2,1)S(1)}, bf16[256,1024]{1,0:T(8,128)(2,1)S(1)}, u32[]{:S(2)}, u32[]{:S(2)}) collective-permute-start(bf16[256,1024]{1,0:T(8,128)(2,1)S(1)} %slice.456), channel_id=1, source_target_pairs={{0,8},{4,12},{8,0},{12,4},{1,9},{5,13},{9,1},{13,5},{2,10},{6,14},... | collective-permute-start | bytes 1572872 | tf_op jit(solution)/shard_map/ppermute | solution.py:524
  355.1 13.1 %collective-permute-start.22 = (bf16[256,1024]{1,0:T(8,128)(2,1)S(1)}, bf16[256,1024]{1,0:T(8,128)(2,1)S(1)}, u32[]{:S(2)}, u32[]{:S(2)}) collective-permute-start(bf16[256,1024]{1,0:T(8,128)(2,1)S(1)} %get-tuple-element.266), channel_id=1, source_target_pairs={{0,8},{4,12},{8,0},{12,4},{1,9},{5,13},{9,1},{13,5},{2,10},{6,14},... | collective-permute-start | bytes 1572872 | tf_op jit(solution)/shard_map/ppermute | solution.py:524
  385.5 37.9 %collective-permute-start.26 = (bf16[256,1024]{1,0:T(8,128)(2,1)S(1)}, bf16[256,1024]{1,0:T(8,128)(2,1)S(1)}, u32[]{:S(2)}, u32[]{:S(2)}) collective-permute-start(bf16[256,1024]{1,0:T(8,128)(2,1)S(1)} %copy-done.19), channel_id=1, source_target_pairs={{0,8},{4,12},{8,0},{12,4},{1,9},{5,13},{9,1},{13,5},{2,10},{6,14},... | collective-permute-start | bytes 1572872 | tf_op jit(solution)/shard_map/ppermute | solution.py:524
  386.7 36.8 %collective-permute-start.27 = (bf16[256,1024]{1,0:T(8,128)(2,1)S(1)}, bf16[256,1024]{1,0:T(8,128)(2,1)S(1)}, u32[]{:S(2)}, u32[]{:S(2)}) collective-permute-start(bf16[256,1024]{1,0:T(8,128)(2,1)S(1)} %slice.455), channel_id=1, source_target_pairs={{0,8},{4,12},{8,0},{12,4},{1,9},{5,13},{9,1},{13,5},{2,10},{6,14},... | collective-permute-start | bytes 1572872 | tf_op jit(solution)/shard_map/ppermute | solution.py:524
  387.6 37.3 %collective-permute-start.28 = (bf16[256,1024]{1,0:T(8,128)(2,1)S(1)}, bf16[256,1024]{1,0:T(8,128)(2,1)S(1)}, u32[]{:S(2)}, u32[]{:S(2)}) collective-permute-start(bf16[256,1024]{1,0:T(8,128)(2,1)S(1)} %slice.454), channel_id=1, source_target_pairs={{0,8},{4,12},{8,0},{12,4},{1,9},{5,13},{9,1},{13,5},{2,10},{6,14},... | collective-permute-start | bytes 1572872 | tf_op jit(solution)/shard_map/ppermute | solution.py:524
  434.3 48.7 %all-to-all-start.2 = ((bf16[8,64,1024]{2,1,0:T(8,128)(2,1)}), bf16[8,64,1024]{2,1,0:T(8,128)(2,1)S(1)}, u32[]{:S(2)}, u32[]{:S(2)}) async-start(bf16[8,64,1024]{2,1,0:T(8,128)(2,1)} %bitcast.58), calls=%async_computation.3 | async-start | bytes 2097152 | tf_op jit(solution)/shard_map/all_to_all | solution.py:640
  438.0 179.9 %reduce-scatter.5.cloned.1.call-start = ((), (), s32[]{:S(2)}) async-start(), calls=%async_computation.9 | async-start | bytes 5013504 | tf_op jit(solution)/shard_map/reduce_scatter | solution.py:594
  522.5 32.7 %collective-permute-start.31 = (bf16[512,1024]{1,0:T(8,128)(2,1)}, bf16[512,1024]{1,0:T(8,128)(2,1)S(1)}, u32[]{:S(2)}, u32[]{:S(2)}) collective-permute-start(bf16[512,1024]{1,0:T(8,128)(2,1)} %slice.453), channel_id=1, source_target_pairs={{0,8},{4,12},{8,0},{12,4},{1,9},{5,13},{9,1},{13,5},{2,10},{6,14},... | collective-permute-start | bytes 3145736 | tf_op jit(solution)/shard_map/ppermute | solution.py:524
  524.0 42.8 %collective-permute-start.32 = (bf16[128,2112]{0,1:T(8,128)(2,1)}, bf16[128,2112]{0,1:T(8,128)(2,1)S(1)}, u32[]{:S(2)}, u32[]{:S(2)}) collective-permute-start(bf16[128,2112]{0,1:T(8,128)(2,1)} %copy.189), channel_id=1, source_target_pairs={{0,0},{1,4},{2,8},{3,12},{4,1},{5,5},{6,9},{7,13},{8,2},{9,6},{10,... | collective-permute-start | bytes 1622024 | tf_op jit(solution)/shard_map/ppermute | solution.py:529
  569.2 54.5 %all-to-all-start.3 = ((bf16[8,64,1024]{2,1,0:T(8,128)(2,1)}), bf16[8,64,1024]{2,1,0:T(8,128)(2,1)}, u32[]{:S(2)}, u32[]{:S(2)}) async-start(bf16[8,64,1024]{2,1,0:T(8,128)(2,1)} %bitcast.75), calls=%async_computation.4 | async-start | bytes 2097152 | tf_op jit(solution)/shard_map/all_to_all | solution.py:640
  578.9 9.1 %collective-permute-start.36 = (f32[8,384]{1,0:T(8,128)S(1)}, f32[8,384]{1,0:T(8,128)S(1)}, u32[]{:S(2)}, u32[]{:S(2)}) collective-permute-start(f32[8,384]{1,0:T(8,128)S(1)} %add.314), channel_id=1, source_target_pairs={{0,1},{1,0},{2,3},{3,2},{4,5},{5,4},{6,7},{7,6},{8,9},{9,8},{10,11... | collective-permute-start | bytes 36872 | tf_op jit(solution)/shard_map/ppermute | solution.py:524
  588.0 9.1 %collective-permute-start.37 = (f32[8,384]{1,0:T(8,128)S(1)}, f32[8,384]{1,0:T(8,128)S(1)}, u32[]{:S(2)}, u32[]{:S(2)}) collective-permute-start(f32[8,384]{1,0:T(8,128)S(1)} %add.315), channel_id=1, source_target_pairs={{0,2},{1,3},{2,0},{3,1},{4,6},{5,7},{6,4},{7,5},{8,10},{9,11},{10,... | collective-permute-start | bytes 36872 | tf_op jit(solution)/shard_map/ppermute | solution.py:524
  617.9 31.0 %collective-permute-start.33 = (bf16[128,2176]{1,0:T(8,128)(2,1)}, bf16[128,2176]{1,0:T(8,128)(2,1)S(1)}, u32[]{:S(2)}, u32[]{:S(2)}) collective-permute-start(bf16[128,2176]{1,0:T(8,128)(2,1)} %reduce-scatter.5.cloned.1.call-done), channel_id=1, source_target_pairs={{0,0},{1,4},{2,8},{3,12},{4,1},{5,5},{6,9},{7,13},{8,2},{9,6},{10,... | collective-permute-start | bytes 1671176 | tf_op jit(solution)/shard_map/ppermute | solution.py:529
  (76 other events, 1018.0 us)
Sparse Core Ops, SparseCore 0:
  42.6 94.9 all-gather.2
  188.7 74.3 all-gather.4
  371.0 110.1 reduce-scatter.2
  497.2 120.6 reduce-scatter.4
